TPU v7x, 128 devices: a whole 4x4x4 slice. The times are simulated.
128 devices in a mesh: front: 8 (over z_hi, x), row: 8 (over y, core), col: 2 (over z_lo).
Axes of the slice: x: 4, y: 4, z: 4 (z_hi: 2, z_lo: 2; z = z_hi * 2 + z_lo), core: 2. Of those that a mesh axis runs over, the one named last changes fastest.
Arguments:
- pivot_block: float32 [16, 512, 512], P(('front', 'col'), 'row'), as said below
- panel_rows: float32 [16, 4096, 512], P(('front', 'col'), 'row'), may hold values from -0.875 to 0.875
- update_block: float32 [16, 4096, 4096], P(('front', 'col'), 'row'), as said below
- tile_map: int32 [16, 32], replicated, may hold values from 0 to 95, as said below
Outputs:
- pivot_factor: float32 [16, 512, 512], P(('front', 'col'), 'row')
- panel_factor: float32 [16, 4096, 512], P(('front', 'col'), 'row')
- parent_update: float32 [2, 12288, 12288], P('col', 'front', 'row')
Inputs may be any that keep to these rules, and one draw needn't show every extreme that they name: `pivot_block`: each child's pivot block is symmetric positive definite. `update_block`: each child's update block is symmetric. `tile_map`: row c lists, strictly increasing, the parent tiles that receive child c's 32 tiles; child c belongs to parent c % 2. At most 5 entries of one row fall in any aligned block of 12 parent tiles, and exactly 5 do in some block.
All inputs are finite; a program needn't handle non-finite values.
Results may differ from a plain program's by a relative error of at most 0.0001.
Values sent between devices are 32-bit elements; how exact they have to be, the bound alone decides.
No kernel may reach another device: no remote copies, remote signals or barrier semaphores. Data moves between devices by JAX's collectives and lax.ppermute only.
A program may use at most 192 MiB of HBM per device.

v0:
```python
import jax
import jax.numpy as jnp
from jax import lax
from jax.sharding import PartitionSpec as P

TILE = 128
PARENT = 12288


def solve_panel(lower_factor, panel_block):
    return jax.scipy.linalg.solve_triangular(lower_factor, panel_block.T, lower=True).T


def block_slots(tile_ids, block_count, block_width, slot_count):
    owners = tile_ids // block_width
    block_ids = jnp.arange(block_count, dtype=jnp.int32)
    starts = jnp.sum((owners[None, :] < block_ids[:, None]).astype(jnp.int32), axis=1)
    counts = jnp.sum((owners[None, :] == block_ids[:, None]).astype(jnp.int32), axis=1)
    slot_ids = jnp.arange(slot_count, dtype=jnp.int32)
    picks = jnp.minimum(starts[:, None] + slot_ids[None, :], tile_ids.shape[0] - 1)
    usable = slot_ids[None, :] < counts[:, None]
    return (picks, usable)


def local_onehot(child_maps, block_me, block_width, slot_count):
    owners = child_maps // block_width
    starts = jnp.sum((owners < block_me).astype(jnp.int32), axis=1)
    counts = jnp.sum((owners == block_me).astype(jnp.int32), axis=1)
    slot_ids = jnp.arange(slot_count, dtype=jnp.int32)
    picks = jnp.minimum(starts[:, None] + slot_ids[None, :], child_maps.shape[1] - 1)
    local_tile = jnp.take_along_axis(child_maps, picks, axis=1) - block_me * block_width
    usable = slot_ids[None, :] < counts[:, None]
    targets = jnp.arange(block_width, dtype=jnp.int32)
    onehot = (local_tile[:, None, :] == targets[None, :, None]) & usable[:, None, :]
    return onehot.astype(jnp.float32)


def local(pivot_block, panel_rows, update_block, tile_map):
    row_count = lax.axis_size("row")
    front_count = lax.axis_size("front")
    col_count = lax.axis_size("col")
    row_me = lax.axis_index("row")
    front_me = lax.axis_index("front")
    col_me = lax.axis_index("col")
    tile_size = TILE
    pivot_share = pivot_block.shape[1]
    own_rows = panel_rows.shape[1]
    contrib_order = update_block.shape[2]
    tile_count = contrib_order // tile_size
    block_width = PARENT // tile_size // row_count
    slot_count = tile_count // row_count + 1
    child_index = front_me * col_count + col_me
    tile_ids = lax.dynamic_index_in_dim(tile_map, child_index, 0, keepdims=False)
    pivot_whole = lax.all_gather(pivot_block[0], "row", axis=0, tiled=True)
    lower_factor = jnp.linalg.cholesky(pivot_whole)
    own_factor = solve_panel(lower_factor, panel_rows[0])
    all_factor = lax.all_gather(own_factor, "row", axis=0, tiled=True)
    col_picks, col_usable = block_slots(tile_ids, row_count, block_width, slot_count)
    contribution = update_block[0] - jnp.dot(
        own_factor, all_factor.T, precision=lax.Precision.HIGHEST
    )
    shaped = contribution.reshape(own_rows, tile_count, tile_size)
    picked = jnp.take(shaped, col_picks.reshape(-1), axis=1)
    picked = picked.reshape(own_rows, row_count, slot_count, tile_size)
    source = jnp.where(col_usable[None, :, :, None], picked, 0.0)
    arrived = lax.all_to_all(source, "row", split_axis=1, concat_axis=0, tiled=True)
    arrived = arrived.reshape(contrib_order, slot_count, tile_size)
    row_picks, row_usable = block_slots(tile_ids, front_count, block_width, slot_count)
    shaped = arrived.reshape(tile_count, tile_size, slot_count, tile_size)
    picked = jnp.take(shaped, row_picks.reshape(-1), axis=0)
    picked = picked.reshape(front_count, slot_count, tile_size, slot_count, tile_size)
    picked = jnp.where(row_usable[:, :, None, None, None], picked, 0.0)
    routed = lax.all_to_all(picked, "front", split_axis=0, concat_axis=0, tiled=True)
    sources = jnp.arange(front_count, dtype=jnp.int32) * col_count + col_me
    child_maps = jnp.take(tile_map, sources, axis=0)
    row_hot = local_onehot(child_maps, front_me, block_width, slot_count)
    col_hot = local_onehot(child_maps, row_me, block_width, slot_count)
    partial_value = jnp.einsum("fsxty,fbt->fsxby", routed, col_hot, precision=lax.Precision.HIGHEST)
    parent = jnp.einsum("fas,fsxby->axby", row_hot, partial_value, precision=lax.Precision.HIGHEST)
    parent = parent.reshape(block_width * tile_size, block_width * tile_size)
    pivot_rows_out = lax.dynamic_slice_in_dim(lower_factor, row_me * pivot_share, pivot_share, 0)
    return (pivot_rows_out[None], own_factor[None], parent[None])


def solution(mesh):
    return jax.shard_map(
        local,
        mesh=mesh,
        in_specs=(
            P(("front", "col"), "row", None),
            P(("front", "col"), "row", None),
            P(("front", "col"), "row", None),
            P(),
        ),
        out_specs=(
            P(("front", "col"), "row", None),
            P(("front", "col"), "row", None),
            P("col", "front", "row"),
        ),
        check_vma=False,
    )
```

profile of v0, /device:TPU:14, one launch (start us, length us, event | category | flops | bytes accessed | tf_op | source)
XLA Modules:
  0.0 727.1 jit_solution(5956696681664558131)
XLA Ops:
  10.6 23.7 %all-gather.6.cloned.1.call-done = f32[1,512,512]{2,0,1:T(1,128)} async-done(((f32[1,64,512]{2,0,1:T(1,128)}), f32[1,512,512]{2,0,1:T(1,128)}) %all-gather.6.cloned.1.call-update) | async-done | bytes 1048592 | tf_op jit(solution)/shard_map/all_gather | solution.py:54
  38.1 11.7 %cholesky.104 = f32[128,128]{1,0:T(8,128)S(1)} custom-call(f32[128,128]{1,0:T(8,128)S(1)} %cholesky.266), custom_call_target="Cholesky" | custom-call | tf_op jit(solution)/shard_map/jit(cholesky)/cholesky | solution.py:55
  49.8 9.8 %custom-call.31 = f32[1,128,128]{1,2,0:T(8,128)S(1)} custom-call(f32[1,128,128]{2,1,0:T(8,128)S(1)} %get-tuple-element.58), custom_call_target="InvertDiagBlocksLowerTriangular" | custom-call | tf_op jit(solution)/shard_map/jit(cholesky)/cholesky | solution.py:55
  60.4 11.7 %cholesky.217 = f32[128,128]{1,0:T(8,128)S(1)} custom-call(f32[128,128]{1,0:T(8,128)S(1)} %cholesky.270), custom_call_target="Cholesky" | custom-call | tf_op jit(solution)/shard_map/jit(cholesky)/cholesky | solution.py:55
  72.2 10.0 %custom-call.32 = f32[1,128,128]{1,2,0:T(8,128)S(1)} custom-call(f32[1,128,128]{2,1,0:T(8,128)S(1)} %get-tuple-element.55), custom_call_target="InvertDiagBlocksLowerTriangular" | custom-call | tf_op jit(solution)/shard_map/jit(cholesky)/cholesky | solution.py:55
  82.9 11.7 %cholesky.238 = f32[128,128]{1,0:T(8,128)S(1)} custom-call(f32[128,128]{1,0:T(8,128)S(1)} %cholesky.275), custom_call_target="Cholesky" | custom-call | tf_op jit(solution)/shard_map/jit(cholesky)/cholesky | solution.py:55
  95.3 9.8 %custom-call.33 = f32[1,128,128]{1,2,0:T(8,128)S(1)} custom-call(f32[1,128,128]{2,1,0:T(8,128)S(1)} %get-tuple-element.52), custom_call_target="InvertDiagBlocksLowerTriangular" | custom-call | tf_op jit(solution)/shard_map/jit(cholesky)/cholesky | solution.py:55
  105.7 11.7 %cholesky.255 = f32[128,128]{1,0:T(8,128)S(1)} custom-call(f32[128,128]{1,0:T(8,128)S(1)} %convolution_subtract_fusion.5), custom_call_target="Cholesky" | custom-call | tf_op jit(solution)/shard_map/jit(cholesky)/cholesky | solution.py:55
  122.5 10.4 %while.1 = (s32[]{:T(128)}, f32[512,512]{1,0:T(8,128)S(1)}, s32[4,2]{0,1:T(2,128)S(1)}, f32[4,128,128]{2,1,0:T(8,128)}, s32[]{:T(128)}) while((s32[]{:T(128)}, f32[512,512]{1,0:T(8,128)S(1)}, s32[4,2]{0,1:T(2,128)S(1)}, f32[4,128,128]{2,1,0:T(8,128)}, s32[]{:T(128)}) %tuple.46), condition=%wide.while_cond, body=%wide.while_body.sunk | while | flops 2 | bytes 132205 | solution.py:11
  133.0 40.6 %custom-call.34 = f32[4,128,128]{1,2,0:T(8,128)S(1)} custom-call(f32[4,128,128]{2,1,0:T(8,128)} %get-tuple-element.11), custom_call_target="InvertDiagBlocksLowerTriangular" | custom-call | tf_op jit(solution)/shard_map/jit(_solve_triangular)/triangular_solve | solution.py:11
  178.4 50.2 %all-gather.4.cloned.1.call-done = f32[4096,512]{0,1:T(8,128)} async-done(((f32[512,512]{0,1:T(8,128)}), f32[4096,512]{0,1:T(8,128)}) %all-gather.4.cloned.1.call-update) | async-done | bytes 8388624 | tf_op jit(solution)/shard_map/all_gather | solution.py:57
  228.6 16.5 %fusion.7 = f32[64,32,8,128]{3,2,1,0:T(8,128)S(1)} fusion(f32[1,512,4096]{2,1,0:T(8,128)} %param.8, f32[4096,512]{0,1:T(8,128)} %all-gather.4.cloned.1.call-done, f32[128,512]{1,0:T(8,128)S(1)} %fusion.33, f32[128,512]{1,0:T(8,128)S(1)} %fusion.34, f32[128,512]{1,0:T(8,128)S(1)} %fusion.36, f32[128,512]{1,0:T(8,128)S(1)} %fusion.21), kind=kOutput, calls=%fused_computation.16 | convolution fusion | flops 12887785472 | bytes 26214400 | tf_op jit(solution)/shard_map/dot_general | solution.py:59
  249.5 10.6 %gather_fusion.1 = f32[40,512,128]{2,1,0:T(8,128)} fusion(f32[512,32,128]{2,0,1:T(8,128)} %bitcast.114, s32[1024]{0:T(1024)S(1)} %pad_clamp_fusion), kind=kCustom, calls=%fused_computation.3 | custom fusion | bytes 20971680 | tf_op jit(solution)/shard_map/jit(_take)/gather | solution.py:63
  260.1 6.3 select_select_fusion.1
  266.4 122.2 %all_to_all.20 = f32[512,8,5,128]{3,0,2,1:T(8,128)} all-to-all(f32[512,8,5,128]{3,0,2,1:T(8,128)S(1)} %select_select_fusion.1), channel_id=1, replica_groups=mesh['front'=8,'row'=8,'col'=2] {'row'}, dimensions={1} | all-to-all | bytes 20971520 | tf_op jit(solution)/shard_map/all_to_all | solution.py:66
  388.6 9.2 %copy.46 = f32[8,512,1,5,128]{4,1,0,3,2:T(8,128)} copy(f32[8,512,1,5,128]{4,1,3,0,2:T(8,128)} %bitcast.116) | data formatting | bytes 20971520 | tf_op jit(solution)/shard_map/all_to_all | solution.py:66
  397.8 12.2 %gather_fusion.2 = f32[40,128,5,128]{3,1,2,0:T(8,128)} fusion(f32[32,128,5,128]{3,1,0,2:T(8,128)} %bitcast.112, s32[1024]{0:T(1024)S(1)} %pad_clamp_fusion), kind=kCustom, calls=%fused_computation.4 | custom fusion | bytes 26214560 | tf_op jit(solution)/shard_map/jit(_take)/gather | solution.py:70
  410.0 12.8 %select_select_fusion = f32[8,5,128,5,128]{4,2,3,1,0:T(8,128)} fusion(f32[8,5,128,5,128]{4,2,3,1,0:T(8,128)} %bitcast.113, pred[8,5]{1,0:T(8,128)(4,1)S(1)} %get-tuple-element.64, pred[8,5]{1,0:T(8,128)(4,1)S(1)} %get-tuple-element.63), kind=kLoop, calls=%fused_computation.12 | loop fusion | flops 6553600 | bytes 26214480 | tf_op jit(solution)/shard_map/jit(_where)/select_n | solution.py:72
  422.8 7.4 %all-to-all-start.1 = ((f32[8,5,128,5,128]{4,2,3,1,0:T(8,128)}), f32[8,5,128,5,128]{4,2,3,1,0:T(8,128)}, u32[]{:S(2)}, u32[]{:S(2)}) async-start(f32[8,5,128,5,128]{4,2,3,1,0:T(8,128)} %select_select_fusion), calls=%async_computation.1 | async-start | bytes 26214400 | tf_op jit(solution)/shard_map/all_to_all | solution.py:73
  436.3 187.8 %all-to-all-done.1 = f32[8,5,128,5,128]{4,2,3,1,0:T(8,128)} async-done(((f32[8,5,128,5,128]{4,2,3,1,0:T(8,128)}), f32[8,5,128,5,128]{4,2,3,1,0:T(8,128)}, u32[]{:S(2)}, u32[]{:S(2)}) %all-to-all-start.1) | async-done | bytes 13107232 | tf_op jit(solution)/shard_map/all_to_all | solution.py:73
  624.1 33.7 %fusion.4 = f32[8,5,128,12,128]{4,3,2,1,0:T(8,128)} fusion(f32[8,5,128,5,128]{4,2,3,1,0:T(8,128)} %all-to-all-done.1, s32[8,5]{1,0:T(8,128)S(1)} %select_subtract_fusion, pred[8,5]{1,0:T(8,128)(4,1)S(1)} %iota_compare_fusion.8), kind=kOutput, calls=%fused_computation.11 | convolution fusion | flops 471860160 | bytes 44564680 | tf_op jit(solution)/shard_map/fsxty,fbt->fsxby/dot_general | solution.py:78
  657.8 37.8 %fusion.8 = f32[12,128,12,128]{3,0,2,1:T(8,128)} fusion(f32[8,5,128,12,128]{4,3,2,1,0:T(8,128)} %fusion.4, s32[8,5]{0,1:T(8,128)S(1)} %copy.44, pred[8,5]{0,1:T(8,128)(4,1)S(1)} %iota_compare_fusion.9), kind=kOutput, calls=%fused_computation.17 | convolution fusion | flops 1132463104 | bytes 40894664 | tf_op jit(solution)/shard_map/fas,fsxby->axby/dot_general | solution.py:79
  695.6 12.4 %copy.49 = f32[12,128,12,128]{3,2,1,0:T(8,128)} copy(f32[12,128,12,128]{3,0,2,1:T(8,128)} %fusion.8) | data formatting | bytes 18874368 | tf_op jit(solution)/shard_map/fas,fsxby->axby/dot_general | solution.py:79
  708.0 11.9 %broadcast_in_dim_reshape.3 = f32[1,1536,1536]{2,1,0:T(8,128)} reshape(f32[12,128,12,128]{3,2,1,0:T(8,128)} %copy.49) | data formatting | bytes 18874368 | tf_op jit(solution)/shard_map/broadcast_in_dim;reshape | solution.py:82
  (79 shorter events, 38.3 us)
Async XLA Ops:
  7.2 27.1 %all-gather.6.cloned.1.call-start = ((), (), s32[]{:S(2)}) async-start(), calls=%async_computation.3 | async-start | bytes 1179648 | tf_op jit(solution)/shard_map/all_gather | solution.py:54
  8.9 219.7 %all-gather.4.cloned.1.call-start = ((), (), s32[]{:S(2)}) async-start(), calls=%async_computation.2 | async-start | bytes 9437184 | tf_op jit(solution)/shard_map/all_gather | solution.py:57
  36.6 141.4 %copy-start = (s32[16,32]{1,0:T(8,128)S(1)}, s32[16,32]{1,0:T(8,128)}, u32[]{:S(2)}) copy-start(s32[16,32]{1,0:T(8,128)} %param.9) | copy-start | bytes 6148
  422.8 201.3 %all-to-all-start.1 = ((f32[8,5,128,5,128]{4,2,3,1,0:T(8,128)}), f32[8,5,128,5,128]{4,2,3,1,0:T(8,128)}, u32[]{:S(2)}, u32[]{:S(2)}) async-start(f32[8,5,128,5,128]{4,2,3,1,0:T(8,128)} %select_select_fusion), calls=%async_computation.1 | async-start | bytes 26214400 | tf_op jit(solution)/shard_map/all_to_all | solution.py:73
Sparse Core Ops, SparseCore 0:
  10.3 23.9 all-gather.5
  178.1 50.4 all-gather.3
where the time goes:
time: 738 us; the launch traced here: 727 us
  waiting for transfers between devices  262 us (36%)
  other arithmetic  143 us (19%)
  blocking collectives  122 us (17%)
  matrix products  92.9 us (13%)
  local copies, waits for them, and re-layouts  82.6 us (11%)
  between operations  17.3 us (2%)
  starting transfers between devices  7.46 us (1%)
    all_to_all x1, waiting for transfers between devices, local(): lax.all_to_all(picked, 'front', split_axis=0, concat_axis=0, tiled=True)  188 us
    all_to_all x1, blocking collectives, local(): lax.all_to_all(source, 'row', split_axis=1, concat_axis=0, tiled=True)  122 us
    another operation x14, other arithmetic, local(): lower_factor = jnp.linalg.cholesky(pivot_whole)  78.6 us
    all_gather x1, waiting for transfers between devices, local(): all_factor = lax.all_gather(own_factor, 'row', axis=0, tiled=True)  50.2 us
    another operation x3, other arithmetic, solve_panel(): jax.scipy.linalg.solve_triangular(lower_factor, panel_block.T, lower=True)  41.8 us
    dot_general x1, matrix products, local(): jnp.einsum('fas,fsxby->axby', row_hot, partial_value, precision=lax.Preci...  37.8 us
    dot_general x1, matrix products, local(): jnp.einsum('fsxty,fbt->fsxby', routed, col_hot, precision=lax.Precision.H...  33.7 us
    all_gather x1, waiting for transfers between devices, local(): pivot_whole = lax.all_gather(pivot_block[0], 'row', axis=0, tiled=True)  23.7 us
  transfers between devices with their start and end apart: 3, of which 3 were waited for; matrix products, arithmetic and copies ran while one was open for 1% of the time, Pallas kernels for 0%

commit v1 on v0

v1 whole, which is shorter than its diff:
```python
import jax
import jax.numpy as jnp
from jax import lax
from jax.experimental import pallas as pl
from jax.experimental.pallas import tpu as pltpu
from jax.sharding import PartitionSpec as P

TILE = 128
BLOCK = 12
SLOTS = 5
GROUPS = 8
CTILES = 32
WIN = SLOTS * TILE
SIDE = BLOCK * TILE
CHUNKS = ((0, 1), (1, 2), (3, 2))
HI = lax.Precision.HIGHEST
F32 = jnp.float32


def any_spec():
    return pl.BlockSpec(memory_space=pl.ANY)


def smem_spec():
    return pl.BlockSpec(memory_space=pltpu.SMEM)


def vmem_spec():
    return pl.BlockSpec(memory_space=pltpu.VMEM)


def window_starts(tile_ids):
    owners = tile_ids // BLOCK
    blocks = jnp.arange(GROUPS, dtype=jnp.int32)
    starts = jnp.sum((owners[..., None, :] < blocks[:, None]).astype(jnp.int32), axis=-1)
    return jnp.minimum(starts, CTILES - SLOTS)


def slot_targets(child_maps, block_me):
    first = jnp.sum((child_maps // BLOCK < block_me).astype(jnp.int32), axis=1)
    first = jnp.minimum(first, CTILES - SLOTS)
    picks = first[:, None] + jnp.arange(SLOTS, dtype=jnp.int32)[None, :]
    tiles = jnp.take_along_axis(child_maps, picks, axis=1)
    return jnp.where(tiles // BLOCK == block_me, tiles - block_me * BLOCK, -1)


def factor_kernel(k, *refs):
    a_ref = refs[0]
    work_ref, urow_ref, w_ref, uw = refs[-4:]
    order = a_ref.shape[0]
    sub = lax.broadcasted_iota(jnp.int32, (8, TILE), 0)
    lane = lax.broadcasted_iota(jnp.int32, (8, TILE), 1)
    c0 = k * TILE
    c1 = c0 + TILE
    uw[...] = jnp.zeros_like(uw)

    def panel(p, carry):
        r0 = pl.multiple_of(p * 8, 8)
        shift = (TILE - r0) % TILE
        rows = a_ref[pl.ds(c0 + r0, 8), c0:c1]
        eye = (lane == r0 + sub).astype(F32)
        lhs = pltpu.roll(uw[:, 0:TILE], shift, 1)[:, 0:8]
        upd = lax.dot_general(lhs, uw[...], (((0,), (0,)), ((), ())), precision=HI, preferred_element_type=F32)
        ru = rows - upd[:, 0:TILE]
        rw = eye - upd[:, TILE:]
        diag = pltpu.roll(ru, shift, 1)
        cols = [jnp.broadcast_to(diag[:, j : j + 1], (8, TILE)) for j in range(8)]
        pivots = jnp.zeros((8, TILE), F32)
        for j in range(8):
            d = jnp.broadcast_to(cols[j][j : j + 1, :], (8, TILE))
            pivots = jnp.where(sub == j, d, pivots)
            f = jnp.where(sub > j, cols[j] / d, 0.0)
            ru = ru - f * jnp.broadcast_to(ru[j : j + 1, :], (8, TILE))
            rw = rw - f * jnp.broadcast_to(rw[j : j + 1, :], (8, TILE))
            for m in range(j + 1, 8):
                cols[m] = cols[m] - f * jnp.broadcast_to(cols[m][j : j + 1, :], (8, TILE))
        scale = lax.rsqrt(pivots)
        uw[pl.ds(r0, 8), 0:TILE] = jnp.where(lane >= r0 + sub, ru * scale, 0.0)
        uw[pl.ds(r0, 8), TILE:] = rw * scale
        return carry

    lax.fori_loop(0, TILE // 8, panel, 0)
    w = uw[:, TILE:]
    w_ref[...] = w
    if k:
        urow_ref[:, 0:c0] = jnp.zeros((TILE, c0), F32)
    urow_ref[:, c0:c1] = uw[:, 0:TILE]
    if c1 < order:
        urow = jnp.dot(w, a_ref[c0:c1, c1:], precision=HI, preferred_element_type=F32)
        urow_ref[:, c1:] = urow
        work_ref[c1:, c1:] = a_ref[c1:, c1:] - lax.dot_general(
            urow, urow, (((0,), (0,)), ((), ())), precision=HI, preferred_element_type=F32
        )


def factor_step(k, work, after):
    order = work.shape[0]
    return pl.pallas_call(
        lambda *refs: factor_kernel(k, *refs),
        out_shape=(
            jax.ShapeDtypeStruct((order, order), F32),
            jax.ShapeDtypeStruct((TILE, order), F32),
            jax.ShapeDtypeStruct((TILE, TILE), F32),
        ),
        in_specs=[vmem_spec()] + [any_spec()] * len(after),
        out_specs=(vmem_spec(), vmem_spec(), vmem_spec()),
        scratch_shapes=[pltpu.VMEM((TILE, 2 * TILE), F32)],
        input_output_aliases={0: 0},
        cost_estimate=pl.CostEstimate(flops=5_000_000_000, transcendentals=0, bytes_accessed=4_000_000),
        name="factor",
    )(work, *after)


def solve_rows(x_ref, u_refs, w_refs):
    for k in range(len(w_refs)):
        c0 = k * TILE
        c1 = c0 + TILE
        rhs = x_ref[:, c0:c1]
        if k:
            above = jnp.concatenate([u_refs[j][:, c0:c1] for j in range(k)], axis=0)
            rhs = rhs - jnp.dot(x_ref[:, 0:c0], above, precision=HI, preferred_element_type=F32)
        x_ref[:, c0:c1] = lax.dot_general(
            rhs, w_refs[k][...], (((1,), (1,)), ((), ())), precision=HI, preferred_element_type=F32
        )


def solve_kernel(start_ref, *refs):
    steps = (len(refs) - 9) // 2
    u_refs, w_refs = refs[:steps], refs[steps : 2 * steps]
    pieces = refs[2 * steps : 2 * steps + 5]
    own_ref, win_ref, band, sems = refs[2 * steps + 5 :]
    far_low, low, own = pieces[:3]
    copies = []
    at = 0
    for n, piece in enumerate(pieces):
        rows = piece.shape[0]
        copies.append(pltpu.make_async_copy(piece, band.at[pl.ds(at, rows)], sems.at[n]))
        at += rows
    for copy in copies:
        copy.start()
    for copy in copies:
        copy.wait()
    start = pl.multiple_of(start_ref[0] * TILE, TILE)
    own_at = far_low.shape[0] + low.shape[0]
    win_ref[...] = band[pl.ds(start, WIN), :]
    own_ref[...] = band[own_at : own_at + own.shape[0], :]
    solve_rows(win_ref, u_refs, w_refs)
    solve_rows(own_ref, u_refs, w_refs)


def solve(start, urows, inverses, pieces):
    rows = sum(piece.shape[0] for piece in pieces)
    width = urows[0].shape[1]
    own = pieces[2].shape
    return pl.pallas_call(
        solve_kernel,
        out_shape=(jax.ShapeDtypeStruct(own, F32), jax.ShapeDtypeStruct((WIN, width), F32)),
        in_specs=[smem_spec()] + [vmem_spec()] * (2 * len(urows)) + [any_spec()] * 5,
        out_specs=(vmem_spec(), vmem_spec()),
        scratch_shapes=[pltpu.VMEM((rows, width), F32), pltpu.SemaphoreType.DMA((5,))],
        compiler_params=pltpu.CompilerParams(vmem_limit_bytes=40 * 1024 * 1024),
        cost_estimate=pl.CostEstimate(flops=6_000_000_000, transcendentals=0, bytes_accessed=12_000_000),
        name="solve",
    )(start, *urows, *inverses, *pieces)


def pack_columns_kernel(starts_ref, u_ref, *rest):
    outs, sems = rest[:-1], rest[-1]
    copies = []
    for c, (slot, width) in enumerate(CHUNKS):
        for k in range(GROUPS):
            n = c * GROUPS + k
            at = pl.multiple_of((starts_ref[k] + slot) * TILE, TILE)
            copies.append(pltpu.make_async_copy(u_ref.at[:, pl.ds(at, width * TILE)], outs[n], sems.at[n]))
    for copy in copies:
        copy.start()
    for copy in copies:
        copy.wait()


def pack_columns(turned_starts, update):
    rows = update.shape[0]
    shapes = [jax.ShapeDtypeStruct((rows, width * TILE), F32) for _, width in CHUNKS for _ in range(GROUPS)]
    outs = pl.pallas_call(
        pack_columns_kernel,
        out_shape=tuple(shapes),
        in_specs=[smem_spec(), any_spec()],
        out_specs=tuple(any_spec() for _ in shapes),
        scratch_shapes=[pltpu.SemaphoreType.DMA((len(shapes),))],
        cost_estimate=pl.CostEstimate(flops=0, transcendentals=0, bytes_accessed=20_000_000),
        name="pack_columns",
    )(turned_starts, update)
    return [outs[c * GROUPS : (c + 1) * GROUPS] for c in range(len(CHUNKS))]


def pack_rows_kernel(group_ref, slot_ref, *rest):
    pieces, out_ref, sems = rest[:GROUPS], rest[GROUPS], rest[GROUPS + 1]
    copies = []
    for k in range(GROUPS):
        for q in range(CTILES // GROUPS):
            n = k * (CTILES // GROUPS) + q
            src = pieces[k].at[pl.ds(q * TILE, TILE)]
            copies.append(pltpu.make_async_copy(src, out_ref.at[group_ref[n], slot_ref[n]], sems.at[n]))
    for copy in copies:
        copy.start()
    for copy in copies:
        copy.wait()


def pack_rows(groups, slots, pieces):
    width = pieces[0].shape[1]
    return pl.pallas_call(
        pack_rows_kernel,
        out_shape=jax.ShapeDtypeStruct((GROUPS, SLOTS, TILE, width), F32),
        in_specs=[smem_spec(), smem_spec()] + [any_spec()] * GROUPS,
        out_specs=any_spec(),
        scratch_shapes=[pltpu.SemaphoreType.DMA((CTILES,))],
        cost_estimate=pl.CostEstimate(flops=0, transcendentals=0, bytes_accessed=5_000_000),
        name="pack_rows",
    )(groups, slots, *pieces)


def split(x):
    high = x.astype(jnp.bfloat16)
    return high, (x - high.astype(F32)).astype(jnp.bfloat16)


def assemble_kernel(rows_ref, cols_ref, *rest):
    parts = rest[: len(CHUNKS)]
    xf_ref, xr_ref, out_ref, acc, sem = rest[len(CHUNKS) :]
    child = pl.program_id(0)

    @pl.when(child == 0)
    def _():
        acc[...] = jnp.zeros_like(acc)

    rh, rl = split(xr_ref[0])
    rhs = jnp.concatenate([rh, rl, rh], axis=1)
    for s in range(SLOTS):
        row = rows_ref[child, s]

        @pl.when(row >= 0)
        def _():
            fh, fl = split(xf_ref[0, s * TILE : (s + 1) * TILE, :])
            lhs = jnp.concatenate([fh, fh, fl], axis=1)
            prod = lax.dot_general(lhs, rhs, (((1,), (1,)), ((), ())), preferred_element_type=F32)
            at = pl.multiple_of(row * TILE, TILE)
            for c, (slot, width) in enumerate(CHUNKS):
                for w in range(width):
                    t = slot + w
                    col = cols_ref[child, t]

                    @pl.when(col >= 0)
                    def _():
                        tile = parts[c][0, s * TILE : (s + 1) * TILE, w * TILE : (w + 1) * TILE]
                        acc[col, pl.ds(at, TILE), :] += tile - prod[:, t * TILE : (t + 1) * TILE]

    @pl.when(child == pl.num_programs(0) - 1)
    def _():
        copies = [
            pltpu.make_async_copy(acc.at[b], out_ref.at[:, pl.ds(b * TILE, TILE)], sem.at[b]) for b in range(BLOCK)
        ]
        for copy in copies:
            copy.start()
        for copy in copies:
            copy.wait()


def assemble(rows, cols, parts, xf, xr):
    width = xf.shape[2]
    block = lambda n: pl.BlockSpec((1, WIN, n), lambda c: (c, 0, 0))
    return pl.pallas_call(
        assemble_kernel,
        grid=(GROUPS,),
        out_shape=jax.ShapeDtypeStruct((SIDE, SIDE), F32),
        in_specs=[smem_spec(), smem_spec()] + [block(w * TILE) for _, w in CHUNKS] + [block(width)] * 2,
        out_specs=any_spec(),
        scratch_shapes=[pltpu.VMEM((BLOCK, SIDE, TILE), F32), pltpu.SemaphoreType.DMA((BLOCK,))],
        compiler_params=pltpu.CompilerParams(vmem_limit_bytes=48 * 1024 * 1024),
        cost_estimate=pl.CostEstimate(flops=20_000_000_000, transcendentals=0, bytes_accessed=40_000_000),
        name="assemble",
    )(rows, cols, *parts, xf, xr)


def local(pivot_block, panel_rows, update_block, tile_map):
    row_me = lax.axis_index("row")
    front_me = lax.axis_index("front")
    col_me = lax.axis_index("col")
    share = pivot_block.shape[1]
    slab = panel_rows[0]
    half = slab.shape[0] // 2

    tile_ids = lax.dynamic_index_in_dim(tile_map, front_me * 2 + col_me, 0, keepdims=False)
    starts = window_starts(tile_ids)
    child_maps = jnp.take(tile_map, jnp.arange(GROUPS, dtype=jnp.int32) * 2 + col_me, axis=0)
    row_slots = slot_targets(child_maps, front_me)
    col_slots = slot_targets(child_maps, row_me)

    pivot = lax.all_gather(pivot_block[0], "row", axis=0, tiled=True)

    up = lambda n: [(i, i + n) for i in range(GROUPS - n)]
    down = lambda n: [(i + n, i) for i in range(GROUPS - n)]
    pieces = (
        lax.ppermute(slab[half:], "row", up(2)),
        lax.ppermute(slab, "row", up(1)),
        slab,
        lax.ppermute(slab, "row", down(1)),
        lax.ppermute(slab[:half], "row", down(2)),
    )
    start = lax.dynamic_index_in_dim(starts, row_me, 0, keepdims=True) - 4 * row_me + 6

    groups = tile_ids // BLOCK
    order = (row_me - jnp.arange(GROUPS, dtype=jnp.int32)) % GROUPS
    tiles = (order[:, None] * 4 + jnp.arange(4, dtype=jnp.int32)[None, :]).reshape(-1)
    tile_groups = jnp.take(groups, tiles)
    tile_slots = tiles - jnp.take(starts, tile_groups)
    ahead = jnp.take(starts, (row_me + jnp.arange(GROUPS, dtype=jnp.int32)) % GROUPS)

    ring = lambda k: [(i, (i + k) % GROUPS) for i in range(GROUPS)]
    chunks = pack_columns(ahead, update_block[0])
    parts = []
    marks = [chunks[0][0]]
    for packed in chunks:
        arrived = [packed[0]] + [lax.ppermute(packed[k], "row", ring(k)) for k in range(1, GROUPS)]
        arrived = pack_rows(tile_groups, tile_slots, arrived).reshape(GROUPS, WIN, -1)
        marks.append(arrived)
        parts.append(lax.all_to_all(arrived, "front", split_axis=0, concat_axis=0, tiled=True))

    urows, inverses = [], []
    work = pivot
    for k in range(4):
        work, urow, inverse = factor_step(k, work, marks[k : k + 1] if k < 3 else [])
        urows.append(urow)
        inverses.append(inverse)
    own_factor, window = solve(start, urows, inverses, pieces)

    mirror = [(a * GROUPS + b, b * GROUPS + a) for a in range(GROUPS) for b in range(GROUPS)]
    turned = lax.ppermute(window, ("front", "row"), mirror)
    xf = lax.all_gather(turned, "row", axis=0)
    xr = lax.all_gather(window, "front", axis=0)
    parent = assemble(row_slots, col_slots, parts, xf, xr)
    lower_rows = jnp.concatenate([lax.dynamic_slice_in_dim(urow, row_me * share, share, 1) for urow in urows], axis=0).T
    return (lower_rows[None], own_factor[None], parent[None])


def solution(mesh):
    return jax.shard_map(
        local,
        mesh=mesh,
        in_specs=(
            P(("front", "col"), "row", None),
            P(("front", "col"), "row", None),
            P(("front", "col"), "row", None),
            P(),
        ),
        out_specs=(
            P(("front", "col"), "row", None),
            P(("front", "col"), "row", None),
            P("col", "front", "row"),
        ),
        check_vma=False,
    )
```

time: 738 us -> 1090 us (1.48)
  Pallas kernels: 0 us -> 735 us
  waiting for transfers between devices: 262 us -> 116 us
  other arithmetic: 143 us -> 2.65 us
  starting transfers between devices: 7.46 us -> 139 us
  matrix products: 92.9 us -> 0 us
  local copies, waits for them, and re-layouts: 82.6 us -> 12.9 us
  blocking collectives: 122 us -> 67.7 us
    pallas_call x0 -> x10, Pallas kernels: none -> 735 us  [the longest x3 324 us: pack_rows(): pl.pallas_call(pack_rows_kernel, out_shape=jax.ShapeDtypeStruct((GROUPS,...]
    another operation x17 -> x0, other arithmetic: 120 us -> none  [the longest x14 78.6 us: local(): lower_factor = jnp.linalg.cholesky(pivot_whole)]
    all_to_all x1 -> x2, waiting for transfers between devices: 188 us -> 72 us  [local(): lax.all_to_all(arrived, 'front', split_axis=0, concat_axis=0, tiled=True)]
    ppermute x0 -> x26, starting transfers between devices: none -> 102 us  [the longest x21 86.6 us: local(): lax.ppermute(packed[k], 'row', ring(k))]
    dot_general x3 -> x0, matrix products: 87.9 us -> none  [the longest x1 37.8 us: local(): jnp.einsum('fas,fsxby->axby', row_hot, partial_value, precision=lax.Preci...]
    all_gather x2 -> x3, waiting for transfers between devices: 73.8 us -> 0.02 us  [the longest x1 0.02 us: local(): pivot = lax.all_gather(pivot_block[0], 'row', axis=0, tiled=True)]
    all_to_all x1, blocking collectives: 122 us -> 67.7 us  [local(): lax.all_to_all(arrived, 'front', split_axis=0, concat_axis=0, tiled=True)]
    ppermute x0 -> x26, waiting for transfers between devices: none -> 43.4 us  [the longest x1 26.1 us: local(): turned = lax.ppermute(window, ('front', 'row'), mirror)]
  transfers between devices with their start and end apart: 3 -> 31, of which waited for: 3 -> 6; matrix products, arithmetic and copies ran while one was open for 1% -> 1% of each run, Pallas kernels for 0% -> 63%
where the time goes in v1:
time: 1090 us
  Pallas kernels  735 us (67%)
  starting transfers between devices  139 us (13%)
  waiting for transfers between devices  116 us (11%)
  blocking collectives  67.7 us (6%)
  between operations  14.8 us (1%)
  local copies, waits for them, and re-layouts  12.9 us (1%)
    pallas_call x3, Pallas kernels, pack_rows(): pl.pallas_call(pack_rows_kernel, out_shape=jax.ShapeDtypeStruct((GROUPS,...  324 us
    pallas_call x1, Pallas kernels, pack_columns(): pl.pallas_call(pack_columns_kernel, out_shape=tuple(shapes), in_specs=[sm...  320 us
    ppermute x21, starting transfers between devices, local(): lax.ppermute(packed[k], 'row', ring(k))  86.6 us
    all_to_all x2, waiting for transfers between devices, local(): lax.all_to_all(arrived, 'front', split_axis=0, concat_axis=0, tiled=True)  72 us
    all_to_all x1, blocking collectives, local(): lax.all_to_all(arrived, 'front', split_axis=0, concat_axis=0, tiled=True)  67.7 us
    pallas_call x4, Pallas kernels, factor_step(): pl.pallas_call(lambda *refs: factor_kernel(k, *refs), out_shape=(jax.Shap...  45.9 us
    all_to_all x2, starting transfers between devices, local(): lax.all_to_all(arrived, 'front', split_axis=0, concat_axis=0, tiled=True)  37 us
    pallas_call x1, Pallas kernels, assemble(): pl.pallas_call(assemble_kernel, grid=(GROUPS,), out_shape=jax.ShapeDtypeS...  35.1 us
  transfers between devices with their start and end apart: 31, of which 6 were waited for; matrix products, arithmetic and copies ran while one was open for 1% of the time, Pallas kernels for 63%

profile of v1, /device:TPU:14, one launch (start us, length us, event | category | flops | bytes accessed | tf_op | source)
XLA Modules:
  0.0 1088.5 jit_solution(17038032965323460100)
XLA Ops:
  10.0 319.6 %pack_columns.1 = (f32[512,128]{1,0:T(8,128)}, f32[512,128]{1,0:T(8,128)}, f32[512,128]{1,0:T(8,128)}, f32[512,128]{1,0:T(8,128)}, f32[512,128]{1,0:T(8,128)}, /...) custom-call(s32[8]{0:T(128)} %get-tuple-element.97.starts_ref, ...), custom_call_target="tpu_custom_call" | custom-call | bytes 20000000 | tf_op jit(solution)/shard_map/pack_columns/pallas_call | solution.py:184
  339.5 5.8 collective-permute-start.4
  345.2 5.1 collective-permute-done.2.rest_3_
  352.1 5.0 collective-permute-start.6
  357.8 10.4 collective-permute-start.9
  368.2 3.5 collective-permute-start.10
  378.8 65.6 %pack_rows.3 = f32[8,5,128,128]{3,2,1,0:T(8,128)} custom-call(s32[32]{0:T(128)} %get-tuple-element.91.group_ref, s32[32]{0:T(128)} %get-tuple-element.90.slot_ref, f32[512,128]{1,0:T(8,128)} %get-tuple-element.41.refs_1_.rest_0_, f32[512,128]{1,0:T(8,128)} %copy-done.13, f32[512,128]{1,0:T(8,128)} %copy-done.14, f32[512,128]{1,0:T(8,128)} %copy-done.15, ...), custom_call_target="tpu_custom_call" | custom-call | bytes 5000000 | tf_op jit(solution)/shard_map/pack_rows/pallas_call | solution.py:212
  450.0 6.5 collective-permute-start.17
  458.6 129.2 %pack_rows.4 = f32[8,5,128,256]{3,2,1,0:T(8,128)} custom-call(s32[32]{0:T(128)} %get-tuple-element.91.group_ref, s32[32]{0:T(128)} %get-tuple-element.90.slot_ref, f32[512,256]{1,0:T(8,128)} %get-tuple-element.53.rest_0_, f32[512,256]{1,0:T(8,128)} %copy-done.10, f32[512,256]{1,0:T(8,128)} %copy-done.11, f32[512,256]{1,0:T(8,128)} %copy-done.12, ...), custom_call_target="tpu_custom_call" | custom-call | bytes 5000000 | tf_op jit(solution)/shard_map/pack_rows/pallas_call | solution.py:212
  587.8 12.0 %factor.4 = (f32[512,512]{1,0:T(8,128)}, f32[128,512]{1,0:T(8,128)}, f32[128,128]{1,0:T(8,128)}) custom-call(f32[512,512]{1,0:T(8,128)} %bitcast.56, f32[512,128]{1,0:T(8,128)} %get-tuple-element.41.refs_1_.rest_0_), custom_call_target="tpu_custom_call", output_to_operand_aliasing={{0}: (0, {})} | custom-call | flops 5000000000 | bytes 4000000 | tf_op jit(solution)/shard_map/factor/pallas_call | solution.py:98
  599.7 11.7 %factor.5 = (f32[512,512]{1,0:T(8,128)}, f32[128,512]{1,0:T(8,128)}, f32[128,128]{1,0:T(8,128)}) custom-call(f32[512,512]{1,0:T(8,128)} %get-tuple-element.43.refs_0_, f32[8,640,128]{2,1,0:T(8,128)} %bitcast.51), custom_call_target="tpu_custom_call", output_to_operand_aliasing={{0}: (0, {})} | custom-call | flops 5000000000 | bytes 4000000 | tf_op jit(solution)/shard_map/factor/pallas_call | solution.py:98
  611.5 11.4 %factor.6 = (f32[512,512]{1,0:T(8,128)}, f32[128,512]{1,0:T(8,128)}, f32[128,128]{1,0:T(8,128)}) custom-call(f32[512,512]{1,0:T(8,128)} %get-tuple-element.52.refs_0_, f32[8,640,256]{2,1,0:T(8,128)} %bitcast.48), custom_call_target="tpu_custom_call", output_to_operand_aliasing={{0}: (0, {})} | custom-call | flops 5000000000 | bytes 4000000 | tf_op jit(solution)/shard_map/factor/pallas_call | solution.py:98
  622.9 10.8 factor.7
  636.4 10.8 solve.1
  649.3 26.1 %collective-permute-done.25 = f32[640,512]{1,0:T(8,128)S(1)} collective-permute-done((f32[640,512]{1,0:T(8,128)}, f32[640,512]{1,0:T(8,128)S(1)}, u32[]{:S(2)}, u32[]{:S(2)}) %collective-permute-start.25) | collective-permute-done | bytes 1310752 | tf_op jit(solution)/shard_map/ppermute | solution.py:338
  676.5 30.2 %all-to-all-start = ((f32[8,640,128]{2,1,0:T(8,128)}), f32[8,640,128]{2,1,0:T(8,128)S(1)}, u32[]{:S(2)}, u32[]{:S(2)}) async-start(f32[8,640,128]{2,1,0:T(8,128)} %bitcast.52), calls=%async_computation | async-start | bytes 5242880 | tf_op jit(solution)/shard_map/all_to_all | solution.py:327
  717.6 7.9 collective-permute-start.23
  725.6 33.4 %collective-permute-start.24 = (f32[512,256]{1,0:T(8,128)}, f32[512,256]{1,0:T(8,128)}, u32[]{:S(2)}, u32[]{:S(2)}) collective-permute-start(f32[512,256]{1,0:T(8,128)} %get-tuple-element.76), channel_id=1, source_target_pairs={{0,14},{2,0},{4,2},{6,4},{8,6},{10,8},{12,10},{14,12},{1,15},{3,1}... | collective-permute-start | bytes 1572872 | tf_op jit(solution)/shard_map/ppermute | solution.py:324
  759.0 7.0 collective-permute-done.24.rest_7_
  766.0 129.1 %pack_rows.5 = f32[8,5,128,256]{3,2,1,0:T(8,128)} custom-call(s32[32]{0:T(128)} %get-tuple-element.91.group_ref, s32[32]{0:T(128)} %get-tuple-element.90.slot_ref, f32[512,256]{1,0:T(8,128)} %get-tuple-element.69.rest_0_, f32[512,256]{1,0:T(8,128)} %collective-permute-done.18.rest_1_, f32[512,256]{1,0:T(8,128)} %collective-permute-done.19.rest_2_, ...), custom_call_target="tpu_custom_call" | custom-call | bytes 5000000 | tf_op jit(solution)/shard_map/pack_rows/pallas_call | solution.py:212
  895.2 67.7 %all_to_all.15.rest_2_ = f32[8,640,256]{2,1,0:T(8,128)} all-to-all(f32[8,640,256]{2,1,0:T(8,128)} %bitcast.50), channel_id=1, replica_groups=mesh['front'=8,'row'=8,'col'=2] {'front'}, dimensions={0} | all-to-all | bytes 10485760 | tf_op jit(solution)/shard_map/all_to_all | solution.py:327
  962.8 6.8 all-to-all-start.1
  974.9 72.0 %all-to-all-done.1.rest_1_ = f32[8,640,256]{2,1,0:T(8,128)} async-done(((f32[8,640,256]{2,1,0:T(8,128)}), f32[8,640,256]{2,1,0:T(8,128)}, u32[]{:S(2)}, u32[]{:S(2)}) %all-to-all-start.1) | async-done | bytes 5242912 | tf_op jit(solution)/shard_map/all_to_all | solution.py:327
  1046.9 35.1 %assemble.1 = f32[1536,1536]{1,0:T(8,128)} custom-call(s32[8,5]{1,0:T(8,128)S(1)} %subtract_select_fusion.1.rows_ref, s32[8,5]{1,0:T(8,128)S(1)} %subtract_select_fusion.cols_ref, f32[8,640,128]{2,1,0:T(8,128)S(1)} %all-to-all-done.rest_0_, f32[8,640,256]{2,1,0:T(8,128)} %all-to-all-done.1.rest_1_, f32[8,640,256]{2,1,0:T(8,128)} %all_to_all.15.rest_2_, ...), custom_call_target="tpu_custom_call" | custom-call | flops 20000000000 | bytes 40000000 | tf_op jit(solution)/shard_map/assemble/pallas_call | solution.py:272
  (130 shorter events, 51.0 us)
Async XLA Ops:
  7.2 580.6 %all-gather.7.cloned.1.call-start = ((), (), s32[]{:S(2)}) async-start(), calls=%async_computation.3 | async-start | bytes 1179648 | tf_op jit(solution)/shard_map/all_gather | solution.py:299
  7.9 1039.0 %all-gather.11.cloned.1.call-start = ((), (), s32[]{:S(2)}) async-start(), calls=%async_computation.5 | async-start | bytes 11796480 | tf_op jit(solution)/shard_map/all_gather | solution.py:340
  332.3 19.8 %collective-permute-start.3 = (f32[512,128]{1,0:T(8,128)}, f32[512,128]{1,0:T(8,128)S(1)}, u32[]{:S(2)}, u32[]{:S(2)}) collective-permute-start(f32[512,128]{1,0:T(8,128)} %get-tuple-element.47), channel_id=1, source_target_pairs={{0,8},{2,10},{4,12},{6,14},{8,0},{10,2},{12,4},{14,6},{1,9},{3,11}... | collective-permute-start | bytes 786440 | tf_op jit(solution)/shard_map/ppermute | solution.py:324
  334.8 37.0 %collective-permute-start.7 = (f32[512,256]{1,0:T(8,128)}, f32[512,256]{1,0:T(8,128)S(1)}, u32[]{:S(2)}, u32[]{:S(2)}) collective-permute-start(f32[512,256]{1,0:T(8,128)} %get-tuple-element.54), channel_id=1, source_target_pairs={{0,2},{2,4},{4,6},{6,8},{8,10},{10,12},{12,14},{14,0},{1,3},{3,5},... | collective-permute-start | bytes 1572872 | tf_op jit(solution)/shard_map/ppermute | solution.py:324
  337.9 35.1 %collective-permute-start.8 = (f32[512,256]{1,0:T(8,128)}, f32[512,256]{1,0:T(8,128)S(1)}, u32[]{:S(2)}, u32[]{:S(2)}) collective-permute-start(f32[512,256]{1,0:T(8,128)} %get-tuple-element.55), channel_id=1, source_target_pairs={{0,4},{2,6},{4,8},{6,10},{8,12},{10,14},{12,0},{14,2},{1,5},{3,7},... | collective-permute-start | bytes 1572872 | tf_op jit(solution)/shard_map/ppermute | solution.py:324
  352.1 19.6 %collective-permute-start.6 = (f32[512,128]{1,0:T(8,128)}, f32[512,128]{1,0:T(8,128)}, u32[]{:S(2)}, u32[]{:S(2)}) collective-permute-start(f32[512,128]{1,0:T(8,128)} %get-tuple-element.50), channel_id=1, source_target_pairs={{0,14},{2,0},{4,2},{6,4},{8,6},{10,8},{12,10},{14,12},{1,15},{3,1}... | collective-permute-start | bytes 786440 | tf_op jit(solution)/shard_map/ppermute | solution.py:324
  357.8 86.6 %collective-permute-start.9 = (f32[512,256]{1,0:T(8,128)}, f32[512,256]{1,0:T(8,128)S(1)}, u32[]{:S(2)}, u32[]{:S(2)}) collective-permute-start(f32[512,256]{1,0:T(8,128)} %get-tuple-element.56), channel_id=1, source_target_pairs={{0,6},{2,8},{4,10},{6,12},{8,14},{10,0},{12,2},{14,4},{1,7},{3,9},... | collective-permute-start | bytes 1572872 | tf_op jit(solution)/shard_map/ppermute | solution.py:324
  368.2 79.0 %collective-permute-start.10 = (f32[512,256]{1,0:T(8,128)}, f32[512,256]{1,0:T(8,128)}, u32[]{:S(2)}, u32[]{:S(2)}) collective-permute-start(f32[512,256]{1,0:T(8,128)} %get-tuple-element.57), channel_id=1, source_target_pairs={{0,8},{2,10},{4,12},{6,14},{8,0},{10,2},{12,4},{14,6},{1,9},{3,11}... | collective-permute-start | bytes 1572872 | tf_op jit(solution)/shard_map/ppermute | solution.py:324
  371.7 78.2 %collective-permute-start.11 = (f32[512,256]{1,0:T(8,128)}, f32[512,256]{1,0:T(8,128)}, u32[]{:S(2)}, u32[]{:S(2)}) collective-permute-start(f32[512,256]{1,0:T(8,128)} %get-tuple-element.58), channel_id=1, source_target_pairs={{0,10},{2,12},{4,14},{6,0},{8,2},{10,4},{12,6},{14,8},{1,11},{3,13... | collective-permute-start | bytes 1572872 | tf_op jit(solution)/shard_map/ppermute | solution.py:324
  371.7 84.7 %collective-permute-start.12 = (f32[512,256]{1,0:T(8,128)}, f32[512,256]{1,0:T(8,128)}, u32[]{:S(2)}, u32[]{:S(2)}) collective-permute-start(f32[512,256]{1,0:T(8,128)} %get-tuple-element.59), channel_id=1, source_target_pairs={{0,12},{2,14},{4,0},{6,2},{8,4},{10,6},{12,8},{14,10},{1,13},{3,15... | collective-permute-start | bytes 1572872 | tf_op jit(solution)/shard_map/ppermute | solution.py:324
  373.0 85.6 %collective-permute-start.13 = (f32[512,256]{1,0:T(8,128)}, f32[512,256]{1,0:T(8,128)}, u32[]{:S(2)}, u32[]{:S(2)}) collective-permute-start(f32[512,256]{1,0:T(8,128)} %get-tuple-element.60), channel_id=1, source_target_pairs={{0,14},{2,0},{4,2},{6,4},{8,6},{10,8},{12,10},{14,12},{1,15},{3,1}... | collective-permute-start | bytes 1572872 | tf_op jit(solution)/shard_map/ppermute | solution.py:324
  445.3 188.5 %collective-permute-start.16 = (f32[512,512]{1,0:T(8,128)S(1)}, f32[512,512]{1,0:T(8,128)S(1)}, u32[]{:S(2)}, u32[]{:S(2)}) collective-permute-start(f32[512,512]{1,0:T(8,128)S(1)} %bitcast.45), channel_id=1, source_target_pairs={{2,0},{4,2},{6,4},{8,6},{10,8},{12,10},{14,12},{3,1},{5,3},{7,5},{... | collective-permute-start | bytes 3145736 | tf_op jit(solution)/shard_map/ppermute | solution.py:307
  447.2 186.6 %collective-permute-start.15 = (f32[512,512]{1,0:T(8,128)S(1)}, f32[512,512]{1,0:T(8,128)}, u32[]{:S(2)}, u32[]{:S(2)}) collective-permute-start(f32[512,512]{1,0:T(8,128)S(1)} %bitcast.46), channel_id=1, source_target_pairs={{0,2},{2,4},{4,6},{6,8},{8,10},{10,12},{12,14},{1,3},{3,5},{5,7},{... | collective-permute-start | bytes 3145736 | tf_op jit(solution)/shard_map/ppermute | solution.py:305
  450.0 183.8 %collective-permute-start.17 = (f32[256,512]{1,0:T(8,128)}, f32[256,512]{1,0:T(8,128)S(1)}, u32[]{:S(2)}, u32[]{:S(2)}) collective-permute-start(f32[256,512]{1,0:T(8,128)} %get-tuple-element.95), channel_id=1, source_target_pairs={{4,0},{6,2},{8,4},{10,6},{12,8},{14,10},{5,1},{7,3},{9,5},{11,7},{... | collective-permute-start | bytes 1572872 | tf_op jit(solution)/shard_map/ppermute | solution.py:308
  456.5 177.3 %collective-permute-start.14 = (f32[256,512]{1,0:T(8,128)}, f32[256,512]{1,0:T(8,128)}, u32[]{:S(2)}, u32[]{:S(2)}) collective-permute-start(f32[256,512]{1,0:T(8,128)} %get-tuple-element.96), channel_id=1, source_target_pairs={{0,4},{2,6},{4,8},{6,10},{8,12},{10,14},{1,5},{3,7},{5,9},{7,11},{... | collective-permute-start | bytes 1572872 | tf_op jit(solution)/shard_map/ppermute | solution.py:304
  647.3 399.6 %all-gather.9.cloned.1.call-start = ((), (), s32[]{:S(2)}) async-start(), calls=%async_computation.4 | async-start | bytes 11796480 | tf_op jit(solution)/shard_map/all_gather | solution.py:339
  647.4 28.1 %collective-permute-start.25 = (f32[640,512]{1,0:T(8,128)}, f32[640,512]{1,0:T(8,128)S(1)}, u32[]{:S(2)}, u32[]{:S(2)}) collective-permute-start(f32[640,512]{1,0:T(8,128)} %get-tuple-element.77), channel_id=1, source_target_pairs={{0,0},{2,16},{4,32},{6,48},{8,64},{10,80},{12,96},{14,112},{16,2},... | collective-permute-start | bytes 3932168 | tf_op jit(solution)/shard_map/ppermute | solution.py:338
  676.5 218.6 %all-to-all-start = ((f32[8,640,128]{2,1,0:T(8,128)}), f32[8,640,128]{2,1,0:T(8,128)S(1)}, u32[]{:S(2)}, u32[]{:S(2)}) async-start(f32[8,640,128]{2,1,0:T(8,128)} %bitcast.52), calls=%async_computation | async-start | bytes 5242880 | tf_op jit(solution)/shard_map/all_to_all | solution.py:327
  711.6 47.3 %collective-permute-start.20 = (f32[512,256]{1,0:T(8,128)}, f32[512,256]{1,0:T(8,128)}, u32[]{:S(2)}, u32[]{:S(2)}) collective-permute-start(f32[512,256]{1,0:T(8,128)} %get-tuple-element.72), channel_id=1, source_target_pairs={{0,6},{2,8},{4,10},{6,12},{8,14},{10,0},{12,2},{14,4},{1,7},{3,9},... | collective-permute-start | bytes 1572872 | tf_op jit(solution)/shard_map/ppermute | solution.py:324
  712.4 46.6 %collective-permute-start.21 = (f32[512,256]{1,0:T(8,128)}, f32[512,256]{1,0:T(8,128)}, u32[]{:S(2)}, u32[]{:S(2)}) collective-permute-start(f32[512,256]{1,0:T(8,128)} %get-tuple-element.73), channel_id=1, source_target_pairs={{0,8},{2,10},{4,12},{6,14},{8,0},{10,2},{12,4},{14,6},{1,9},{3,11}... | collective-permute-start | bytes 1572872 | tf_op jit(solution)/shard_map/ppermute | solution.py:324
  715.1 43.9 %collective-permute-start.22 = (f32[512,256]{1,0:T(8,128)}, f32[512,256]{1,0:T(8,128)}, u32[]{:S(2)}, u32[]{:S(2)}) collective-permute-start(f32[512,256]{1,0:T(8,128)} %get-tuple-element.74), channel_id=1, source_target_pairs={{0,10},{2,12},{4,14},{6,0},{8,2},{10,4},{12,6},{14,8},{1,11},{3,13... | collective-permute-start | bytes 1572872 | tf_op jit(solution)/shard_map/ppermute | solution.py:324
  717.6 41.4 %collective-permute-start.23 = (f32[512,256]{1,0:T(8,128)}, f32[512,256]{1,0:T(8,128)}, u32[]{:S(2)}, u32[]{:S(2)}) collective-permute-start(f32[512,256]{1,0:T(8,128)} %get-tuple-element.75), channel_id=1, source_target_pairs={{0,12},{2,14},{4,0},{6,2},{8,4},{10,6},{12,8},{14,10},{1,13},{3,15... | collective-permute-start | bytes 1572872 | tf_op jit(solution)/shard_map/ppermute | solution.py:324
  725.6 40.4 %collective-permute-start.24 = (f32[512,256]{1,0:T(8,128)}, f32[512,256]{1,0:T(8,128)}, u32[]{:S(2)}, u32[]{:S(2)}) collective-permute-start(f32[512,256]{1,0:T(8,128)} %get-tuple-element.76), channel_id=1, source_target_pairs={{0,14},{2,0},{4,2},{6,4},{8,6},{10,8},{12,10},{14,12},{1,15},{3,1}... | collective-permute-start | bytes 1572872 | tf_op jit(solution)/shard_map/ppermute | solution.py:324
  962.8 84.0 %all-to-all-start.1 = ((f32[8,640,256]{2,1,0:T(8,128)}), f32[8,640,256]{2,1,0:T(8,128)}, u32[]{:S(2)}, u32[]{:S(2)}) async-start(f32[8,640,256]{2,1,0:T(8,128)} %bitcast.49), calls=%async_computation.1 | async-start | bytes 10485760 | tf_op jit(solution)/shard_map/all_to_all | solution.py:327
  (25 other events, 788.4 us)
Sparse Core Ops, SparseCore 0:
  9.7 23.9 all-gather.6
  647.4 168.4 all-gather.10
  817.6 58.6 all-gather.8

commit v2 on v0

v2 whole, which is shorter than its diff:
```python
import jax
import jax.numpy as jnp
from jax import lax
from jax.experimental import pallas as pl
from jax.experimental.pallas import tpu as pltpu
from jax.sharding import PartitionSpec as P

TILE = 128
BLOCK = 12
SLOTS = 5
GROUPS = 8
CTILES = 32
WIN = SLOTS * TILE
SIDE = BLOCK * TILE
CHUNKS = ((0, 1), (1, 2), (3, 2))
HI = lax.Precision.HIGHEST
F32 = jnp.float32


def any_spec():
    return pl.BlockSpec(memory_space=pl.ANY)


def hbm(x):
    return pltpu.with_memory_space_constraint(x, pltpu.HBM)


def smem_spec():
    return pl.BlockSpec(memory_space=pltpu.SMEM)


def vmem_spec():
    return pl.BlockSpec(memory_space=pltpu.VMEM)


def window_starts(tile_ids):
    owners = tile_ids // BLOCK
    blocks = jnp.arange(GROUPS, dtype=jnp.int32)
    starts = jnp.sum((owners[..., None, :] < blocks[:, None]).astype(jnp.int32), axis=-1)
    return jnp.minimum(starts, CTILES - SLOTS)


def slot_targets(child_maps, block_me):
    first = jnp.sum((child_maps // BLOCK < block_me).astype(jnp.int32), axis=1)
    first = jnp.minimum(first, CTILES - SLOTS)
    picks = first[:, None] + jnp.arange(SLOTS, dtype=jnp.int32)[None, :]
    tiles = jnp.take_along_axis(child_maps, picks, axis=1)
    return jnp.where(tiles // BLOCK == block_me, tiles - block_me * BLOCK, -1)


def factor_kernel(a_ref, *refs):
    u_ref, v_ref, work, uw = refs[-4:]
    order = a_ref.shape[0]
    sub = lax.broadcasted_iota(jnp.int32, (8, TILE), 0)
    lane = lax.broadcasted_iota(jnp.int32, (8, TILE), 1)
    work[...] = a_ref[...]
    u_ref[...] = jnp.zeros_like(u_ref)
    v_ref[...] = jnp.zeros_like(v_ref)
    for k in range(order // TILE):
        c0 = k * TILE
        c1 = c0 + TILE
        uw[...] = jnp.zeros_like(uw)

        def panel(p, carry):
            r0 = pl.multiple_of(p * 8, 8)
            shift = (TILE - r0) % TILE
            rows = work[pl.ds(c0 + r0, 8), c0:c1]
            eye = (lane == r0 + sub).astype(F32)
            lhs = pltpu.roll(uw[:, 0:TILE], shift, 1)[:, 0:8]
            upd = lax.dot_general(lhs, uw[...], (((0,), (0,)), ((), ())), precision=HI, preferred_element_type=F32)
            ru = rows - upd[:, 0:TILE]
            rw = eye - upd[:, TILE:]
            diag = pltpu.roll(ru, shift, 1)
            cols = [jnp.broadcast_to(diag[:, j : j + 1], (8, TILE)) for j in range(8)]
            pivots = jnp.zeros((8, TILE), F32)
            for j in range(8):
                d = jnp.broadcast_to(cols[j][j : j + 1, :], (8, TILE))
                pivots = jnp.where(sub == j, d, pivots)
                f = jnp.where(sub > j, cols[j] / d, 0.0)
                ru = ru - f * jnp.broadcast_to(ru[j : j + 1, :], (8, TILE))
                rw = rw - f * jnp.broadcast_to(rw[j : j + 1, :], (8, TILE))
                for m in range(j + 1, 8):
                    cols[m] = cols[m] - f * jnp.broadcast_to(cols[m][j : j + 1, :], (8, TILE))
            scale = lax.rsqrt(pivots)
            uw[pl.ds(r0, 8), 0:TILE] = jnp.where(lane >= r0 + sub, ru * scale, 0.0)
            uw[pl.ds(r0, 8), TILE:] = rw * scale
            return carry

        lax.fori_loop(0, TILE // 8, panel, 0)
        w = uw[:, TILE:]
        u_ref[c0:c1, c0:c1] = uw[:, 0:TILE]
        if c1 < order:
            urow = jnp.dot(w, work[c0:c1, c1:], precision=HI, preferred_element_type=F32)
            u_ref[c0:c1, c1:] = urow
            work[c1:, c1:] = work[c1:, c1:] - lax.dot_general(
                urow, urow, (((0,), (0,)), ((), ())), precision=HI, preferred_element_type=F32
            )
        wt = w.T
        v_ref[c0:c1, c0:c1] = wt
        if k:
            above = jnp.dot(u_ref[0:c0, c0:c1], wt, precision=HI, preferred_element_type=F32)
            v_ref[0:c0, c0:c1] = -jnp.dot(v_ref[0:c0, 0:c0], above, precision=HI, preferred_element_type=F32)


def factor(pivot, after):
    whole = jax.ShapeDtypeStruct(pivot.shape, F32)
    return pl.pallas_call(
        factor_kernel,
        out_shape=(whole, whole),
        in_specs=[vmem_spec()] + [any_spec()] * len(after),
        out_specs=(vmem_spec(), vmem_spec()),
        scratch_shapes=[pltpu.VMEM(pivot.shape, F32), pltpu.VMEM((TILE, 2 * TILE), F32)],
        compiler_params=pltpu.CompilerParams(vmem_limit_bytes=16 * 1024 * 1024),
        cost_estimate=pl.CostEstimate(flops=20_000_000_000, transcendentals=0, bytes_accessed=4_000_000),
        name="factor",
    )(pivot, *after)


def split(x):
    high = x.astype(jnp.bfloat16)
    return high, (x - high.astype(F32)).astype(jnp.bfloat16)


def solve_kernel(all_ref, own_ref, v_ref, *refs):
    high_ref, low_ref, out_ref, rhs = refs[-4:]
    order = v_ref.shape[0]

    @pl.when(pl.program_id(0) == 0)
    def _():
        vh, vl = split(v_ref[...])
        rhs[0:order] = vh
        rhs[order : 2 * order] = vl
        rhs[2 * order :] = vh
        out_ref[...] = jnp.dot(own_ref[...], v_ref[...], precision=HI, preferred_element_type=F32)

    bh, bl = split(all_ref[...])
    lhs = jnp.concatenate([bh, bh, bl], axis=1)
    x = jnp.dot(lhs, rhs[...], preferred_element_type=F32)
    high_ref[...], low_ref[...] = split(x)


def solve(panel_all, slab, inverse, after):
    rows, order = slab.shape
    blocks = panel_all.shape[0] // rows
    whole = lambda shape: pl.BlockSpec(shape, lambda i: (0, 0))
    block = pl.BlockSpec((rows, order), lambda i: (i, 0))
    return pl.pallas_call(
        solve_kernel,
        grid=(blocks,),
        out_shape=(
            pltpu.HBM(panel_all.shape, jnp.bfloat16),
            pltpu.HBM(panel_all.shape, jnp.bfloat16),
            jax.ShapeDtypeStruct(slab.shape, F32),
        ),
        in_specs=[block, whole(slab.shape), whole(inverse.shape)] + [any_spec()] * len(after),
        out_specs=(block, block, whole(slab.shape)),
        scratch_shapes=[pltpu.VMEM((3 * order, order), jnp.bfloat16)],
        compiler_params=pltpu.CompilerParams(vmem_limit_bytes=32 * 1024 * 1024),
        cost_estimate=pl.CostEstimate(flops=8_000_000_000, transcendentals=0, bytes_accessed=20_000_000),
        name="solve",
    )(hbm(panel_all), slab, inverse, *after)


def pack_columns_kernel(starts_ref, turned_ref, u_ref, first_ref, *rest):
    outs, (held, in_sems, out_sems) = rest[:-3], rest[-3:]
    bands = in_sems.shape[0]
    rows = u_ref.shape[0] // bands
    loads = []
    for b in range(bands):
        band = pl.ds(b * rows, rows)
        loads.append(pltpu.make_async_copy(u_ref.at[band], held.at[band], in_sems.at[b]))
    for load in loads:
        load.start()
    stores = []
    for b in range(bands):
        band = pl.ds(b * rows, rows)
        loads[b].wait()
        for k in range(GROUPS):
            for c, (slot, width) in enumerate(CHUNKS):
                starts = turned_ref if c else starts_ref
                at = pl.multiple_of((starts[k] + slot) * TILE, TILE)
                src = held.at[band, pl.ds(at, width * TILE)]
                dst = outs[(c - 1) * GROUPS + k].at[band] if c else first_ref.at[k, band]
                store = pltpu.make_async_copy(src, dst, out_sems.at[b, c, k])
                store.start()
                stores.append(store)
    for store in stores:
        store.wait()


def pack_columns(starts, turned_starts, update):
    rows = update.shape[0]
    first, *others = (width * TILE for _, width in CHUNKS)
    pieces = tuple(pltpu.HBM((rows, other), F32) for other in others for _ in range(GROUPS))
    outs = pl.pallas_call(
        pack_columns_kernel,
        out_shape=(pltpu.HBM((GROUPS, rows, first), F32), *pieces),
        in_specs=[smem_spec()] * 2 + [any_spec()],
        out_specs=(any_spec(),) * (1 + len(pieces)),
        scratch_shapes=[
            pltpu.VMEM(update.shape, F32),
            pltpu.SemaphoreType.DMA((4,)),
            pltpu.SemaphoreType.DMA((4, len(CHUNKS), GROUPS)),
        ],
        compiler_params=pltpu.CompilerParams(vmem_limit_bytes=20 * 1024 * 1024),
        cost_estimate=pl.CostEstimate(flops=0, transcendentals=0, bytes_accessed=20_000_000),
        name="pack_columns",
    )(starts, turned_starts, hbm(update))
    return outs[0], [outs[1 + n * GROUPS : 1 + (n + 1) * GROUPS] for n in range(len(others))]


def form_kernel(slot, count, group_ref, slot_ref, me_ref, *rest):
    pieces = rest[:count]
    xh_ref, xl_ref = rest[count : count + 2]
    out_ref, held, xh, xl, ph, plow, pick_sems, x_sems, in_sems, out_sems = rest[-10:]
    rows, width = held.shape[1:]
    per = CTILES // GROUPS
    sel = pl.multiple_of((me_ref[1] + slot) * TILE, TILE)

    def slab_of(k):
        return k if count == 1 else (me_ref[0] + GROUPS - k) % GROUPS

    def x_loads(k):
        band = pl.ds(pl.multiple_of(slab_of(k) * rows, rows), rows)
        return [
            pltpu.make_async_copy(src.at[band], dst.at[k], x_sems.at[n, k])
            for n, (src, dst) in enumerate(((xh_ref, xh), (xl_ref, xl)))
        ]

    picks = [
        pltpu.make_async_copy(src.at[pl.ds(sel, width)], dst, pick_sems.at[n])
        for n, (src, dst) in enumerate(((xh_ref, ph), (xl_ref, plow)))
    ]
    for copy in picks:
        copy.start()
    for k in range(GROUPS):
        for copy in x_loads(k):
            copy.start()
        src = pieces[0].at[k] if count == 1 else pieces[k]
        pltpu.make_async_copy(src, held.at[k], in_sems.at[k]).start()
    for copy in picks:
        copy.wait()
    rhs = jnp.concatenate([ph[...], plow[...], ph[...]], axis=1)

    def source(k, carry):
        for copy in x_loads(k):
            copy.wait()
        lhs = jnp.concatenate([xh[k], xh[k], xl[k]], axis=1)
        prod = lax.dot_general(lhs, rhs, (((1,), (1,)), ((), ())), preferred_element_type=F32)
        src = pieces[0].at[0] if count == 1 else pieces[0]
        pltpu.make_async_copy(src, held.at[k], in_sems.at[k]).wait()
        held[k] -= prod
        for q in range(per):
            tile = slab_of(k) * per + q
            src = held.at[k, pl.ds(q * TILE, TILE)]
            pltpu.make_async_copy(src, out_ref.at[group_ref[tile], slot_ref[tile]], out_sems.at[k, q]).start()
        return carry

    lax.fori_loop(0, GROUPS, source, 0)
    for k in range(GROUPS):
        for q in range(per):
            src = held.at[k, pl.ds(q * TILE, TILE)]
            pltpu.make_async_copy(src, out_ref.at[0, 0], out_sems.at[k, q]).wait()


def form(slot, groups, slots, me, pieces, xs, after):
    rows, width = pieces[0].shape[-2:]
    order = xs[0].shape[1]
    count = len(pieces)
    low = jnp.bfloat16
    return pl.pallas_call(
        lambda *refs: form_kernel(slot, count, *refs),
        out_shape=pltpu.HBM((GROUPS, SLOTS, TILE, width), F32),
        in_specs=[smem_spec()] * 3 + [any_spec()] * (count + 2 + len(after)),
        out_specs=any_spec(),
        scratch_shapes=[
            pltpu.VMEM((GROUPS, rows, width), F32),
            pltpu.VMEM((GROUPS, rows, order), low),
            pltpu.VMEM((GROUPS, rows, order), low),
            pltpu.VMEM((width, order), low),
            pltpu.VMEM((width, order), low),
            pltpu.SemaphoreType.DMA((2,)),
            pltpu.SemaphoreType.DMA((2, GROUPS)),
            pltpu.SemaphoreType.DMA((GROUPS,)),
            pltpu.SemaphoreType.DMA((GROUPS, CTILES // GROUPS)),
        ],
        compiler_params=pltpu.CompilerParams(vmem_limit_bytes=32 * 1024 * 1024),
        cost_estimate=pl.CostEstimate(flops=5_000_000_000, transcendentals=0, bytes_accessed=15_000_000),
        name="form",
    )(groups, slots, me, *pieces, *[hbm(x) for x in xs], *after)


def assemble_kernel(rows_ref, cols_ref, *rest):
    parts = rest[: len(CHUNKS)]
    out_ref, acc, sem = rest[len(CHUNKS) :]
    child = pl.program_id(0)

    @pl.when(child == 0)
    def _():
        acc[...] = jnp.zeros_like(acc)

    for s in range(SLOTS):
        row = rows_ref[child, s]
        at = pl.multiple_of(row * TILE, TILE)
        here = slice(s * TILE, (s + 1) * TILE)
        for c, (slot, width) in enumerate(CHUNKS):
            for w in range(width):
                col = cols_ref[child, slot + w]

                @pl.when(jnp.logical_and(row >= 0, col >= 0))
                def _():
                    acc[col, pl.ds(at, TILE), :] += parts[c][0, here, w * TILE : (w + 1) * TILE]

    @pl.when(child == pl.num_programs(0) - 1)
    def _():
        copies = [
            pltpu.make_async_copy(acc.at[b], out_ref.at[:, pl.ds(b * TILE, TILE)], sem.at[b]) for b in range(BLOCK)
        ]
        for copy in copies:
            copy.start()
        for copy in copies:
            copy.wait()


def assemble(rows, cols, parts):
    block = lambda n: pl.BlockSpec((1, WIN, n), lambda c: (c, 0, 0))
    return pl.pallas_call(
        assemble_kernel,
        grid=(GROUPS,),
        out_shape=jax.ShapeDtypeStruct((SIDE, SIDE), F32),
        in_specs=[smem_spec(), smem_spec()] + [block(w * TILE) for _, w in CHUNKS],
        out_specs=any_spec(),
        scratch_shapes=[pltpu.VMEM((BLOCK, SIDE, TILE), F32), pltpu.SemaphoreType.DMA((BLOCK,))],
        compiler_params=pltpu.CompilerParams(vmem_limit_bytes=40 * 1024 * 1024),
        cost_estimate=pl.CostEstimate(flops=0, transcendentals=0, bytes_accessed=40_000_000),
        name="assemble",
    )(rows, cols, *parts)


def local(pivot_block, panel_rows, update_block, tile_map):
    row_me = lax.axis_index("row")
    front_me = lax.axis_index("front")
    col_me = lax.axis_index("col")
    share, order = pivot_block.shape[1:]
    slab = panel_rows[0]

    panel_all = lax.all_gather(slab, "row", axis=0, tiled=True)
    pivot = jnp.broadcast_to(pivot_block[0], (GROUPS, share, order))
    pivot = lax.all_to_all(pivot, "row", split_axis=0, concat_axis=0, tiled=True).reshape(order, order)

    tile_ids = lax.dynamic_index_in_dim(tile_map, front_me * 2 + col_me, 0, keepdims=False)
    starts = window_starts(tile_ids)
    ahead = jnp.take(starts, (row_me + jnp.arange(GROUPS, dtype=jnp.int32)) % GROUPS)
    groups = tile_ids // BLOCK
    slots = jnp.arange(CTILES, dtype=jnp.int32) - jnp.take(starts, groups)
    me = jnp.stack([row_me, ahead[0]])

    ring = lambda k: [(i, (i + k) % GROUPS) for i in range(GROUPS)]
    first, others = pack_columns(starts, ahead, update_block[0])
    first = lax.all_to_all(first, "row", split_axis=0, concat_axis=0, tiled=True)
    arrived = [[first]]
    for sent in others:
        arrived.append([sent[0]] + [lax.ppermute(sent[k], "row", ring(k)) for k in range(1, GROUPS)])

    upper, inverse = factor(pivot, [others[0][0]])
    *xs, own_factor = solve(panel_all, slab, inverse, [first])

    parts = []
    for n, (slot, _) in enumerate(CHUNKS):
        after = arrived[n + 1][1:4] if n + 1 < len(CHUNKS) else []
        sent = form(slot, groups, slots, me, arrived[n], xs, after)
        sent = sent.reshape(GROUPS, WIN, sent.shape[3])
        parts.append(lax.all_to_all(sent, "front", split_axis=0, concat_axis=0, tiled=True))

    child_maps = jnp.take(tile_map, jnp.arange(GROUPS, dtype=jnp.int32) * 2 + col_me, axis=0)
    parent = assemble(slot_targets(child_maps, front_me), slot_targets(child_maps, row_me), parts)
    lower_rows = lax.dynamic_slice_in_dim(upper, row_me * share, share, 1).T
    return (lower_rows[None], own_factor[None], parent[None])


def solution(mesh):
    return jax.shard_map(
        local,
        mesh=mesh,
        in_specs=(
            P(("front", "col"), "row", None),
            P(("front", "col"), "row", None),
            P(("front", "col"), "row", None),
            P(),
        ),
        out_specs=(
            P(("front", "col"), "row", None),
            P(("front", "col"), "row", None),
            P("col", "front", "row"),
        ),
        check_vma=False,
    )
```

time: 738 us -> 391 us (0.53); the launches traced: 727 us -> 390 us
  other arithmetic: 143 us -> 1.55 us
  blocking collectives: 122 us -> 0 us
  Pallas kernels: 0 us -> 98.4 us
  matrix products: 92.9 us -> 0 us
  local copies, waits for them, and re-layouts: 82.6 us -> 18.8 us
  waiting for transfers between devices: 262 us -> 203 us
  starting transfers between devices: 7.46 us -> 53.4 us
    all_to_all x1 -> x0, blocking collectives: 122 us -> none  [local(): lax.all_to_all(source, 'row', split_axis=1, concat_axis=0, tiled=True)]
    another operation x17 -> x1, other arithmetic: 120 us -> 0.12 us  [local(): me = jnp.stack([row_me, ahead[0]])]
    pallas_call x0 -> x7, Pallas kernels: none -> 98.4 us  [the longest x1 38.9 us: factor(): pl.pallas_call(factor_kernel, out_shape=(whole, whole), in_specs=[vmem_sp...]
    dot_general x3 -> x0, matrix products: 87.9 us -> none  [the longest x1 37.8 us: local(): jnp.einsum('fas,fsxby->axby', row_hot, partial_value, precision=lax.Preci...]
    all_gather x2 -> x1, waiting for transfers between devices: 73.8 us -> 0.01 us  [local(): panel_all = lax.all_gather(slab, 'row', axis=0, tiled=True)]
    ppermute x0 -> x14, waiting for transfers between devices: none -> 72.8 us  [local(): lax.ppermute(sent[k], 'row', ring(k))]
    all_to_all x1 -> x5, waiting for transfers between devices: 188 us -> 130 us  [the longest x3 97.7 us: local(): lax.all_to_all(sent, 'front', split_axis=0, concat_axis=0, tiled=True)]
    all_to_all x1 -> x5, starting transfers between devices: 7.38 us -> 33.4 us  [the longest x3 22.9 us: local(): lax.all_to_all(sent, 'front', split_axis=0, concat_axis=0, tiled=True)]
  transfers between devices with their start and end apart: 3 -> 20, of which waited for: 3 -> 13; matrix products, arithmetic and copies ran while one was open for 1% -> 2% of each run, Pallas kernels for 0% -> 20%
where the time goes in v2:
time: 391 us; the launch traced here: 390 us
  waiting for transfers between devices  203 us (52%)
  Pallas kernels  98.4 us (25%)
  starting transfers between devices  53.4 us (14%)
  local copies, waits for them, and re-layouts  18.8 us (5%)
  between operations  14.2 us (4%)
    all_to_all x3, waiting for transfers between devices, local(): lax.all_to_all(sent, 'front', split_axis=0, concat_axis=0, tiled=True)  97.7 us
    ppermute x14, waiting for transfers between devices, local(): lax.ppermute(sent[k], 'row', ring(k))  72.8 us
    pallas_call x1, Pallas kernels, factor(): pl.pallas_call(factor_kernel, out_shape=(whole, whole), in_specs=[vmem_sp...  38.9 us
    all_to_all x1, waiting for transfers between devices, local(): lax.all_to_all(first, 'row', split_axis=0, concat_axis=0, tiled=True)  27.1 us
    pallas_call x3, Pallas kernels, form(): pl.pallas_call(lambda *refs: form_kernel(slot, count, *refs), out_shape=p...  24.8 us
    all_to_all x3, starting transfers between devices, local(): lax.all_to_all(sent, 'front', split_axis=0, concat_axis=0, tiled=True)  22.9 us
    ppermute x14, starting transfers between devices, local(): lax.ppermute(sent[k], 'row', ring(k))  20 us
    pallas_call x1, Pallas kernels, solve(): pl.pallas_call(solve_kernel, grid=(blocks,), out_shape=(pltpu.HBM(panel_a...  14.5 us
  transfers between devices with their start and end apart: 20, of which 13 were waited for; matrix products, arithmetic and copies ran while one was open for 2% of the time, Pallas kernels for 20%

profile of v2, /device:TPU:14, one launch (start us, length us, event | category | flops | bytes accessed | tf_op | source)
XLA Modules:
  0.0 389.7 jit_solution(1814323417782430170)
XLA Ops:
  9.9 4.9 %all-to-all-start = ((f32[8,64,512]{2,1,0:T(8,128)}), f32[8,64,512]{2,1,0:T(8,128)S(1)}, u32[]{:S(2)}, u32[]{:S(2)}) async-start(f32[8,64,512]{2,1,0:T(8,128)} %broadcast_in_dim.42), calls=%async_computation | async-start | bytes 2097152 | tf_op jit(solution)/shard_map/all_to_all | solution.py:349
  16.4 8.6 %pack_columns.1 = (f32[8,512,128]{2,1,0:T(8,128)}, f32[512,256]{1,0:T(8,128)}, f32[512,256]{1,0:T(8,128)}, f32[512,256]{1,0:T(8,128)}, f32[512,256]{1,0:T(8,128)...) custom-call(s32[8]{0:T(128)S(1)} %broadcast_minimum_fusion.2.starts_, ...), custom_call_target="tpu_custom_call" | custom-call | bytes 20000000 | tf_op jit(solution)/shard_map/pack_columns/pallas_call | solution.py:195
  28.2 5.1 %all-to-all-done = f32[8,64,512]{2,1,0:T(8,128)S(1)} async-done(((f32[8,64,512]{2,1,0:T(8,128)}), f32[8,64,512]{2,1,0:T(8,128)S(1)}, u32[]{:S(2)}, u32[]{:S(2)}) %all-to-all-start) | async-done | bytes 1048608 | tf_op jit(solution)/shard_map/all_to_all | solution.py:349
  33.3 5.6 %all-to-all-start.1 = ((f32[8,512,128]{2,1,0:T(8,128)}), f32[8,512,128]{2,1,0:T(8,128)S(1)}, u32[]{:S(2)}, u32[]{:S(2)}) async-start(f32[8,512,128]{2,1,0:T(8,128)} %get-tuple-element.29), calls=%async_computation.1 | async-start | bytes 4194304 | tf_op jit(solution)/shard_map/all_to_all | solution.py:360
  41.2 38.9 %factor.1 = (f32[512,512]{1,0:T(8,128)S(1)}, f32[512,512]{1,0:T(8,128)S(1)}) custom-call(f32[512,512]{1,0:T(8,128)S(1)} %bitcast.49, f32[512,256]{1,0:T(8,128)S(1)} %copy-done.3), custom_call_target="tpu_custom_call" | custom-call | flops 20000000000 | bytes 4000000 | tf_op jit(solution)/shard_map/factor/pallas_call | solution.py:107
  82.1 27.1 %all-to-all-done.1.refs_0_.refs_3_ = f32[8,512,128]{2,1,0:T(8,128)S(1)} async-done(((f32[8,512,128]{2,1,0:T(8,128)}), f32[8,512,128]{2,1,0:T(8,128)S(1)}, u32[]{:S(2)}, u32[]{:S(2)}) %all-to-all-start.1) | async-done | bytes 2097184 | tf_op jit(solution)/shard_map/all_to_all | solution.py:360
  110.3 14.5 %solve.1 = (bf16[4096,512]{1,0:T(8,128)(2,1)}, bf16[4096,512]{1,0:T(8,128)(2,1)}, f32[512,512]{1,0:T(8,128)}) custom-call(f32[4096,512]{1,0:T(8,128)} %bitcast.57, f32[512,512]{1,0:T(8,128)S(1)} %bitcast.48, f32[512,512]{1,0:T(8,128)S(1)} %copy-done.14, f32[8,512,128]{2,1,0:T(8,128)S(1)} %all-to-all-done.1.refs_0_.refs_3_), custom_call_target="tpu_custom_call" | custom-call | flops 8000000000 | bytes 20000000 | tf_op jit(solution)/shard_map/solve/pallas_call | solution.py:147
  124.9 7.8 %form.3 = f32[8,5,128,128]{3,2,1,0:T(8,128)} custom-call(s32[32]{0:T(128)S(1)} %get-tuple-element.60.refs_0_, s32[32]{0:T(128)S(1)} %get-tuple-element.59.refs_1_, s32[2]{0:T(128)S(1)} %pad_add_fusion.refs_2_, f32[8,512,128]{2,1,0:T(8,128)S(1)} %all-to-all-done.1.refs_0_.refs_3_, bf16[4096,512]{1,0:T(8,128)(2,1)} %get-tuple-element.31.refs_4_.refs_11_, ...), custom_call_target="tpu_custom_call" | custom-call | flops 5000000000 | bytes 15000000 | tf_op jit(solution)/shard_map/form/pallas_call | solution.py:271
  132.8 8.2 %all-to-all-start.2 = ((f32[8,640,128]{2,1,0:T(8,128)}), f32[8,640,128]{2,1,0:T(8,128)S(1)}, u32[]{:S(2)}, u32[]{:S(2)}) async-start(f32[8,640,128]{2,1,0:T(8,128)} %bitcast.55), calls=%async_computation.2 | async-start | bytes 5242880 | tf_op jit(solution)/shard_map/all_to_all | solution.py:373
  143.6 5.7 %collective-permute-start.5 = (f32[512,256]{1,0:T(8,128)}, f32[512,256]{1,0:T(8,128)S(1)}, u32[]{:S(2)}, u32[]{:S(2)}) collective-permute-start(f32[512,256]{1,0:T(8,128)} %get-tuple-element.38), channel_id=1, source_target_pairs={{0,12},{2,14},{4,0},{6,2},{8,4},{10,6},{12,8},{14,10},{1,13},{3,15... | collective-permute-start | bytes 1572872 | tf_op jit(solution)/shard_map/ppermute | solution.py:363
  149.7 7.9 %collective-permute-done.3.refs_7_ = f32[512,256]{1,0:T(8,128)S(1)} collective-permute-done((f32[512,256]{1,0:T(8,128)}, f32[512,256]{1,0:T(8,128)S(1)}, u32[]{:S(2)}, u32[]{:S(2)}) %collective-permute-start.3) | collective-permute-done | bytes 524320 | tf_op jit(solution)/shard_map/ppermute | solution.py:363
  157.8 14.0 %collective-permute-done.4.refs_8_ = f32[512,256]{1,0:T(8,128)S(1)} collective-permute-done((f32[512,256]{1,0:T(8,128)}, f32[512,256]{1,0:T(8,128)S(1)}, u32[]{:S(2)}, u32[]{:S(2)}) %collective-permute-start.4) | collective-permute-done | bytes 524320 | tf_op jit(solution)/shard_map/ppermute | solution.py:363
  171.8 5.0 %collective-permute-done.5.refs_9_ = f32[512,256]{1,0:T(8,128)S(1)} collective-permute-done((f32[512,256]{1,0:T(8,128)}, f32[512,256]{1,0:T(8,128)S(1)}, u32[]{:S(2)}, u32[]{:S(2)}) %collective-permute-start.5) | collective-permute-done | bytes 524320 | tf_op jit(solution)/shard_map/ppermute | solution.py:363
  176.8 10.2 %collective-permute-done.6.refs_10_ = f32[512,256]{1,0:T(8,128)S(1)} collective-permute-done((f32[512,256]{1,0:T(8,128)}, f32[512,256]{1,0:T(8,128)S(1)}, u32[]{:S(2)}, u32[]{:S(2)}) %collective-permute-start.6) | collective-permute-done | bytes 524320 | tf_op jit(solution)/shard_map/ppermute | solution.py:363
  188.8 8.5 %form.4 = f32[8,5,128,256]{3,2,1,0:T(8,128)} custom-call(s32[32]{0:T(128)S(1)} %get-tuple-element.60.refs_0_, s32[32]{0:T(128)S(1)} %get-tuple-element.59.refs_1_, s32[2]{0:T(128)S(1)} %pad_add_fusion.refs_2_, f32[512,256]{1,0:T(8,128)S(1)} %copy-done.4, f32[512,256]{1,0:T(8,128)} %collective-permute-done.refs_6_.refs_4_, ...), custom_call_target="tpu_custom_call" | custom-call | flops 5000000000 | bytes 15000000 | tf_op jit(solution)/shard_map/form/pallas_call | solution.py:271
  199.8 7.6 %all-to-all-start.3 = ((f32[8,640,256]{2,1,0:T(8,128)}), f32[8,640,256]{2,1,0:T(8,128)}, u32[]{:S(2)}, u32[]{:S(2)}) async-start(f32[8,640,256]{2,1,0:T(8,128)} %bitcast.51), calls=%async_computation.3 | async-start | bytes 10485760 | tf_op jit(solution)/shard_map/all_to_all | solution.py:373
  216.0 8.0 %collective-permute-done.10.refs_7_ = f32[512,256]{1,0:T(8,128)S(1)} collective-permute-done((f32[512,256]{1,0:T(8,128)}, f32[512,256]{1,0:T(8,128)S(1)}, u32[]{:S(2)}, u32[]{:S(2)}) %collective-permute-start.10) | collective-permute-done | bytes 524320 | tf_op jit(solution)/shard_map/ppermute | solution.py:363
  223.9 16.5 %collective-permute-done.11.refs_8_ = f32[512,256]{1,0:T(8,128)S(1)} collective-permute-done((f32[512,256]{1,0:T(8,128)}, f32[512,256]{1,0:T(8,128)S(1)}, u32[]{:S(2)}, u32[]{:S(2)}) %collective-permute-start.11) | collective-permute-done | bytes 524320 | tf_op jit(solution)/shard_map/ppermute | solution.py:363
  244.3 5.6 %collective-permute-done.13.refs_10_ = f32[512,256]{1,0:T(8,128)S(1)} collective-permute-done((f32[512,256]{1,0:T(8,128)}, f32[512,256]{1,0:T(8,128)S(1)}, u32[]{:S(2)}, u32[]{:S(2)}) %collective-permute-start.13) | collective-permute-done | bytes 524320 | tf_op jit(solution)/shard_map/ppermute | solution.py:363
  253.0 8.5 %form.5 = f32[8,5,128,256]{3,2,1,0:T(8,128)} custom-call(s32[32]{0:T(128)S(1)} %get-tuple-element.60.refs_0_, s32[32]{0:T(128)S(1)} %get-tuple-element.59.refs_1_, s32[2]{0:T(128)S(1)} %pad_add_fusion.refs_2_, f32[512,256]{1,0:T(8,128)S(1)} %copy-done.12, f32[512,256]{1,0:T(8,128)S(1)} %copy-done.6, f32[512,256]{1,0:T(8,128)S(1)} %copy-done.8, ...), custom_call_target="tpu_custom_call" | custom-call | flops 5000000000 | bytes 15000000 | tf_op jit(solution)/shard_map/form/pallas_call | solution.py:271
  261.5 25.4 %all-to-all-done.3.rest_1_ = f32[8,640,256]{2,1,0:T(8,128)} async-done(((f32[8,640,256]{2,1,0:T(8,128)}), f32[8,640,256]{2,1,0:T(8,128)}, u32[]{:S(2)}, u32[]{:S(2)}) %all-to-all-start.3) | async-done | bytes 5242912 | tf_op jit(solution)/shard_map/all_to_all | solution.py:373
  286.9 7.0 %all-to-all-start.4 = ((f32[8,640,256]{2,1,0:T(8,128)}), f32[8,640,256]{2,1,0:T(8,128)}, u32[]{:S(2)}, u32[]{:S(2)}) async-start(f32[8,640,256]{2,1,0:T(8,128)} %bitcast.54), calls=%async_computation.4 | async-start | bytes 10485760 | tf_op jit(solution)/shard_map/all_to_all | solution.py:373
  299.0 72.3 %all-to-all-done.4.rest_2_ = f32[8,640,256]{2,1,0:T(8,128)} async-done(((f32[8,640,256]{2,1,0:T(8,128)}), f32[8,640,256]{2,1,0:T(8,128)}, u32[]{:S(2)}, u32[]{:S(2)}) %all-to-all-start.4) | async-done | bytes 5242912 | tf_op jit(solution)/shard_map/all_to_all | solution.py:373
  371.3 11.5 %assemble.1 = f32[1536,1536]{1,0:T(8,128)} custom-call(s32[8,5]{1,0:T(8,128)S(1)} %subtract_select_fusion.1.rows_ref, s32[8,5]{1,0:T(8,128)S(1)} %subtract_select_fusion.cols_ref, f32[8,640,128]{2,1,0:T(8,128)S(1)} %all-to-all-done.2.rest_0_, f32[8,640,256]{2,1,0:T(8,128)} %all-to-all-done.3.rest_1_, f32[8,640,256]{2,1,0:T(8,128)} %all-to-all-done.4.rest_2_), custom_call_target="tpu_custom_call" | custom-call | bytes 40000000 | tf_op jit(solution)/shard_map/assemble/pallas_call | solution.py:327
  (87 shorter events, 40.9 us)
Async XLA Ops:
  7.2 102.0 %all-gather.3.cloned.1.call-start = ((), (), s32[]{:S(2)}) async-start(), calls=%async_computation.5 | async-start | bytes 9437184 | tf_op jit(solution)/shard_map/all_gather | solution.py:347
  9.9 23.4 %all-to-all-start = ((f32[8,64,512]{2,1,0:T(8,128)}), f32[8,64,512]{2,1,0:T(8,128)S(1)}, u32[]{:S(2)}, u32[]{:S(2)}) async-start(f32[8,64,512]{2,1,0:T(8,128)} %broadcast_in_dim.42), calls=%async_computation | async-start | bytes 2097152 | tf_op jit(solution)/shard_map/all_to_all | solution.py:349
  25.0 99.9 %collective-permute-start = (f32[512,256]{1,0:T(8,128)}, f32[512,256]{1,0:T(8,128)}, u32[]{:S(2)}, u32[]{:S(2)}) collective-permute-start(f32[512,256]{1,0:T(8,128)} %get-tuple-element.33), channel_id=1, source_target_pairs={{0,2},{2,4},{4,6},{6,8},{8,10},{10,12},{12,14},{14,0},{1,3},{3,5},... | collective-permute-start | bytes 1572872 | tf_op jit(solution)/shard_map/ppermute | solution.py:363
  25.2 99.7 %collective-permute-start.1 = (f32[512,256]{1,0:T(8,128)}, f32[512,256]{1,0:T(8,128)}, u32[]{:S(2)}, u32[]{:S(2)}) collective-permute-start(f32[512,256]{1,0:T(8,128)} %get-tuple-element.34), channel_id=1, source_target_pairs={{0,4},{2,6},{4,8},{6,10},{8,12},{10,14},{12,0},{14,2},{1,5},{3,7},... | collective-permute-start | bytes 1572872 | tf_op jit(solution)/shard_map/ppermute | solution.py:363
  26.6 98.3 %collective-permute-start.2 = (f32[512,256]{1,0:T(8,128)}, f32[512,256]{1,0:T(8,128)}, u32[]{:S(2)}, u32[]{:S(2)}) collective-permute-start(f32[512,256]{1,0:T(8,128)} %get-tuple-element.35), channel_id=1, source_target_pairs={{0,6},{2,8},{4,10},{6,12},{8,14},{10,0},{12,2},{14,4},{1,7},{3,9},... | collective-permute-start | bytes 1572872 | tf_op jit(solution)/shard_map/ppermute | solution.py:363
  33.3 75.8 %all-to-all-start.1 = ((f32[8,512,128]{2,1,0:T(8,128)}), f32[8,512,128]{2,1,0:T(8,128)S(1)}, u32[]{:S(2)}, u32[]{:S(2)}) async-start(f32[8,512,128]{2,1,0:T(8,128)} %get-tuple-element.29), calls=%async_computation.1 | async-start | bytes 4194304 | tf_op jit(solution)/shard_map/all_to_all | solution.py:360
  41.2 67.9 %copy-start = (f32[1,512,512]{2,1,0:T(8,128)S(1)}, f32[1,512,512]{2,1,0:T(8,128)}, u32[]{:S(2)}) copy-start(f32[1,512,512]{2,1,0:T(8,128)} %param.7) | copy-start | bytes 3145732
  132.7 56.1 %copy-start.4 = (f32[512,256]{1,0:T(8,128)S(1)}, f32[512,256]{1,0:T(8,128)}, u32[]{:S(2)}) copy-start(f32[512,256]{1,0:T(8,128)} %get-tuple-element.26.refs_0_.refs_3_) | copy-start | bytes 1572868
  132.8 67.0 %all-to-all-start.2 = ((f32[8,640,128]{2,1,0:T(8,128)}), f32[8,640,128]{2,1,0:T(8,128)S(1)}, u32[]{:S(2)}, u32[]{:S(2)}) async-start(f32[8,640,128]{2,1,0:T(8,128)} %bitcast.55), calls=%async_computation.2 | async-start | bytes 5242880 | tf_op jit(solution)/shard_map/all_to_all | solution.py:373
  141.0 16.6 %collective-permute-start.3 = (f32[512,256]{1,0:T(8,128)}, f32[512,256]{1,0:T(8,128)S(1)}, u32[]{:S(2)}, u32[]{:S(2)}) collective-permute-start(f32[512,256]{1,0:T(8,128)} %get-tuple-element.36), channel_id=1, source_target_pairs={{0,8},{2,10},{4,12},{6,14},{8,0},{10,2},{12,4},{14,6},{1,9},{3,11}... | collective-permute-start | bytes 1572872 | tf_op jit(solution)/shard_map/ppermute | solution.py:363
  143.5 28.3 %collective-permute-start.4 = (f32[512,256]{1,0:T(8,128)}, f32[512,256]{1,0:T(8,128)S(1)}, u32[]{:S(2)}, u32[]{:S(2)}) collective-permute-start(f32[512,256]{1,0:T(8,128)} %get-tuple-element.37), channel_id=1, source_target_pairs={{0,10},{2,12},{4,14},{6,0},{8,2},{10,4},{12,6},{14,8},{1,11},{3,13... | collective-permute-start | bytes 1572872 | tf_op jit(solution)/shard_map/ppermute | solution.py:363
  143.6 33.3 %collective-permute-start.5 = (f32[512,256]{1,0:T(8,128)}, f32[512,256]{1,0:T(8,128)S(1)}, u32[]{:S(2)}, u32[]{:S(2)}) collective-permute-start(f32[512,256]{1,0:T(8,128)} %get-tuple-element.38), channel_id=1, source_target_pairs={{0,12},{2,14},{4,0},{6,2},{8,4},{10,6},{12,8},{14,10},{1,13},{3,15... | collective-permute-start | bytes 1572872 | tf_op jit(solution)/shard_map/ppermute | solution.py:363
  149.2 37.9 %collective-permute-start.6 = (f32[512,256]{1,0:T(8,128)}, f32[512,256]{1,0:T(8,128)S(1)}, u32[]{:S(2)}, u32[]{:S(2)}) collective-permute-start(f32[512,256]{1,0:T(8,128)} %get-tuple-element.39), channel_id=1, source_target_pairs={{0,14},{2,0},{4,2},{6,4},{8,6},{10,8},{12,10},{14,12},{1,15},{3,1}... | collective-permute-start | bytes 1572872 | tf_op jit(solution)/shard_map/ppermute | solution.py:363
  149.2 37.9 %collective-permute-start.7 = (f32[512,256]{1,0:T(8,128)}, f32[512,256]{1,0:T(8,128)S(1)}, u32[]{:S(2)}, u32[]{:S(2)}) collective-permute-start(f32[512,256]{1,0:T(8,128)} %get-tuple-element.40), channel_id=1, source_target_pairs={{0,2},{2,4},{4,6},{6,8},{8,10},{10,12},{12,14},{14,0},{1,3},{3,5},... | collective-permute-start | bytes 1572872 | tf_op jit(solution)/shard_map/ppermute | solution.py:363
  157.6 29.5 %collective-permute-start.8 = (f32[512,256]{1,0:T(8,128)}, f32[512,256]{1,0:T(8,128)S(1)}, u32[]{:S(2)}, u32[]{:S(2)}) collective-permute-start(f32[512,256]{1,0:T(8,128)} %get-tuple-element.41), channel_id=1, source_target_pairs={{0,4},{2,6},{4,8},{6,10},{8,12},{10,14},{12,0},{14,2},{1,5},{3,7},... | collective-permute-start | bytes 1572872 | tf_op jit(solution)/shard_map/ppermute | solution.py:363
  171.8 17.0 %collective-permute-start.9 = (f32[512,256]{1,0:T(8,128)}, f32[512,256]{1,0:T(8,128)S(1)}, u32[]{:S(2)}, u32[]{:S(2)}) collective-permute-start(f32[512,256]{1,0:T(8,128)} %get-tuple-element.42), channel_id=1, source_target_pairs={{0,6},{2,8},{4,10},{6,12},{8,14},{10,0},{12,2},{14,4},{1,7},{3,9},... | collective-permute-start | bytes 1572872 | tf_op jit(solution)/shard_map/ppermute | solution.py:363
  199.8 50.1 %copy-start.6 = (f32[512,256]{1,0:T(8,128)S(1)}, f32[512,256]{1,0:T(8,128)}, u32[]{:S(2)}) copy-start(f32[512,256]{1,0:T(8,128)} %copy-done.5) | copy-start | bytes 1572868
  199.8 87.1 %all-to-all-start.3 = ((f32[8,640,256]{2,1,0:T(8,128)}), f32[8,640,256]{2,1,0:T(8,128)}, u32[]{:S(2)}, u32[]{:S(2)}) async-start(f32[8,640,256]{2,1,0:T(8,128)} %bitcast.51), calls=%async_computation.3 | async-start | bytes 10485760 | tf_op jit(solution)/shard_map/all_to_all | solution.py:373
  207.4 16.6 %collective-permute-start.10 = (f32[512,256]{1,0:T(8,128)}, f32[512,256]{1,0:T(8,128)S(1)}, u32[]{:S(2)}, u32[]{:S(2)}) collective-permute-start(f32[512,256]{1,0:T(8,128)} %get-tuple-element.44), channel_id=1, source_target_pairs={{0,8},{2,10},{4,12},{6,14},{8,0},{10,2},{12,4},{14,6},{1,9},{3,11}... | collective-permute-start | bytes 1572872 | tf_op jit(solution)/shard_map/ppermute | solution.py:363
  209.3 31.2 %collective-permute-start.11 = (f32[512,256]{1,0:T(8,128)}, f32[512,256]{1,0:T(8,128)S(1)}, u32[]{:S(2)}, u32[]{:S(2)}) collective-permute-start(f32[512,256]{1,0:T(8,128)} %get-tuple-element.45), channel_id=1, source_target_pairs={{0,10},{2,12},{4,14},{6,0},{8,2},{10,4},{12,6},{14,8},{1,11},{3,13... | collective-permute-start | bytes 1572872 | tf_op jit(solution)/shard_map/ppermute | solution.py:363
  211.0 33.2 %collective-permute-start.12 = (f32[512,256]{1,0:T(8,128)}, f32[512,256]{1,0:T(8,128)S(1)}, u32[]{:S(2)}, u32[]{:S(2)}) collective-permute-start(f32[512,256]{1,0:T(8,128)} %get-tuple-element.46), channel_id=1, source_target_pairs={{0,12},{2,14},{4,0},{6,2},{8,4},{10,6},{12,8},{14,10},{1,13},{3,15... | collective-permute-start | bytes 1572872 | tf_op jit(solution)/shard_map/ppermute | solution.py:363
  213.3 36.5 %collective-permute-start.13 = (f32[512,256]{1,0:T(8,128)}, f32[512,256]{1,0:T(8,128)S(1)}, u32[]{:S(2)}, u32[]{:S(2)}) collective-permute-start(f32[512,256]{1,0:T(8,128)} %get-tuple-element.47), channel_id=1, source_target_pairs={{0,14},{2,0},{4,2},{6,4},{8,6},{10,8},{12,10},{14,12},{1,15},{3,1}... | collective-permute-start | bytes 1572872 | tf_op jit(solution)/shard_map/ppermute | solution.py:363
  286.9 7.1 %copy-start.15 = (s32[16,32]{1,0:T(8,128)S(1)}, s32[16,32]{1,0:T(8,128)}, u32[]{:S(2)}) copy-start(s32[16,32]{1,0:T(8,128)} %param.9) | copy-start | bytes 6148
  286.9 84.5 %all-to-all-start.4 = ((f32[8,640,256]{2,1,0:T(8,128)}), f32[8,640,256]{2,1,0:T(8,128)}, u32[]{:S(2)}, u32[]{:S(2)}) async-start(f32[8,640,256]{2,1,0:T(8,128)} %bitcast.54), calls=%async_computation.4 | async-start | bytes 10485760 | tf_op jit(solution)/shard_map/all_to_all | solution.py:373
  (12 other events, 16.6 us)
Sparse Core Ops, SparseCore 0:
  9.7 96.1 all-gather.2

commit v3 on v2

--- a/solution.py
+++ b/solution.py
@@ -12,7 +12,9 @@
 CTILES = 32
 WIN = SLOTS * TILE
 SIDE = BLOCK * TILE
-CHUNKS = ((0, 1), (1, 2), (3, 2))
+CHUNKS = ((0, 1), (1, 1), (2, 1), (3, 1), (4, 1))
+AHEAD = (3, 3, 3, 3)
+ORDER = (4, 2, 6, 1, 7, 3, 5)
 HI = lax.Precision.HIGHEST
 F32 = jnp.float32
 
@@ -121,44 +123,45 @@
     return high, (x - high.astype(F32)).astype(jnp.bfloat16)
 
 
-def solve_kernel(all_ref, own_ref, v_ref, *refs):
-    high_ref, low_ref, out_ref, rhs = refs[-4:]
+def solve_kernel(all_ref, v_ref, *refs):
+    high_ref, low_ref, *rhs = refs[-4:]
     order = v_ref.shape[0]
+    step = order // len(rhs)
 
     @pl.when(pl.program_id(0) == 0)
     def _():
-        vh, vl = split(v_ref[...])
-        rhs[0:order] = vh
-        rhs[order : 2 * order] = vl
-        rhs[2 * order :] = vh
-        out_ref[...] = jnp.dot(own_ref[...], v_ref[...], precision=HI, preferred_element_type=F32)
+        for n, held in enumerate(rhs):
+            depth = (n + 1) * step
+            vh, vl = split(v_ref[0:depth, n * step : depth])
+            held[0:depth] = vh
+            held[depth : 2 * depth] = vl
+            held[2 * depth :] = vh
 
     bh, bl = split(all_ref[...])
-    lhs = jnp.concatenate([bh, bh, bl], axis=1)
-    x = jnp.dot(lhs, rhs[...], preferred_element_type=F32)
-    high_ref[...], low_ref[...] = split(x)
-
-
-def solve(panel_all, slab, inverse, after):
-    rows, order = slab.shape
-    blocks = panel_all.shape[0] // rows
-    whole = lambda shape: pl.BlockSpec(shape, lambda i: (0, 0))
+    for n, held in enumerate(rhs):
+        depth = (n + 1) * step
+        lhs = jnp.concatenate([bh[:, 0:depth], bh[:, 0:depth], bl[:, 0:depth]], axis=1)
+        x = jnp.dot(lhs, held[...], preferred_element_type=F32)
+        here = slice(n * step, depth)
+        high_ref[:, here], low_ref[:, here] = split(x)
+
+
+def solve(panel_all, inverse, after):
+    order = inverse.shape[0]
+    rows = 1024
+    half = order // 2
     block = pl.BlockSpec((rows, order), lambda i: (i, 0))
     return pl.pallas_call(
         solve_kernel,
-        grid=(blocks,),
-        out_shape=(
-            pltpu.HBM(panel_all.shape, jnp.bfloat16),
-            pltpu.HBM(panel_all.shape, jnp.bfloat16),
-            jax.ShapeDtypeStruct(slab.shape, F32),
-        ),
-        in_specs=[block, whole(slab.shape), whole(inverse.shape)] + [any_spec()] * len(after),
-        out_specs=(block, block, whole(slab.shape)),
-        scratch_shapes=[pltpu.VMEM((3 * order, order), jnp.bfloat16)],
-        compiler_params=pltpu.CompilerParams(vmem_limit_bytes=32 * 1024 * 1024),
+        grid=(panel_all.shape[0] // rows,),
+        out_shape=(pltpu.HBM(panel_all.shape, jnp.bfloat16),) * 2,
+        in_specs=[block, pl.BlockSpec(inverse.shape, lambda i: (0, 0))] + [any_spec()] * len(after),
+        out_specs=(block, block),
+        scratch_shapes=[pltpu.VMEM((3 * half, half), jnp.bfloat16), pltpu.VMEM((3 * order, half), jnp.bfloat16)],
+        compiler_params=pltpu.CompilerParams(vmem_limit_bytes=40 * 1024 * 1024),
         cost_estimate=pl.CostEstimate(flops=8_000_000_000, transcendentals=0, bytes_accessed=20_000_000),
         name="solve",
-    )(hbm(panel_all), slab, inverse, *after)
+    )(hbm(panel_all), inverse, *after)
 
 
 def pack_columns_kernel(starts_ref, turned_ref, u_ref, first_ref, *rest):
@@ -263,7 +266,7 @@
             pltpu.make_async_copy(src, out_ref.at[0, 0], out_sems.at[k, q]).wait()
 
 
-def form(slot, groups, slots, me, pieces, xs, after):
+def form(slot, groups, slots, me, pieces, xs):
     rows, width = pieces[0].shape[-2:]
     order = xs[0].shape[1]
     count = len(pieces)
@@ -271,7 +274,7 @@
     return pl.pallas_call(
         lambda *refs: form_kernel(slot, count, *refs),
         out_shape=pltpu.HBM((GROUPS, SLOTS, TILE, width), F32),
-        in_specs=[smem_spec()] * 3 + [any_spec()] * (count + 2 + len(after)),
+        in_specs=[smem_spec()] * 3 + [any_spec()] * (count + 2),
         out_specs=any_spec(),
         scratch_shapes=[
             pltpu.VMEM((GROUPS, rows, width), F32),
@@ -287,7 +290,7 @@
         compiler_params=pltpu.CompilerParams(vmem_limit_bytes=32 * 1024 * 1024),
         cost_estimate=pl.CostEstimate(flops=5_000_000_000, transcendentals=0, bytes_accessed=15_000_000),
         name="form",
-    )(groups, slots, me, *pieces, *[hbm(x) for x in xs], *after)
+    )(groups, slots, me, *pieces, *[hbm(x) for x in xs])
 
 
 def assemble_kernel(rows_ref, cols_ref, *rest):
@@ -357,20 +360,28 @@
 
     ring = lambda k: [(i, (i + k) % GROUPS) for i in range(GROUPS)]
     first, others = pack_columns(starts, ahead, update_block[0])
+    upper, inverse = factor(pivot, [others[0][0]])
     first = lax.all_to_all(first, "row", split_axis=0, concat_axis=0, tiled=True)
+    xs = solve(panel_all, inverse, [first])
+
+    *others[0], first = lax.optimization_barrier((*others[0], first))
     arrived = [[first]]
     for sent in others:
-        arrived.append([sent[0]] + [lax.ppermute(sent[k], "row", ring(k)) for k in range(1, GROUPS)])
-
-    upper, inverse = factor(pivot, [others[0][0]])
-    *xs, own_factor = solve(panel_all, slab, inverse, [first])
+        pieces = [sent[0]] + [None] * (GROUPS - 1)
+        for k in ORDER:
+            pieces[k] = lax.ppermute(sent[k], "row", ring(k))
+        arrived.append(pieces)
 
     parts = []
     for n, (slot, _) in enumerate(CHUNKS):
-        after = arrived[n + 1][1:4] if n + 1 < len(CHUNKS) else []
-        sent = form(slot, groups, slots, me, arrived[n], xs, after)
+        sent = form(slot, groups, slots, me, arrived[n], xs)
+        if n == 0:
+            late, _ = lax.optimization_barrier((slab, sent))
         sent = sent.reshape(GROUPS, WIN, sent.shape[3])
+        if n + 1 < len(CHUNKS):
+            sent, *_ = lax.optimization_barrier((sent, *[arrived[n + 1][k] for k in ORDER[: AHEAD[n]]]))
         parts.append(lax.all_to_all(sent, "front", split_axis=0, concat_axis=0, tiled=True))
+    own_factor = jnp.dot(late, inverse, precision=HI)
 
     child_maps = jnp.take(tile_map, jnp.arange(GROUPS, dtype=jnp.int32) * 2 + col_me, axis=0)
     parent = assemble(slot_targets(child_maps, front_me), slot_targets(child_maps, row_me), parts)

time: 391 us -> 338 us (0.86); the launches traced: 390 us -> 332 us
  waiting for transfers between devices: 203 us -> 93.2 us
  starting transfers between devices: 53.4 us -> 91.3 us
  Pallas kernels: 98.4 us -> 109 us
  matrix products: 0 us -> 4.35 us
    all_to_all x3 -> x5, waiting for transfers between devices: 97.7 us -> 39 us  [local(): lax.all_to_all(sent, 'front', split_axis=0, concat_axis=0, tiled=True)]
    ppermute x14 -> x28, waiting for transfers between devices: 72.8 us -> 40.6 us  [local(): pieces[k] = lax.ppermute(sent[k], 'row', ring(k))]
    ppermute x14 -> x28, starting transfers between devices: 20 us -> 44.5 us  [local(): pieces[k] = lax.ppermute(sent[k], 'row', ring(k))]
    all_to_all x1, waiting for transfers between devices: 27.1 us -> 5.93 us  [local(): lax.all_to_all(first, 'row', split_axis=0, concat_axis=0, tiled=True)]
    pallas_call x3 -> x5, Pallas kernels: 24.8 us -> 39.5 us  [form(): pl.pallas_call(lambda *refs: form_kernel(slot, count, *refs), out_shape=p...]
    all_to_all x3 -> x5, starting transfers between devices: 22.9 us -> 36.3 us  [local(): lax.all_to_all(sent, 'front', split_axis=0, concat_axis=0, tiled=True)]
    pallas_call x1, Pallas kernels: 14.5 us -> 9.9 us  [solve(): pl.pallas_call(solve_kernel, grid=(panel_all.shape[0] // rows,), out_shap...]
    dot_general x0 -> x1, matrix products: none -> 4.35 us  [local(): own_factor = jnp.dot(late, inverse, precision=HI)]
  transfers between devices with their start and end apart: 20 -> 36, of which waited for: 13 -> 16; matrix products, arithmetic and copies ran while one was open for 2% -> 4% of each run, Pallas kernels for 20% -> 29%
where the time goes in v3:
time: 338 us; the launch traced here: 332 us
  Pallas kernels  109 us (32%)
  waiting for transfers between devices  93.2 us (28%)
  starting transfers between devices  91.3 us (27%)
  local copies, waits for them, and re-layouts  19 us (6%)
  between operations  14.4 us (4%)
  matrix products  4.35 us (1%)
    ppermute x28, starting transfers between devices, local(): pieces[k] = lax.ppermute(sent[k], 'row', ring(k))  44.5 us
    ppermute x28, waiting for transfers between devices, local(): pieces[k] = lax.ppermute(sent[k], 'row', ring(k))  40.6 us
    pallas_call x5, Pallas kernels, form(): pl.pallas_call(lambda *refs: form_kernel(slot, count, *refs), out_shape=p...  39.5 us
    all_to_all x5, waiting for transfers between devices, local(): lax.all_to_all(sent, 'front', split_axis=0, concat_axis=0, tiled=True)  39 us
    pallas_call x1, Pallas kernels, factor(): pl.pallas_call(factor_kernel, out_shape=(whole, whole), in_specs=[vmem_sp...  38.9 us
    all_to_all x5, starting transfers between devices, local(): lax.all_to_all(sent, 'front', split_axis=0, concat_axis=0, tiled=True)  36.3 us
    unnamed x45, local copies, waits for them, and re-layouts  12 us
    pallas_call x1, Pallas kernels, assemble(): pl.pallas_call(assemble_kernel, grid=(GROUPS,), out_shape=jax.ShapeDtypeS...  11.4 us
  transfers between devices with their start and end apart: 36, of which 16 were waited for; matrix products, arithmetic and copies ran while one was open for 4% of the time, Pallas kernels for 29%

profile of v3, /device:TPU:14, one launch (start us, length us, event | category | flops | bytes accessed | tf_op | source)
XLA Modules:
  0.0 332.2 jit_solution(18207210890469537083)
XLA Ops:
  16.4 9.3 %pack_columns.1 = (f32[8,512,128]{2,1,0:T(8,128)}, f32[512,128]{1,0:T(8,128)}, f32[512,128]{1,0:T(8,128)}, f32[512,128]{1,0:T(8,128)}, f32[512,128]{1,0:T(8,128)...) custom-call(s32[8]{0:T(128)S(1)} %broadcast_minimum_fusion.2.starts_, ...), custom_call_target="tpu_custom_call" | custom-call | bytes 20000000 | tf_op jit(solution)/shard_map/pack_columns/pallas_call | solution.py:198
  25.8 7.1 %all-to-all-done = f32[8,64,512]{2,1,0:T(8,128)S(1)} async-done(((f32[8,64,512]{2,1,0:T(8,128)}), f32[8,64,512]{2,1,0:T(8,128)S(1)}, u32[]{:S(2)}, u32[]{:S(2)}) %all-to-all-start) | async-done | bytes 1048608 | tf_op jit(solution)/shard_map/all_to_all | solution.py:352
  32.9 5.6 %all-to-all-start.1 = ((f32[8,512,128]{2,1,0:T(8,128)}), f32[8,512,128]{2,1,0:T(8,128)S(1)}, u32[]{:S(2)}, u32[]{:S(2)}) async-start(f32[8,512,128]{2,1,0:T(8,128)} %get-tuple-element.64), calls=%async_computation.1 | async-start | bytes 4194304 | tf_op jit(solution)/shard_map/all_to_all | solution.py:364
  39.7 38.9 %factor.1 = (f32[512,512]{1,0:T(8,128)S(1)}, f32[512,512]{1,0:T(8,128)S(1)}) custom-call(f32[512,512]{1,0:T(8,128)S(1)} %bitcast.53, f32[512,128]{1,0:T(8,128)S(1)} %copy-done.7), custom_call_target="tpu_custom_call" | custom-call | flops 20000000000 | bytes 4000000 | tf_op jit(solution)/shard_map/factor/pallas_call | solution.py:109
  79.6 5.9 %all-to-all-done.1.refs_0_.refs_3_ = f32[8,512,128]{2,1,0:T(8,128)S(1)} async-done(((f32[8,512,128]{2,1,0:T(8,128)}), f32[8,512,128]{2,1,0:T(8,128)S(1)}, u32[]{:S(2)}, u32[]{:S(2)}) %all-to-all-start.1) | async-done | bytes 2097184 | tf_op jit(solution)/shard_map/all_to_all | solution.py:364
  89.0 9.9 %solve.1 = (bf16[4096,512]{1,0:T(8,128)(2,1)}, bf16[4096,512]{1,0:T(8,128)(2,1)}) custom-call(f32[4096,512]{1,0:T(8,128)} %bitcast.64, f32[512,512]{1,0:T(8,128)S(1)} %get-tuple-element.66.v_ref, f32[8,512,128]{2,1,0:T(8,128)S(1)} %all-to-all-done.1.refs_0_.refs_3_), custom_call_target="tpu_custom_call" | custom-call | flops 8000000000 | bytes 20000000 | tf_op jit(solution)/shard_map/solve/pallas_call | solution.py:154
  98.9 7.8 %form.5 = f32[8,5,128,128]{3,2,1,0:T(8,128)} custom-call(s32[32]{0:T(128)S(1)} %get-tuple-element.119.refs_0_, s32[32]{0:T(128)S(1)} %get-tuple-element.118.refs_1_, s32[2]{0:T(128)S(1)} %pad_add_fusion.refs_2_, f32[8,512,128]{2,1,0:T(8,128)S(1)} %all-to-all-done.1.refs_0_.refs_3_, bf16[4096,512]{1,0:T(8,128)(2,1)} %get-tuple-element.67.refs_4_.refs_11_, ...), custom_call_target="tpu_custom_call" | custom-call | flops 5000000000 | bytes 15000000 | tf_op jit(solution)/shard_map/form/pallas_call | solution.py:274
  106.8 8.2 %all-to-all-start.2 = ((f32[8,640,128]{2,1,0:T(8,128)}), f32[8,640,128]{2,1,0:T(8,128)S(1)}, u32[]{:S(2)}, u32[]{:S(2)}) async-start(f32[8,640,128]{2,1,0:T(8,128)} %bitcast.61), calls=%async_computation.2 | async-start | bytes 5242880 | tf_op jit(solution)/shard_map/all_to_all | solution.py:383
  124.3 9.2 %collective-permute-done.4.refs_6_ = f32[512,128]{1,0:T(8,128)S(1)} collective-permute-done((f32[512,128]{1,0:T(8,128)S(1)}, f32[512,128]{1,0:T(8,128)S(1)}, u32[]{:S(2)}, u32[]{:S(2)}) %collective-permute-start.4) | collective-permute-done | bytes 262176 | tf_op jit(solution)/shard_map/ppermute | solution.py:372
  133.5 7.9 %form.6 = f32[8,5,128,128]{3,2,1,0:T(8,128)} custom-call(s32[32]{0:T(128)S(1)} %get-tuple-element.119.refs_0_, s32[32]{0:T(128)S(1)} %get-tuple-element.118.refs_1_, s32[2]{0:T(128)S(1)} %pad_add_fusion.refs_2_, f32[512,128]{1,0:T(8,128)S(1)} %copy-done.7, f32[512,128]{1,0:T(8,128)S(1)} %collective-permute-done.3.refs_4_, ...), custom_call_target="tpu_custom_call" | custom-call | flops 5000000000 | bytes 15000000 | tf_op jit(solution)/shard_map/form/pallas_call | solution.py:274
  147.7 6.9 %all-to-all-start.3 = ((f32[8,640,128]{2,1,0:T(8,128)}), f32[8,640,128]{2,1,0:T(8,128)}, u32[]{:S(2)}, u32[]{:S(2)}) async-start(f32[8,640,128]{2,1,0:T(8,128)} %bitcast.58), calls=%async_computation.3 | async-start | bytes 5242880 | tf_op jit(solution)/shard_map/all_to_all | solution.py:383
  163.7 9.5 %collective-permute-done.11.refs_6_ = f32[512,128]{1,0:T(8,128)S(1)} collective-permute-done((f32[512,128]{1,0:T(8,128)}, f32[512,128]{1,0:T(8,128)S(1)}, u32[]{:S(2)}, u32[]{:S(2)}) %collective-permute-start.11) | collective-permute-done | bytes 262176 | tf_op jit(solution)/shard_map/ppermute | solution.py:372
  175.1 8.0 %form.7 = f32[8,5,128,128]{3,2,1,0:T(8,128)} custom-call(s32[32]{0:T(128)S(1)} %get-tuple-element.119.refs_0_, s32[32]{0:T(128)S(1)} %get-tuple-element.118.refs_1_, s32[2]{0:T(128)S(1)} %pad_add_fusion.refs_2_, f32[512,128]{1,0:T(8,128)S(1)} %copy-done.6, f32[512,128]{1,0:T(8,128)S(1)} %collective-permute-done.10.refs_4_, f32[512,128]{1,0:T(8,128)S(1)} %copy-done.9, ...), custom_call_target="tpu_custom_call" | custom-call | flops 5000000000 | bytes 15000000 | tf_op jit(solution)/shard_map/form/pallas_call | solution.py:274
  185.1 6.9 %all-to-all-start.4 = ((f32[8,640,128]{2,1,0:T(8,128)}), f32[8,640,128]{2,1,0:T(8,128)}, u32[]{:S(2)}, u32[]{:S(2)}) async-start(f32[8,640,128]{2,1,0:T(8,128)} %bitcast.59), calls=%async_computation.4 | async-start | bytes 5242880 | tf_op jit(solution)/shard_map/all_to_all | solution.py:383
  204.4 6.3 %collective-permute-done.18.refs_6_ = f32[512,128]{1,0:T(8,128)S(1)} collective-permute-done((f32[512,128]{1,0:T(8,128)}, f32[512,128]{1,0:T(8,128)S(1)}, u32[]{:S(2)}, u32[]{:S(2)}) %collective-permute-start.18) | collective-permute-done | bytes 262176 | tf_op jit(solution)/shard_map/ppermute | solution.py:372
  217.0 7.9 %form.8 = f32[8,5,128,128]{3,2,1,0:T(8,128)} custom-call(s32[32]{0:T(128)S(1)} %get-tuple-element.119.refs_0_, s32[32]{0:T(128)S(1)} %get-tuple-element.118.refs_1_, s32[2]{0:T(128)S(1)} %pad_add_fusion.refs_2_, f32[512,128]{1,0:T(8,128)S(1)} %copy-done.5, f32[512,128]{1,0:T(8,128)S(1)} %collective-permute-done.17.refs_4_, f32[512,128]{1,0:T(8,128)S(1)} %copy-done.11, ...), custom_call_target="tpu_custom_call" | custom-call | flops 5000000000 | bytes 15000000 | tf_op jit(solution)/shard_map/form/pallas_call | solution.py:274
  226.4 7.3 %all-to-all-start.5 = ((f32[8,640,128]{2,1,0:T(8,128)}), f32[8,640,128]{2,1,0:T(8,128)}, u32[]{:S(2)}, u32[]{:S(2)}) async-start(f32[8,640,128]{2,1,0:T(8,128)} %bitcast.62), calls=%async_computation.5 | async-start | bytes 5242880 | tf_op jit(solution)/shard_map/all_to_all | solution.py:383
  233.7 6.1 %collective-permute-start.25 = (f32[512,128]{1,0:T(8,128)}, f32[512,128]{1,0:T(8,128)S(1)}, u32[]{:S(2)}, u32[]{:S(2)}) collective-permute-start(f32[512,128]{1,0:T(8,128)} %get-tuple-element.103), channel_id=1, source_target_pairs={{0,6},{2,8},{4,10},{6,12},{8,14},{10,0},{12,2},{14,4},{1,7},{3,9},... | collective-permute-start | bytes 786440 | tf_op jit(solution)/shard_map/ppermute | solution.py:372
  249.3 5.3 %collective-permute-done.26.refs_8_ = f32[512,128]{1,0:T(8,128)S(1)} collective-permute-done((f32[512,128]{1,0:T(8,128)}, f32[512,128]{1,0:T(8,128)S(1)}, u32[]{:S(2)}, u32[]{:S(2)}) %collective-permute-start.26) | collective-permute-done | bytes 262176 | tf_op jit(solution)/shard_map/ppermute | solution.py:372
  255.5 7.9 %form.9 = f32[8,5,128,128]{3,2,1,0:T(8,128)} custom-call(s32[32]{0:T(128)S(1)} %get-tuple-element.119.refs_0_, s32[32]{0:T(128)S(1)} %get-tuple-element.118.refs_1_, s32[2]{0:T(128)S(1)} %pad_add_fusion.refs_2_, f32[512,128]{1,0:T(8,128)S(1)} %copy-done.4, f32[512,128]{1,0:T(8,128)S(1)} %collective-permute-done.24.refs_4_, f32[512,128]{1,0:T(8,128)S(1)} %copy-done.13, ...), custom_call_target="tpu_custom_call" | custom-call | flops 5000000000 | bytes 15000000 | tf_op jit(solution)/shard_map/form/pallas_call | solution.py:274
  263.4 9.5 %all-to-all-done.5.rest_3_ = f32[8,640,128]{2,1,0:T(8,128)} async-done(((f32[8,640,128]{2,1,0:T(8,128)}), f32[8,640,128]{2,1,0:T(8,128)}, u32[]{:S(2)}, u32[]{:S(2)}) %all-to-all-start.5) | async-done | bytes 2621472 | tf_op jit(solution)/shard_map/all_to_all | solution.py:383
  272.9 6.9 %all-to-all-start.6 = ((f32[8,640,128]{2,1,0:T(8,128)}), f32[8,640,128]{2,1,0:T(8,128)}, u32[]{:S(2)}, u32[]{:S(2)}) async-start(f32[8,640,128]{2,1,0:T(8,128)} %bitcast.60), calls=%async_computation.6 | async-start | bytes 5242880 | tf_op jit(solution)/shard_map/all_to_all | solution.py:383
  289.2 24.7 %all-to-all-done.6.rest_4_ = f32[8,640,128]{2,1,0:T(8,128)} async-done(((f32[8,640,128]{2,1,0:T(8,128)}), f32[8,640,128]{2,1,0:T(8,128)}, u32[]{:S(2)}, u32[]{:S(2)}) %all-to-all-start.6) | async-done | bytes 2621472 | tf_op jit(solution)/shard_map/all_to_all | solution.py:383
  313.9 11.4 %assemble.1 = f32[1536,1536]{1,0:T(8,128)} custom-call(s32[8,5]{1,0:T(8,128)S(1)} %subtract_select_fusion.1.rows_ref, s32[8,5]{1,0:T(8,128)S(1)} %subtract_select_fusion.cols_ref, f32[8,640,128]{2,1,0:T(8,128)S(1)} %all-to-all-done.2.rest_0_, f32[8,640,128]{2,1,0:T(8,128)} %all-to-all-done.3.rest_1_, f32[8,640,128]{2,1,0:T(8,128)} %all-to-all-done.4.rest_2_, ...), custom_call_target="tpu_custom_call" | custom-call | bytes 40000000 | tf_op jit(solution)/shard_map/assemble/pallas_call | solution.py:330
  (134 shorter events, 83.3 us)
Async XLA Ops:
  7.2 81.8 %all-gather.3.cloned.1.call-start = ((), (), s32[]{:S(2)}) async-start(), calls=%async_computation.7 | async-start | bytes 9437184 | tf_op jit(solution)/shard_map/all_gather | solution.py:350
  9.9 22.9 %all-to-all-start = ((f32[8,64,512]{2,1,0:T(8,128)}), f32[8,64,512]{2,1,0:T(8,128)S(1)}, u32[]{:S(2)}, u32[]{:S(2)}) async-start(f32[8,64,512]{2,1,0:T(8,128)} %broadcast_in_dim.42), calls=%async_computation | async-start | bytes 2097152 | tf_op jit(solution)/shard_map/all_to_all | solution.py:352
  32.9 52.7 %all-to-all-start.1 = ((f32[8,512,128]{2,1,0:T(8,128)}), f32[8,512,128]{2,1,0:T(8,128)S(1)}, u32[]{:S(2)}, u32[]{:S(2)}) async-start(f32[8,512,128]{2,1,0:T(8,128)} %get-tuple-element.64), calls=%async_computation.1 | async-start | bytes 4194304 | tf_op jit(solution)/shard_map/all_to_all | solution.py:364
  85.5 21.2 %collective-permute-start = (f32[512,128]{1,0:T(8,128)}, f32[512,128]{1,0:T(8,128)}, u32[]{:S(2)}, u32[]{:S(2)}) collective-permute-start(f32[512,128]{1,0:T(8,128)} %get-tuple-element.70), channel_id=1, source_target_pairs={{0,8},{2,10},{4,12},{6,14},{8,0},{10,2},{12,4},{14,6},{1,9},{3,11}... | collective-permute-start | bytes 786440 | tf_op jit(solution)/shard_map/ppermute | solution.py:372
  87.0 19.8 %collective-permute-start.1 = (f32[512,128]{1,0:T(8,128)}, f32[512,128]{1,0:T(8,128)}, u32[]{:S(2)}, u32[]{:S(2)}) collective-permute-start(f32[512,128]{1,0:T(8,128)} %get-tuple-element.71), channel_id=1, source_target_pairs={{0,4},{2,6},{4,8},{6,10},{8,12},{10,14},{12,0},{14,2},{1,5},{3,7},... | collective-permute-start | bytes 786440 | tf_op jit(solution)/shard_map/ppermute | solution.py:372
  88.4 18.3 %collective-permute-start.2 = (f32[512,128]{1,0:T(8,128)}, f32[512,128]{1,0:T(8,128)}, u32[]{:S(2)}, u32[]{:S(2)}) collective-permute-start(f32[512,128]{1,0:T(8,128)} %get-tuple-element.72), channel_id=1, source_target_pairs={{0,12},{2,14},{4,0},{6,2},{8,4},{10,6},{12,8},{14,10},{1,13},{3,15... | collective-permute-start | bytes 786440 | tf_op jit(solution)/shard_map/ppermute | solution.py:372
  106.8 40.9 %all-to-all-start.2 = ((f32[8,640,128]{2,1,0:T(8,128)}), f32[8,640,128]{2,1,0:T(8,128)S(1)}, u32[]{:S(2)}, u32[]{:S(2)}) async-start(f32[8,640,128]{2,1,0:T(8,128)} %bitcast.61), calls=%async_computation.2 | async-start | bytes 5242880 | tf_op jit(solution)/shard_map/all_to_all | solution.py:383
  115.0 18.5 %collective-permute-start.4 = (f32[512,128]{1,0:T(8,128)S(1)}, f32[512,128]{1,0:T(8,128)S(1)}, u32[]{:S(2)}, u32[]{:S(2)}) collective-permute-start(f32[512,128]{1,0:T(8,128)S(1)} %copy-done.21), channel_id=1, source_target_pairs={{0,6},{2,8},{4,10},{6,12},{8,14},{10,0},{12,2},{14,4},{1,7},{3,9},... | collective-permute-start | bytes 786440 | tf_op jit(solution)/shard_map/ppermute | solution.py:372
  117.4 16.2 %collective-permute-start.5 = (f32[512,128]{1,0:T(8,128)}, f32[512,128]{1,0:T(8,128)S(1)}, u32[]{:S(2)}, u32[]{:S(2)}) collective-permute-start(f32[512,128]{1,0:T(8,128)} %get-tuple-element.77), channel_id=1, source_target_pairs={{0,10},{2,12},{4,14},{6,0},{8,2},{10,4},{12,6},{14,8},{1,11},{3,13... | collective-permute-start | bytes 786440 | tf_op jit(solution)/shard_map/ppermute | solution.py:372
  119.7 21.7 %collective-permute-start.7 = (f32[512,128]{1,0:T(8,128)}, f32[512,128]{1,0:T(8,128)S(1)}, u32[]{:S(2)}, u32[]{:S(2)}) collective-permute-start(f32[512,128]{1,0:T(8,128)} %get-tuple-element.79), channel_id=1, source_target_pairs={{0,8},{2,10},{4,12},{6,14},{8,0},{10,2},{12,4},{14,6},{1,9},{3,11}... | collective-permute-start | bytes 786440 | tf_op jit(solution)/shard_map/ppermute | solution.py:372
  122.2 19.2 %collective-permute-start.8 = (f32[512,128]{1,0:T(8,128)}, f32[512,128]{1,0:T(8,128)S(1)}, u32[]{:S(2)}, u32[]{:S(2)}) collective-permute-start(f32[512,128]{1,0:T(8,128)} %get-tuple-element.80), channel_id=1, source_target_pairs={{0,4},{2,6},{4,8},{6,10},{8,12},{10,14},{12,0},{14,2},{1,5},{3,7},... | collective-permute-start | bytes 786440 | tf_op jit(solution)/shard_map/ppermute | solution.py:372
  147.7 37.4 %all-to-all-start.3 = ((f32[8,640,128]{2,1,0:T(8,128)}), f32[8,640,128]{2,1,0:T(8,128)}, u32[]{:S(2)}, u32[]{:S(2)}) async-start(f32[8,640,128]{2,1,0:T(8,128)} %bitcast.58), calls=%async_computation.3 | async-start | bytes 5242880 | tf_op jit(solution)/shard_map/all_to_all | solution.py:383
  154.6 18.6 %collective-permute-start.11 = (f32[512,128]{1,0:T(8,128)}, f32[512,128]{1,0:T(8,128)S(1)}, u32[]{:S(2)}, u32[]{:S(2)}) collective-permute-start(f32[512,128]{1,0:T(8,128)} %get-tuple-element.85), channel_id=1, source_target_pairs={{0,6},{2,8},{4,10},{6,12},{8,14},{10,0},{12,2},{14,4},{1,7},{3,9},... | collective-permute-start | bytes 786440 | tf_op jit(solution)/shard_map/ppermute | solution.py:372
  156.9 16.3 %collective-permute-start.12 = (f32[512,128]{1,0:T(8,128)}, f32[512,128]{1,0:T(8,128)S(1)}, u32[]{:S(2)}, u32[]{:S(2)}) collective-permute-start(f32[512,128]{1,0:T(8,128)} %get-tuple-element.86), channel_id=1, source_target_pairs={{0,10},{2,12},{4,14},{6,0},{8,2},{10,4},{12,6},{14,8},{1,11},{3,13... | collective-permute-start | bytes 786440 | tf_op jit(solution)/shard_map/ppermute | solution.py:372
  159.3 23.9 %collective-permute-start.14 = (f32[512,128]{1,0:T(8,128)}, f32[512,128]{1,0:T(8,128)S(1)}, u32[]{:S(2)}, u32[]{:S(2)}) collective-permute-start(f32[512,128]{1,0:T(8,128)} %get-tuple-element.88), channel_id=1, source_target_pairs={{0,8},{2,10},{4,12},{6,14},{8,0},{10,2},{12,4},{14,6},{1,9},{3,11}... | collective-permute-start | bytes 786440 | tf_op jit(solution)/shard_map/ppermute | solution.py:372
  161.6 21.6 %collective-permute-start.15 = (f32[512,128]{1,0:T(8,128)}, f32[512,128]{1,0:T(8,128)S(1)}, u32[]{:S(2)}, u32[]{:S(2)}) collective-permute-start(f32[512,128]{1,0:T(8,128)} %get-tuple-element.89), channel_id=1, source_target_pairs={{0,4},{2,6},{4,8},{6,10},{8,12},{10,14},{12,0},{14,2},{1,5},{3,7},... | collective-permute-start | bytes 786440 | tf_op jit(solution)/shard_map/ppermute | solution.py:372
  185.1 41.3 %all-to-all-start.4 = ((f32[8,640,128]{2,1,0:T(8,128)}), f32[8,640,128]{2,1,0:T(8,128)}, u32[]{:S(2)}, u32[]{:S(2)}) async-start(f32[8,640,128]{2,1,0:T(8,128)} %bitcast.59), calls=%async_computation.4 | async-start | bytes 5242880 | tf_op jit(solution)/shard_map/all_to_all | solution.py:383
  194.7 16.0 %collective-permute-start.18 = (f32[512,128]{1,0:T(8,128)}, f32[512,128]{1,0:T(8,128)S(1)}, u32[]{:S(2)}, u32[]{:S(2)}) collective-permute-start(f32[512,128]{1,0:T(8,128)} %get-tuple-element.94), channel_id=1, source_target_pairs={{0,6},{2,8},{4,10},{6,12},{8,14},{10,0},{12,2},{14,4},{1,7},{3,9},... | collective-permute-start | bytes 786440 | tf_op jit(solution)/shard_map/ppermute | solution.py:372
  194.7 20.4 %collective-permute-start.19 = (f32[512,128]{1,0:T(8,128)}, f32[512,128]{1,0:T(8,128)S(1)}, u32[]{:S(2)}, u32[]{:S(2)}) collective-permute-start(f32[512,128]{1,0:T(8,128)} %get-tuple-element.95), channel_id=1, source_target_pairs={{0,10},{2,12},{4,14},{6,0},{8,2},{10,4},{12,6},{14,8},{1,11},{3,13... | collective-permute-start | bytes 786440 | tf_op jit(solution)/shard_map/ppermute | solution.py:372
  197.9 17.2 %collective-permute-start.20 = (f32[512,128]{1,0:T(8,128)}, f32[512,128]{1,0:T(8,128)S(1)}, u32[]{:S(2)}, u32[]{:S(2)}) collective-permute-start(f32[512,128]{1,0:T(8,128)} %get-tuple-element.96), channel_id=1, source_target_pairs={{0,14},{2,0},{4,2},{6,4},{8,6},{10,8},{12,10},{14,12},{1,15},{3,1}... | collective-permute-start | bytes 786440 | tf_op jit(solution)/shard_map/ppermute | solution.py:372
  197.9 27.0 %collective-permute-start.21 = (f32[512,128]{1,0:T(8,128)}, f32[512,128]{1,0:T(8,128)S(1)}, u32[]{:S(2)}, u32[]{:S(2)}) collective-permute-start(f32[512,128]{1,0:T(8,128)} %get-tuple-element.97), channel_id=1, source_target_pairs={{0,8},{2,10},{4,12},{6,14},{8,0},{10,2},{12,4},{14,6},{1,9},{3,11}... | collective-permute-start | bytes 786440 | tf_op jit(solution)/shard_map/ppermute | solution.py:372
  199.6 25.3 %collective-permute-start.22 = (f32[512,128]{1,0:T(8,128)}, f32[512,128]{1,0:T(8,128)S(1)}, u32[]{:S(2)}, u32[]{:S(2)}) collective-permute-start(f32[512,128]{1,0:T(8,128)} %get-tuple-element.98), channel_id=1, source_target_pairs={{0,4},{2,6},{4,8},{6,10},{8,12},{10,14},{12,0},{14,2},{1,5},{3,7},... | collective-permute-start | bytes 786440 | tf_op jit(solution)/shard_map/ppermute | solution.py:372
  226.4 46.5 %all-to-all-start.5 = ((f32[8,640,128]{2,1,0:T(8,128)}), f32[8,640,128]{2,1,0:T(8,128)}, u32[]{:S(2)}, u32[]{:S(2)}) async-start(f32[8,640,128]{2,1,0:T(8,128)} %bitcast.62), calls=%async_computation.5 | async-start | bytes 5242880 | tf_op jit(solution)/shard_map/all_to_all | solution.py:383
  272.9 41.0 %all-to-all-start.6 = ((f32[8,640,128]{2,1,0:T(8,128)}), f32[8,640,128]{2,1,0:T(8,128)}, u32[]{:S(2)}, u32[]{:S(2)}) async-start(f32[8,640,128]{2,1,0:T(8,128)} %bitcast.60), calls=%async_computation.6 | async-start | bytes 5242880 | tf_op jit(solution)/shard_map/all_to_all | solution.py:383
  (34 other events, 321.3 us)
Sparse Core Ops, SparseCore 0:
  9.7 75.5 all-gather.2

commit v4 on v3

--- a/solution.py
+++ b/solution.py
@@ -133,15 +133,15 @@
         for n, held in enumerate(rhs):
             depth = (n + 1) * step
             vh, vl = split(v_ref[0:depth, n * step : depth])
-            held[0:depth] = vh
-            held[depth : 2 * depth] = vl
-            held[2 * depth :] = vh
+            held[0] = vh
+            held[1] = vl
 
     bh, bl = split(all_ref[...])
     for n, held in enumerate(rhs):
         depth = (n + 1) * step
-        lhs = jnp.concatenate([bh[:, 0:depth], bh[:, 0:depth], bl[:, 0:depth]], axis=1)
-        x = jnp.dot(lhs, held[...], preferred_element_type=F32)
+        x = jnp.dot(bh[:, 0:depth], held[0], preferred_element_type=F32)
+        x = x + jnp.dot(bh[:, 0:depth], held[1], preferred_element_type=F32)
+        x = x + jnp.dot(bl[:, 0:depth], held[0], preferred_element_type=F32)
         here = slice(n * step, depth)
         high_ref[:, here], low_ref[:, here] = split(x)
 
@@ -157,7 +157,7 @@
         out_shape=(pltpu.HBM(panel_all.shape, jnp.bfloat16),) * 2,
         in_specs=[block, pl.BlockSpec(inverse.shape, lambda i: (0, 0))] + [any_spec()] * len(after),
         out_specs=(block, block),
-        scratch_shapes=[pltpu.VMEM((3 * half, half), jnp.bfloat16), pltpu.VMEM((3 * order, half), jnp.bfloat16)],
+        scratch_shapes=[pltpu.VMEM((2, half, half), jnp.bfloat16), pltpu.VMEM((2, order, half), jnp.bfloat16)],
         compiler_params=pltpu.CompilerParams(vmem_limit_bytes=40 * 1024 * 1024),
         cost_estimate=pl.CostEstimate(flops=8_000_000_000, transcendentals=0, bytes_accessed=20_000_000),
         name="solve",
@@ -243,13 +243,15 @@
         pltpu.make_async_copy(src, held.at[k], in_sems.at[k]).start()
     for copy in picks:
         copy.wait()
-    rhs = jnp.concatenate([ph[...], plow[...], ph[...]], axis=1)
+    rhs = jnp.concatenate([ph[...], plow[...]], axis=0)
+    dims = (((1,), (1,)), ((), ()))
 
     def source(k, carry):
         for copy in x_loads(k):
             copy.wait()
-        lhs = jnp.concatenate([xh[k], xh[k], xl[k]], axis=1)
-        prod = lax.dot_general(lhs, rhs, (((1,), (1,)), ((), ())), preferred_element_type=F32)
+        both = lax.dot_general(xh[k], rhs, dims, preferred_element_type=F32)
+        prod = lax.dot_general(xl[k], ph[...], dims, preferred_element_type=F32)
+        prod = both[:, 0:width] + both[:, width:] + prod
         src = pieces[0].at[0] if count == 1 else pieces[0]
         pltpu.make_async_copy(src, held.at[k], in_sems.at[k]).wait()
         held[k] -= prod
@@ -293,51 +295,101 @@
     )(groups, slots, me, *pieces, *[hbm(x) for x in xs])
 
 
-def assemble_kernel(rows_ref, cols_ref, *rest):
-    parts = rest[: len(CHUNKS)]
-    out_ref, acc, sem = rest[len(CHUNKS) :]
-    child = pl.program_id(0)
-
-    @pl.when(child == 0)
-    def _():
-        acc[...] = jnp.zeros_like(acc)
-
+def add_tiles(rows_ref, cols_ref, child, parts, slots, acc):
     for s in range(SLOTS):
         row = rows_ref[child, s]
         at = pl.multiple_of(row * TILE, TILE)
         here = slice(s * TILE, (s + 1) * TILE)
-        for c, (slot, width) in enumerate(CHUNKS):
-            for w in range(width):
-                col = cols_ref[child, slot + w]
-
-                @pl.when(jnp.logical_and(row >= 0, col >= 0))
-                def _():
-                    acc[col, pl.ds(at, TILE), :] += parts[c][0, here, w * TILE : (w + 1) * TILE]
-
-    @pl.when(child == pl.num_programs(0) - 1)
+        for part, slot in zip(parts, slots):
+            col = cols_ref[child, slot]
+
+            @pl.when(jnp.logical_and(row >= 0, col >= 0))
+            def _():
+                acc[col, pl.ds(at, TILE), :] += part[0, here, :]
+
+
+def collect_kernel(rows_ref, cols_ref, *rest):
+    parts, acc = rest[:-1], rest[-1]
+    child = pl.program_id(0)
+
+    @pl.when(child == 0)
     def _():
-        copies = [
-            pltpu.make_async_copy(acc.at[b], out_ref.at[:, pl.ds(b * TILE, TILE)], sem.at[b]) for b in range(BLOCK)
-        ]
-        for copy in copies:
-            copy.start()
-        for copy in copies:
-            copy.wait()
-
-
-def assemble(rows, cols, parts):
-    block = lambda n: pl.BlockSpec((1, WIN, n), lambda c: (c, 0, 0))
+        acc[...] = jnp.zeros_like(acc)
+
+    add_tiles(rows_ref, cols_ref, child, parts, range(len(parts)), acc)
+
+
+def collect(rows, cols, parts):
+    block = pl.BlockSpec((1, WIN, TILE), lambda c: (c, 0, 0))
+    shape = (BLOCK, SIDE, TILE)
     return pl.pallas_call(
-        assemble_kernel,
+        collect_kernel,
         grid=(GROUPS,),
+        out_shape=jax.ShapeDtypeStruct(shape, F32),
+        in_specs=[smem_spec(), smem_spec()] + [block for _ in parts],
+        out_specs=vmem_spec(),
+        compiler_params=pltpu.CompilerParams(vmem_limit_bytes=24 * 1024 * 1024),
+        cost_estimate=pl.CostEstimate(flops=0, transcendentals=0, bytes_accessed=20_000_000),
+        name="collect",
+    )(rows, cols, *parts)
+
+
+def finish_kernel(rows_ref, cols_ref, part_ref, acc_ref, out_ref, part, acc, part_sem, in_sems, out_sems):
+    def load(b):
+        return pltpu.make_async_copy(acc_ref.at[b], acc.at[b], in_sems.at[b])
+
+    def store(b):
+        at = pl.multiple_of(b * TILE, TILE)
+        return pltpu.make_async_copy(acc.at[b], out_ref.at[:, pl.ds(at, TILE)], out_sems.at[b])
+
+    whole = pltpu.make_async_copy(part_ref, part, part_sem.at[0])
+    whole.start()
+    for b in range(BLOCK):
+        load(b).start()
+    whole.wait()
+
+    def column(b, carry):
+        load(b).wait()
+
+        def add(child, inner):
+            @pl.when(cols_ref[child, SLOTS - 1] == b)
+            def _():
+                for s in range(SLOTS):
+                    row = rows_ref[child, s]
+
+                    @pl.when(row >= 0)
+                    def _():
+                        at = pl.ds(pl.multiple_of(row * TILE, TILE), TILE)
+                        acc[b, at, :] += part[child, s * TILE : (s + 1) * TILE, :]
+
+            return inner
+
+        lax.fori_loop(0, GROUPS, add, 0)
+        store(b).start()
+        return carry
+
+    lax.fori_loop(0, BLOCK, column, 0)
+    for b in range(BLOCK):
+        store(b).wait()
+
+
+def finish(rows, cols, part, acc):
+    return pl.pallas_call(
+        finish_kernel,
         out_shape=jax.ShapeDtypeStruct((SIDE, SIDE), F32),
-        in_specs=[smem_spec(), smem_spec()] + [block(w * TILE) for _, w in CHUNKS],
+        in_specs=[smem_spec(), smem_spec(), any_spec(), any_spec()],
         out_specs=any_spec(),
-        scratch_shapes=[pltpu.VMEM((BLOCK, SIDE, TILE), F32), pltpu.SemaphoreType.DMA((BLOCK,))],
-        compiler_params=pltpu.CompilerParams(vmem_limit_bytes=40 * 1024 * 1024),
-        cost_estimate=pl.CostEstimate(flops=0, transcendentals=0, bytes_accessed=40_000_000),
-        name="assemble",
-    )(rows, cols, *parts)
+        scratch_shapes=[
+            pltpu.VMEM(part.shape, F32),
+            pltpu.VMEM(acc.shape, F32),
+            pltpu.SemaphoreType.DMA((1,)),
+            pltpu.SemaphoreType.DMA((BLOCK,)),
+            pltpu.SemaphoreType.DMA((BLOCK,)),
+        ],
+        compiler_params=pltpu.CompilerParams(vmem_limit_bytes=24 * 1024 * 1024),
+        cost_estimate=pl.CostEstimate(flops=0, transcendentals=0, bytes_accessed=20_000_000),
+        name="finish",
+    )(rows, cols, part, hbm(acc))
 
 
 def local(pivot_block, panel_rows, update_block, tile_map):
@@ -384,7 +436,8 @@
     own_factor = jnp.dot(late, inverse, precision=HI)
 
     child_maps = jnp.take(tile_map, jnp.arange(GROUPS, dtype=jnp.int32) * 2 + col_me, axis=0)
-    parent = assemble(slot_targets(child_maps, front_me), slot_targets(child_maps, row_me), parts)
+    rows, cols = slot_targets(child_maps, front_me), slot_targets(child_maps, row_me)
+    parent = finish(rows, cols, parts[-1], collect(rows, cols, parts[:-1]))
     lower_rows = lax.dynamic_slice_in_dim(upper, row_me * share, share, 1).T
     return (lower_rows[None], own_factor[None], parent[None])
 

time: 338 us -> 333 us (0.985); the launches traced: 332 us -> 332 us
  waiting for transfers between devices: 93.2 us -> 88.6 us
  local copies, waits for them, and re-layouts: 19 us -> 22.7 us
    ppermute x28, waiting for transfers between devices: 40.6 us -> 33.2 us  [local(): pieces[k] = lax.ppermute(sent[k], 'row', ring(k))]
    pallas_call x5, Pallas kernels: 39.5 us -> 35.2 us  [form(): pl.pallas_call(lambda *refs: form_kernel(slot, count, *refs), out_shape=p...]
    pallas_call x1 -> x2, Pallas kernels: 11.4 us -> 15.7 us  [the longest x1 8.81 us: finish(): pl.pallas_call(finish_kernel, out_shape=jax.ShapeDtypeStruct((SIDE, SIDE)...]
    unnamed x45 -> x47, local copies, waits for them, and re-layouts: 12 us -> 15.7 us
  transfers between devices with their start and end apart: 36 -> 36, of which waited for: 16 -> 20; matrix products, arithmetic and copies ran while one was open for 4% -> 4% of each run, Pallas kernels for 29% -> 30%
where the time goes in v4:
time: 333 us; the launch traced here: 332 us
  Pallas kernels  109 us (33%)
  starting transfers between devices  92.6 us (28%)
  waiting for transfers between devices  88.6 us (27%)
  local copies, waits for them, and re-layouts  22.7 us (7%)
  between operations  14.4 us (4%)
  matrix products  4.35 us (1%)
    ppermute x28, starting transfers between devices, local(): pieces[k] = lax.ppermute(sent[k], 'row', ring(k))  45.7 us
    all_to_all x5, waiting for transfers between devices, local(): lax.all_to_all(sent, 'front', split_axis=0, concat_axis=0, tiled=True)  41.7 us
    pallas_call x1, Pallas kernels, factor(): pl.pallas_call(factor_kernel, out_shape=(whole, whole), in_specs=[vmem_sp...  38.9 us
    all_to_all x5, starting transfers between devices, local(): lax.all_to_all(sent, 'front', split_axis=0, concat_axis=0, tiled=True)  36.3 us
    pallas_call x5, Pallas kernels, form(): pl.pallas_call(lambda *refs: form_kernel(slot, count, *refs), out_shape=p...  35.2 us
    ppermute x28, waiting for transfers between devices, local(): pieces[k] = lax.ppermute(sent[k], 'row', ring(k))  33.2 us
    unnamed x47, local copies, waits for them, and re-layouts  15.7 us
    pallas_call x1, Pallas kernels, solve(): pl.pallas_call(solve_kernel, grid=(panel_all.shape[0] // rows,), out_shap...  9.91 us
  transfers between devices with their start and end apart: 36, of which 20 were waited for; matrix products, arithmetic and copies ran while one was open for 4% of the time, Pallas kernels for 30%

profile of v4, /device:TPU:14, one launch (start us, length us, event | category | flops | bytes accessed | tf_op | source)
XLA Modules:
  0.0 332.4 jit_solution(14647668457327607026)
XLA Ops:
  16.4 9.3 %pack_columns.1 = (f32[8,512,128]{2,1,0:T(8,128)}, f32[512,128]{1,0:T(8,128)}, f32[512,128]{1,0:T(8,128)}, f32[512,128]{1,0:T(8,128)}, f32[512,128]{1,0:T(8,128)...) custom-call(s32[8]{0:T(128)S(1)} %broadcast_minimum_fusion.2.starts_, ...), custom_call_target="tpu_custom_call" | custom-call | bytes 20000000 | tf_op jit(solution)/shard_map/pack_columns/pallas_call | solution.py:198
  25.8 7.1 %all-to-all-done = f32[8,64,512]{2,1,0:T(8,128)S(1)} async-done(((f32[8,64,512]{2,1,0:T(8,128)}), f32[8,64,512]{2,1,0:T(8,128)S(1)}, u32[]{:S(2)}, u32[]{:S(2)}) %all-to-all-start) | async-done | bytes 1048608 | tf_op jit(solution)/shard_map/all_to_all | solution.py:404
  39.7 38.9 %factor.1 = (f32[512,512]{1,0:T(8,128)S(1)}, f32[512,512]{1,0:T(8,128)S(1)}) custom-call(f32[512,512]{1,0:T(8,128)S(1)} %bitcast.53, f32[512,128]{1,0:T(8,128)S(1)} %copy-done.8), custom_call_target="tpu_custom_call" | custom-call | flops 20000000000 | bytes 4000000 | tf_op jit(solution)/shard_map/factor/pallas_call | solution.py:109
  79.6 5.9 %all-to-all-done.1.refs_0_.refs_3_ = f32[8,512,128]{2,1,0:T(8,128)S(1)} async-done(((f32[8,512,128]{2,1,0:T(8,128)}), f32[8,512,128]{2,1,0:T(8,128)S(1)}, u32[]{:S(2)}, u32[]{:S(2)}) %all-to-all-start.1) | async-done | bytes 2097184 | tf_op jit(solution)/shard_map/all_to_all | solution.py:416
  89.0 9.9 %solve.1 = (bf16[4096,512]{1,0:T(8,128)(2,1)}, bf16[4096,512]{1,0:T(8,128)(2,1)}) custom-call(f32[4096,512]{1,0:T(8,128)} %bitcast.64, f32[512,512]{1,0:T(8,128)S(1)} %get-tuple-element.66.v_ref, f32[8,512,128]{2,1,0:T(8,128)S(1)} %all-to-all-done.1.refs_0_.refs_3_), custom_call_target="tpu_custom_call" | custom-call | flops 8000000000 | bytes 20000000 | tf_op jit(solution)/shard_map/solve/pallas_call | solution.py:154
  98.9 7.0 %form.5 = f32[8,5,128,128]{3,2,1,0:T(8,128)} custom-call(s32[32]{0:T(128)S(1)} %get-tuple-element.119.refs_0_, s32[32]{0:T(128)S(1)} %get-tuple-element.118.refs_1_, s32[2]{0:T(128)S(1)} %pad_add_fusion.refs_2_, f32[8,512,128]{2,1,0:T(8,128)S(1)} %all-to-all-done.1.refs_0_.refs_3_, bf16[4096,512]{1,0:T(8,128)(2,1)} %get-tuple-element.67.refs_4_.refs_11_, ...), custom_call_target="tpu_custom_call" | custom-call | flops 5000000000 | bytes 15000000 | tf_op jit(solution)/shard_map/form/pallas_call | solution.py:276
  105.9 8.5 %all-to-all-start.3 = ((f32[8,640,128]{2,1,0:T(8,128)}), f32[8,640,128]{2,1,0:T(8,128)S(1)}, u32[]{:S(2)}, u32[]{:S(2)}) async-start(f32[8,640,128]{2,1,0:T(8,128)} %bitcast.61), calls=%async_computation.3 | async-start | bytes 5242880 | tf_op jit(solution)/shard_map/all_to_all | solution.py:435
  123.4 6.1 %collective-permute-start.16 = (f32[512,128]{1,0:T(8,128)}, f32[512,128]{1,0:T(8,128)S(1)}, u32[]{:S(2)}, u32[]{:S(2)}) collective-permute-start(f32[512,128]{1,0:T(8,128)} %get-tuple-element.89), channel_id=1, source_target_pairs={{0,12},{2,14},{4,0},{6,2},{8,4},{10,6},{12,8},{14,10},{1,13},{3,15... | collective-permute-start | bytes 786440 | tf_op jit(solution)/shard_map/ppermute | solution.py:424
  132.3 7.2 %form.7 = f32[8,5,128,128]{3,2,1,0:T(8,128)} custom-call(s32[32]{0:T(128)S(1)} %get-tuple-element.119.refs_0_, s32[32]{0:T(128)S(1)} %get-tuple-element.118.refs_1_, s32[2]{0:T(128)S(1)} %pad_add_fusion.refs_2_, f32[512,128]{1,0:T(8,128)S(1)} %copy-done.8, f32[512,128]{1,0:T(8,128)S(1)} %collective-permute-done.10.refs_4_, ...), custom_call_target="tpu_custom_call" | custom-call | flops 5000000000 | bytes 15000000 | tf_op jit(solution)/shard_map/form/pallas_call | solution.py:276
  145.4 6.9 %all-to-all-start.4 = ((f32[8,640,128]{2,1,0:T(8,128)}), f32[8,640,128]{2,1,0:T(8,128)}, u32[]{:S(2)}, u32[]{:S(2)}) async-start(f32[8,640,128]{2,1,0:T(8,128)} %bitcast.58), calls=%async_computation.4 | async-start | bytes 5242880 | tf_op jit(solution)/shard_map/all_to_all | solution.py:435
  159.3 6.0 %collective-permute-start.22 = (f32[512,128]{1,0:T(8,128)}, f32[512,128]{1,0:T(8,128)S(1)}, u32[]{:S(2)}, u32[]{:S(2)}) collective-permute-start(f32[512,128]{1,0:T(8,128)} %get-tuple-element.97), channel_id=1, source_target_pairs={{0,4},{2,6},{4,8},{6,10},{8,12},{10,14},{12,0},{14,2},{1,5},{3,7},... | collective-permute-start | bytes 786440 | tf_op jit(solution)/shard_map/ppermute | solution.py:424
  165.3 7.9 %collective-permute-done.18.refs_6_ = f32[512,128]{1,0:T(8,128)S(1)} collective-permute-done((f32[512,128]{1,0:T(8,128)}, f32[512,128]{1,0:T(8,128)S(1)}, u32[]{:S(2)}, u32[]{:S(2)}) %collective-permute-start.18) | collective-permute-done | bytes 262176 | tf_op jit(solution)/shard_map/ppermute | solution.py:424
  175.1 7.0 %form.8 = f32[8,5,128,128]{3,2,1,0:T(8,128)} custom-call(s32[32]{0:T(128)S(1)} %get-tuple-element.119.refs_0_, s32[32]{0:T(128)S(1)} %get-tuple-element.118.refs_1_, s32[2]{0:T(128)S(1)} %pad_add_fusion.refs_2_, f32[512,128]{1,0:T(8,128)S(1)} %copy-done.7, f32[512,128]{1,0:T(8,128)S(1)} %collective-permute-done.17.refs_4_, f32[512,128]{1,0:T(8,128)S(1)} %copy-done.10, ...), custom_call_target="tpu_custom_call" | custom-call | flops 5000000000 | bytes 15000000 | tf_op jit(solution)/shard_map/form/pallas_call | solution.py:276
  187.6 6.9 %all-to-all-start.5 = ((f32[8,640,128]{2,1,0:T(8,128)}), f32[8,640,128]{2,1,0:T(8,128)}, u32[]{:S(2)}, u32[]{:S(2)}) async-start(f32[8,640,128]{2,1,0:T(8,128)} %bitcast.59), calls=%async_computation.5 | async-start | bytes 5242880 | tf_op jit(solution)/shard_map/all_to_all | solution.py:435
  211.5 7.0 %form.9 = f32[8,5,128,128]{3,2,1,0:T(8,128)} custom-call(s32[32]{0:T(128)S(1)} %get-tuple-element.119.refs_0_, s32[32]{0:T(128)S(1)} %get-tuple-element.118.refs_1_, s32[2]{0:T(128)S(1)} %pad_add_fusion.refs_2_, f32[512,128]{1,0:T(8,128)S(1)} %copy-done.6, f32[512,128]{1,0:T(8,128)S(1)} %collective-permute-done.24.refs_4_, f32[512,128]{1,0:T(8,128)S(1)} %copy-done.12, ...), custom_call_target="tpu_custom_call" | custom-call | flops 5000000000 | bytes 15000000 | tf_op jit(solution)/shard_map/form/pallas_call | solution.py:276
  224.6 7.0 %all-to-all-start.6 = ((f32[8,640,128]{2,1,0:T(8,128)}), f32[8,640,128]{2,1,0:T(8,128)}, u32[]{:S(2)}, u32[]{:S(2)}) async-start(f32[8,640,128]{2,1,0:T(8,128)} %bitcast.62), calls=%async_computation.6 | async-start | bytes 5242880 | tf_op jit(solution)/shard_map/all_to_all | solution.py:435
  232.9 6.0 %collective-permute-start.2 = (f32[512,128]{1,0:T(8,128)}, f32[512,128]{1,0:T(8,128)S(1)}, u32[]{:S(2)}, u32[]{:S(2)}) collective-permute-start(f32[512,128]{1,0:T(8,128)} %get-tuple-element.73), channel_id=1, source_target_pairs={{0,6},{2,8},{4,10},{6,12},{8,14},{10,0},{12,2},{14,4},{1,7},{3,9},... | collective-permute-start | bytes 786440 | tf_op jit(solution)/shard_map/ppermute | solution.py:424
  241.8 6.8 %collective-permute-done.2.refs_6_ = f32[512,128]{1,0:T(8,128)S(1)} collective-permute-done((f32[512,128]{1,0:T(8,128)}, f32[512,128]{1,0:T(8,128)S(1)}, u32[]{:S(2)}, u32[]{:S(2)}) %collective-permute-start.2) | collective-permute-done | bytes 262176 | tf_op jit(solution)/shard_map/ppermute | solution.py:424
  252.2 7.1 %form.6 = f32[8,5,128,128]{3,2,1,0:T(8,128)} custom-call(s32[32]{0:T(128)S(1)} %get-tuple-element.119.refs_0_, s32[32]{0:T(128)S(1)} %get-tuple-element.118.refs_1_, s32[2]{0:T(128)S(1)} %pad_add_fusion.refs_2_, f32[512,128]{1,0:T(8,128)S(1)} %copy-done.5, f32[512,128]{1,0:T(8,128)S(1)} %collective-permute-done.refs_4_, ...), custom_call_target="tpu_custom_call" | custom-call | flops 5000000000 | bytes 15000000 | tf_op jit(solution)/shard_map/form/pallas_call | solution.py:276
  259.2 11.6 %all-to-all-done.6.rest_3_ = f32[8,640,128]{2,1,0:T(8,128)} async-done(((f32[8,640,128]{2,1,0:T(8,128)}), f32[8,640,128]{2,1,0:T(8,128)}, u32[]{:S(2)}, u32[]{:S(2)}) %all-to-all-start.6) | async-done | bytes 2621472 | tf_op jit(solution)/shard_map/all_to_all | solution.py:435
  270.8 7.0 %all-to-all-start.2 = ((f32[8,640,128]{2,1,0:T(8,128)}), f32[8,640,128]{2,1,0:T(8,128)}, u32[]{:S(2)}, u32[]{:S(2)}) async-start(f32[8,640,128]{2,1,0:T(8,128)} %bitcast.60), calls=%async_computation.2 | async-start | bytes 5242880 | tf_op jit(solution)/shard_map/all_to_all | solution.py:435
  287.2 6.9 %collect.1.acc_ref = f32[12,1536,128]{2,1,0:T(8,128)S(1)} custom-call(s32[8,5]{1,0:T(8,128)S(1)} %subtract_select_fusion.1.rows_ref, s32[8,5]{1,0:T(8,128)S(1)} %subtract_select_fusion.cols_ref, f32[8,640,128]{2,1,0:T(8,128)S(1)} %all-to-all-done.3.rest_0_, f32[8,640,128]{2,1,0:T(8,128)} %all-to-all-done.4.rest_1_, f32[8,640,128]{2,1,0:T(8,128)} %all-to-all-done.5.rest_2_, ...), custom_call_target="tpu_custom_call" | custom-call | bytes 20000000 | tf_op jit(solution)/shard_map/collect/pallas_call | solution.py:325
  297.8 19.0 %all-to-all-done.2.part_ref = f32[8,640,128]{2,1,0:T(8,128)} async-done(((f32[8,640,128]{2,1,0:T(8,128)}), f32[8,640,128]{2,1,0:T(8,128)}, u32[]{:S(2)}, u32[]{:S(2)}) %all-to-all-start.2) | async-done | bytes 2621472 | tf_op jit(solution)/shard_map/all_to_all | solution.py:435
  316.8 8.8 %finish.1 = f32[1536,1536]{1,0:T(8,128)} custom-call(s32[8,5]{1,0:T(8,128)S(1)} %subtract_select_fusion.1.rows_ref, s32[8,5]{1,0:T(8,128)S(1)} %subtract_select_fusion.cols_ref, f32[8,640,128]{2,1,0:T(8,128)} %all-to-all-done.2.part_ref, f32[12,1536,128]{2,1,0:T(8,128)} %copy-done), custom_call_target="tpu_custom_call" | custom-call | bytes 20000000 | tf_op jit(solution)/shard_map/finish/pallas_call | solution.py:377
  (137 shorter events, 96.4 us)
Async XLA Ops:
  7.2 81.8 %all-gather.3.cloned.1.call-start = ((), (), s32[]{:S(2)}) async-start(), calls=%async_computation.7 | async-start | bytes 9437184 | tf_op jit(solution)/shard_map/all_gather | solution.py:402
  9.9 22.9 %all-to-all-start = ((f32[8,64,512]{2,1,0:T(8,128)}), f32[8,64,512]{2,1,0:T(8,128)S(1)}, u32[]{:S(2)}, u32[]{:S(2)}) async-start(f32[8,64,512]{2,1,0:T(8,128)} %broadcast_in_dim.42), calls=%async_computation | async-start | bytes 2097152 | tf_op jit(solution)/shard_map/all_to_all | solution.py:404
  32.9 52.7 %all-to-all-start.1 = ((f32[8,512,128]{2,1,0:T(8,128)}), f32[8,512,128]{2,1,0:T(8,128)S(1)}, u32[]{:S(2)}, u32[]{:S(2)}) async-start(f32[8,512,128]{2,1,0:T(8,128)} %get-tuple-element.64), calls=%async_computation.1 | async-start | bytes 4194304 | tf_op jit(solution)/shard_map/all_to_all | solution.py:416
  85.5 20.4 %collective-permute-start.7 = (f32[512,128]{1,0:T(8,128)}, f32[512,128]{1,0:T(8,128)}, u32[]{:S(2)}, u32[]{:S(2)}) collective-permute-start(f32[512,128]{1,0:T(8,128)} %get-tuple-element.78), channel_id=1, source_target_pairs={{0,8},{2,10},{4,12},{6,14},{8,0},{10,2},{12,4},{14,6},{1,9},{3,11}... | collective-permute-start | bytes 786440 | tf_op jit(solution)/shard_map/ppermute | solution.py:424
  87.0 18.9 %collective-permute-start.8 = (f32[512,128]{1,0:T(8,128)}, f32[512,128]{1,0:T(8,128)}, u32[]{:S(2)}, u32[]{:S(2)}) collective-permute-start(f32[512,128]{1,0:T(8,128)} %get-tuple-element.79), channel_id=1, source_target_pairs={{0,4},{2,6},{4,8},{6,10},{8,12},{10,14},{12,0},{14,2},{1,5},{3,7},... | collective-permute-start | bytes 786440 | tf_op jit(solution)/shard_map/ppermute | solution.py:424
  88.4 17.5 %collective-permute-start.9 = (f32[512,128]{1,0:T(8,128)}, f32[512,128]{1,0:T(8,128)}, u32[]{:S(2)}, u32[]{:S(2)}) collective-permute-start(f32[512,128]{1,0:T(8,128)} %get-tuple-element.80), channel_id=1, source_target_pairs={{0,12},{2,14},{4,0},{6,2},{8,4},{10,6},{12,8},{14,10},{1,13},{3,15... | collective-permute-start | bytes 786440 | tf_op jit(solution)/shard_map/ppermute | solution.py:424
  105.9 39.5 %all-to-all-start.3 = ((f32[8,640,128]{2,1,0:T(8,128)}), f32[8,640,128]{2,1,0:T(8,128)S(1)}, u32[]{:S(2)}, u32[]{:S(2)}) async-start(f32[8,640,128]{2,1,0:T(8,128)} %bitcast.61), calls=%async_computation.3 | async-start | bytes 5242880 | tf_op jit(solution)/shard_map/all_to_all | solution.py:435
  116.5 15.8 %collective-permute-start.12 = (f32[512,128]{1,0:T(8,128)}, f32[512,128]{1,0:T(8,128)S(1)}, u32[]{:S(2)}, u32[]{:S(2)}) collective-permute-start(f32[512,128]{1,0:T(8,128)} %get-tuple-element.85), channel_id=1, source_target_pairs={{0,10},{2,12},{4,14},{6,0},{8,2},{10,4},{12,6},{14,8},{1,11},{3,13... | collective-permute-start | bytes 786440 | tf_op jit(solution)/shard_map/ppermute | solution.py:424
  119.2 20.4 %collective-permute-start.14 = (f32[512,128]{1,0:T(8,128)}, f32[512,128]{1,0:T(8,128)S(1)}, u32[]{:S(2)}, u32[]{:S(2)}) collective-permute-start(f32[512,128]{1,0:T(8,128)} %get-tuple-element.87), channel_id=1, source_target_pairs={{0,8},{2,10},{4,12},{6,14},{8,0},{10,2},{12,4},{14,6},{1,9},{3,11}... | collective-permute-start | bytes 786440 | tf_op jit(solution)/shard_map/ppermute | solution.py:424
  122.0 18.2 %collective-permute-start.15 = (f32[512,128]{1,0:T(8,128)}, f32[512,128]{1,0:T(8,128)S(1)}, u32[]{:S(2)}, u32[]{:S(2)}) collective-permute-start(f32[512,128]{1,0:T(8,128)} %get-tuple-element.88), channel_id=1, source_target_pairs={{0,4},{2,6},{4,8},{6,10},{8,12},{10,14},{12,0},{14,2},{1,5},{3,7},... | collective-permute-start | bytes 786440 | tf_op jit(solution)/shard_map/ppermute | solution.py:424
  123.4 17.7 %collective-permute-start.16 = (f32[512,128]{1,0:T(8,128)}, f32[512,128]{1,0:T(8,128)S(1)}, u32[]{:S(2)}, u32[]{:S(2)}) collective-permute-start(f32[512,128]{1,0:T(8,128)} %get-tuple-element.89), channel_id=1, source_target_pairs={{0,12},{2,14},{4,0},{6,2},{8,4},{10,6},{12,8},{14,10},{1,13},{3,15... | collective-permute-start | bytes 786440 | tf_op jit(solution)/shard_map/ppermute | solution.py:424
  145.4 42.2 %all-to-all-start.4 = ((f32[8,640,128]{2,1,0:T(8,128)}), f32[8,640,128]{2,1,0:T(8,128)}, u32[]{:S(2)}, u32[]{:S(2)}) async-start(f32[8,640,128]{2,1,0:T(8,128)} %bitcast.58), calls=%async_computation.4 | async-start | bytes 5242880 | tf_op jit(solution)/shard_map/all_to_all | solution.py:435
  152.3 20.9 %collective-permute-start.18 = (f32[512,128]{1,0:T(8,128)}, f32[512,128]{1,0:T(8,128)S(1)}, u32[]{:S(2)}, u32[]{:S(2)}) collective-permute-start(f32[512,128]{1,0:T(8,128)} %get-tuple-element.93), channel_id=1, source_target_pairs={{0,6},{2,8},{4,10},{6,12},{8,14},{10,0},{12,2},{14,4},{1,7},{3,9},... | collective-permute-start | bytes 786440 | tf_op jit(solution)/shard_map/ppermute | solution.py:424
  156.1 17.1 %collective-permute-start.19 = (f32[512,128]{1,0:T(8,128)}, f32[512,128]{1,0:T(8,128)S(1)}, u32[]{:S(2)}, u32[]{:S(2)}) collective-permute-start(f32[512,128]{1,0:T(8,128)} %get-tuple-element.94), channel_id=1, source_target_pairs={{0,10},{2,12},{4,14},{6,0},{8,2},{10,4},{12,6},{14,8},{1,11},{3,13... | collective-permute-start | bytes 786440 | tf_op jit(solution)/shard_map/ppermute | solution.py:424
  157.6 15.6 %collective-permute-start.20 = (f32[512,128]{1,0:T(8,128)}, f32[512,128]{1,0:T(8,128)S(1)}, u32[]{:S(2)}, u32[]{:S(2)}) collective-permute-start(f32[512,128]{1,0:T(8,128)} %get-tuple-element.95), channel_id=1, source_target_pairs={{0,14},{2,0},{4,2},{6,4},{8,6},{10,8},{12,10},{14,12},{1,15},{3,1}... | collective-permute-start | bytes 786440 | tf_op jit(solution)/shard_map/ppermute | solution.py:424
  157.6 24.6 %collective-permute-start.21 = (f32[512,128]{1,0:T(8,128)}, f32[512,128]{1,0:T(8,128)S(1)}, u32[]{:S(2)}, u32[]{:S(2)}) collective-permute-start(f32[512,128]{1,0:T(8,128)} %get-tuple-element.96), channel_id=1, source_target_pairs={{0,8},{2,10},{4,12},{6,14},{8,0},{10,2},{12,4},{14,6},{1,9},{3,11}... | collective-permute-start | bytes 786440 | tf_op jit(solution)/shard_map/ppermute | solution.py:424
  159.3 22.9 %collective-permute-start.22 = (f32[512,128]{1,0:T(8,128)}, f32[512,128]{1,0:T(8,128)S(1)}, u32[]{:S(2)}, u32[]{:S(2)}) collective-permute-start(f32[512,128]{1,0:T(8,128)} %get-tuple-element.97), channel_id=1, source_target_pairs={{0,4},{2,6},{4,8},{6,10},{8,12},{10,14},{12,0},{14,2},{1,5},{3,7},... | collective-permute-start | bytes 786440 | tf_op jit(solution)/shard_map/ppermute | solution.py:424
  187.6 37.0 %all-to-all-start.5 = ((f32[8,640,128]{2,1,0:T(8,128)}), f32[8,640,128]{2,1,0:T(8,128)}, u32[]{:S(2)}, u32[]{:S(2)}) async-start(f32[8,640,128]{2,1,0:T(8,128)} %bitcast.59), calls=%async_computation.5 | async-start | bytes 5242880 | tf_op jit(solution)/shard_map/all_to_all | solution.py:435
  199.3 19.3 %collective-permute-start.1 = (f32[512,128]{1,0:T(8,128)}, f32[512,128]{1,0:T(8,128)S(1)}, u32[]{:S(2)}, u32[]{:S(2)}) collective-permute-start(f32[512,128]{1,0:T(8,128)} %get-tuple-element.72), channel_id=1, source_target_pairs={{0,4},{2,6},{4,8},{6,10},{8,12},{10,14},{12,0},{14,2},{1,5},{3,7},... | collective-permute-start | bytes 786440 | tf_op jit(solution)/shard_map/ppermute | solution.py:424
  203.4 15.1 %collective-permute-start.3 = (f32[512,128]{1,0:T(8,128)}, f32[512,128]{1,0:T(8,128)S(1)}, u32[]{:S(2)}, u32[]{:S(2)}) collective-permute-start(f32[512,128]{1,0:T(8,128)} %get-tuple-element.74), channel_id=1, source_target_pairs={{0,8},{2,10},{4,12},{6,14},{8,0},{10,2},{12,4},{14,6},{1,9},{3,11}... | collective-permute-start | bytes 786440 | tf_op jit(solution)/shard_map/ppermute | solution.py:424
  204.1 16.2 %collective-permute-start.5 = (f32[512,128]{1,0:T(8,128)}, f32[512,128]{1,0:T(8,128)S(1)}, u32[]{:S(2)}, u32[]{:S(2)}) collective-permute-start(f32[512,128]{1,0:T(8,128)} %get-tuple-element.76), channel_id=1, source_target_pairs={{0,12},{2,14},{4,0},{6,2},{8,4},{10,6},{12,8},{14,10},{1,13},{3,15... | collective-permute-start | bytes 786440 | tf_op jit(solution)/shard_map/ppermute | solution.py:424
  224.6 46.2 %all-to-all-start.6 = ((f32[8,640,128]{2,1,0:T(8,128)}), f32[8,640,128]{2,1,0:T(8,128)}, u32[]{:S(2)}, u32[]{:S(2)}) async-start(f32[8,640,128]{2,1,0:T(8,128)} %bitcast.62), calls=%async_computation.6 | async-start | bytes 5242880 | tf_op jit(solution)/shard_map/all_to_all | solution.py:435
  232.9 15.7 %collective-permute-start.2 = (f32[512,128]{1,0:T(8,128)}, f32[512,128]{1,0:T(8,128)S(1)}, u32[]{:S(2)}, u32[]{:S(2)}) collective-permute-start(f32[512,128]{1,0:T(8,128)} %get-tuple-element.73), channel_id=1, source_target_pairs={{0,6},{2,8},{4,10},{6,12},{8,14},{10,0},{12,2},{14,4},{1,7},{3,9},... | collective-permute-start | bytes 786440 | tf_op jit(solution)/shard_map/ppermute | solution.py:424
  270.8 45.9 %all-to-all-start.2 = ((f32[8,640,128]{2,1,0:T(8,128)}), f32[8,640,128]{2,1,0:T(8,128)}, u32[]{:S(2)}, u32[]{:S(2)}) async-start(f32[8,640,128]{2,1,0:T(8,128)} %bitcast.60), calls=%async_computation.2 | async-start | bytes 5242880 | tf_op jit(solution)/shard_map/all_to_all | solution.py:435
  (35 other events, 309.7 us)
Sparse Core Ops, SparseCore 0:
  9.7 75.5 all-gather.2

commit v5 on v4

--- a/solution.py
+++ b/solution.py
@@ -148,7 +148,7 @@
 
 def solve(panel_all, inverse, after):
     order = inverse.shape[0]
-    rows = 1024
+    rows = 512
     half = order // 2
     block = pl.BlockSpec((rows, order), lambda i: (i, 0))
     return pl.pallas_call(

time: 333 us -> 336 us (level)
  waiting for transfers between devices: 88.6 us -> 78.4 us
  starting transfers between devices: 92.6 us -> 102 us
    ppermute x28, starting transfers between devices: 45.7 us -> 55.7 us  [local(): pieces[k] = lax.ppermute(sent[k], 'row', ring(k))]
    ppermute x28, waiting for transfers between devices: 33.2 us -> 27.6 us  [local(): pieces[k] = lax.ppermute(sent[k], 'row', ring(k))]
    all_to_all x5, waiting for transfers between devices: 41.7 us -> 37.1 us  [local(): lax.all_to_all(sent, 'front', split_axis=0, concat_axis=0, tiled=True)]
  transfers between devices with their start and end apart: 36 -> 36, of which waited for: 20 -> 16; matrix products, arithmetic and copies ran while one was open for 4% -> 4% of each run, Pallas kernels for 30% -> 31%
where the time goes in v5:
time: 336 us; the launch traced here: 334 us
  Pallas kernels  111 us (33%)
  starting transfers between devices  102 us (30%)
  waiting for transfers between devices  78.4 us (23%)
  local copies, waits for them, and re-layouts  22.7 us (7%)
  between operations  14.4 us (4%)
  matrix products  4.35 us (1%)
    ppermute x28, starting transfers between devices, local(): pieces[k] = lax.ppermute(sent[k], 'row', ring(k))  55.7 us
    pallas_call x1, Pallas kernels, factor(): pl.pallas_call(factor_kernel, out_shape=(whole, whole), in_specs=[vmem_sp...  38.9 us
    all_to_all x5, waiting for transfers between devices, local(): lax.all_to_all(sent, 'front', split_axis=0, concat_axis=0, tiled=True)  37.1 us
    all_to_all x5, starting transfers between devices, local(): lax.all_to_all(sent, 'front', split_axis=0, concat_axis=0, tiled=True)  35.7 us
    pallas_call x5, Pallas kernels, form(): pl.pallas_call(lambda *refs: form_kernel(slot, count, *refs), out_shape=p...  35.7 us
    ppermute x28, waiting for transfers between devices, local(): pieces[k] = lax.ppermute(sent[k], 'row', ring(k))  27.6 us
    unnamed x47, local copies, waits for them, and re-layouts  15.7 us
    pallas_call x1, Pallas kernels, solve(): pl.pallas_call(solve_kernel, grid=(panel_all.shape[0] // rows,), out_shap...  11.5 us
  transfers between devices with their start and end apart: 36, of which 16 were waited for; matrix products, arithmetic and copies ran while one was open for 4% of the time, Pallas kernels for 31%

profile of v5, /device:TPU:14, one launch (start us, length us, event | category | flops | bytes accessed | tf_op | source)
XLA Modules:
  0.0 333.7 jit_solution(2961925300233211815)
XLA Ops:
  16.4 9.3 %pack_columns.1 = (f32[8,512,128]{2,1,0:T(8,128)}, f32[512,128]{1,0:T(8,128)}, f32[512,128]{1,0:T(8,128)}, f32[512,128]{1,0:T(8,128)}, f32[512,128]{1,0:T(8,128)...) custom-call(s32[8]{0:T(128)S(1)} %broadcast_minimum_fusion.2.starts_, ...), custom_call_target="tpu_custom_call" | custom-call | bytes 20000000 | tf_op jit(solution)/shard_map/pack_columns/pallas_call | solution.py:198
  25.8 7.1 %all-to-all-done = f32[8,64,512]{2,1,0:T(8,128)S(1)} async-done(((f32[8,64,512]{2,1,0:T(8,128)}), f32[8,64,512]{2,1,0:T(8,128)S(1)}, u32[]{:S(2)}, u32[]{:S(2)}) %all-to-all-start) | async-done | bytes 1048608 | tf_op jit(solution)/shard_map/all_to_all | solution.py:404
  32.9 5.6 %all-to-all-start.1 = ((f32[8,512,128]{2,1,0:T(8,128)}), f32[8,512,128]{2,1,0:T(8,128)S(1)}, u32[]{:S(2)}, u32[]{:S(2)}) async-start(f32[8,512,128]{2,1,0:T(8,128)} %get-tuple-element.64), calls=%async_computation.1 | async-start | bytes 4194304 | tf_op jit(solution)/shard_map/all_to_all | solution.py:416
  39.7 38.9 %factor.1 = (f32[512,512]{1,0:T(8,128)S(1)}, f32[512,512]{1,0:T(8,128)S(1)}) custom-call(f32[512,512]{1,0:T(8,128)S(1)} %bitcast.53, f32[512,128]{1,0:T(8,128)S(1)} %copy-done.8), custom_call_target="tpu_custom_call" | custom-call | flops 20000000000 | bytes 4000000 | tf_op jit(solution)/shard_map/factor/pallas_call | solution.py:109
  79.6 5.9 %all-to-all-done.1.refs_0_.refs_3_ = f32[8,512,128]{2,1,0:T(8,128)S(1)} async-done(((f32[8,512,128]{2,1,0:T(8,128)}), f32[8,512,128]{2,1,0:T(8,128)S(1)}, u32[]{:S(2)}, u32[]{:S(2)}) %all-to-all-start.1) | async-done | bytes 2097184 | tf_op jit(solution)/shard_map/all_to_all | solution.py:416
  89.0 11.5 %solve.1 = (bf16[4096,512]{1,0:T(8,128)(2,1)}, bf16[4096,512]{1,0:T(8,128)(2,1)}) custom-call(f32[4096,512]{1,0:T(8,128)} %bitcast.64, f32[512,512]{1,0:T(8,128)S(1)} %get-tuple-element.66.v_ref, f32[8,512,128]{2,1,0:T(8,128)S(1)} %all-to-all-done.1.refs_0_.refs_3_), custom_call_target="tpu_custom_call" | custom-call | flops 8000000000 | bytes 20000000 | tf_op jit(solution)/shard_map/solve/pallas_call | solution.py:154
  100.5 7.5 %form.5 = f32[8,5,128,128]{3,2,1,0:T(8,128)} custom-call(s32[32]{0:T(128)S(1)} %get-tuple-element.119.refs_0_, s32[32]{0:T(128)S(1)} %get-tuple-element.118.refs_1_, s32[2]{0:T(128)S(1)} %pad_add_fusion.refs_2_, f32[8,512,128]{2,1,0:T(8,128)S(1)} %all-to-all-done.1.refs_0_.refs_3_, bf16[4096,512]{1,0:T(8,128)(2,1)} %get-tuple-element.67.refs_4_.refs_11_, ...), custom_call_target="tpu_custom_call" | custom-call | flops 5000000000 | bytes 15000000 | tf_op jit(solution)/shard_map/form/pallas_call | solution.py:276
  108.1 7.7 %all-to-all-start.3 = ((f32[8,640,128]{2,1,0:T(8,128)}), f32[8,640,128]{2,1,0:T(8,128)S(1)}, u32[]{:S(2)}, u32[]{:S(2)}) async-start(f32[8,640,128]{2,1,0:T(8,128)} %bitcast.61), calls=%async_computation.3 | async-start | bytes 5242880 | tf_op jit(solution)/shard_map/all_to_all | solution.py:435
  127.2 7.0 %collective-permute-done.11.refs_6_ = f32[512,128]{1,0:T(8,128)S(1)} collective-permute-done((f32[512,128]{1,0:T(8,128)S(1)}, f32[512,128]{1,0:T(8,128)S(1)}, u32[]{:S(2)}, u32[]{:S(2)}) %collective-permute-start.11) | collective-permute-done | bytes 262176 | tf_op jit(solution)/shard_map/ppermute | solution.py:424
  134.2 7.0 %form.7 = f32[8,5,128,128]{3,2,1,0:T(8,128)} custom-call(s32[32]{0:T(128)S(1)} %get-tuple-element.119.refs_0_, s32[32]{0:T(128)S(1)} %get-tuple-element.118.refs_1_, s32[2]{0:T(128)S(1)} %pad_add_fusion.refs_2_, f32[512,128]{1,0:T(8,128)S(1)} %copy-done.8, f32[512,128]{1,0:T(8,128)S(1)} %collective-permute-done.10.refs_4_, ...), custom_call_target="tpu_custom_call" | custom-call | flops 5000000000 | bytes 15000000 | tf_op jit(solution)/shard_map/form/pallas_call | solution.py:276
  148.4 6.9 %all-to-all-start.4 = ((f32[8,640,128]{2,1,0:T(8,128)}), f32[8,640,128]{2,1,0:T(8,128)}, u32[]{:S(2)}, u32[]{:S(2)}) async-start(f32[8,640,128]{2,1,0:T(8,128)} %bitcast.58), calls=%async_computation.4 | async-start | bytes 5242880 | tf_op jit(solution)/shard_map/all_to_all | solution.py:435
  164.0 6.6 %collective-permute-start.23 = (f32[512,128]{1,0:T(8,128)}, f32[512,128]{1,0:T(8,128)S(1)}, u32[]{:S(2)}, u32[]{:S(2)}) collective-permute-start(f32[512,128]{1,0:T(8,128)} %get-tuple-element.98), channel_id=1, source_target_pairs={{0,12},{2,14},{4,0},{6,2},{8,4},{10,6},{12,8},{14,10},{1,13},{3,15... | collective-permute-start | bytes 786440 | tf_op jit(solution)/shard_map/ppermute | solution.py:424
  175.5 7.0 %form.8 = f32[8,5,128,128]{3,2,1,0:T(8,128)} custom-call(s32[32]{0:T(128)S(1)} %get-tuple-element.119.refs_0_, s32[32]{0:T(128)S(1)} %get-tuple-element.118.refs_1_, s32[2]{0:T(128)S(1)} %pad_add_fusion.refs_2_, f32[512,128]{1,0:T(8,128)S(1)} %copy-done.7, f32[512,128]{1,0:T(8,128)S(1)} %collective-permute-done.17.refs_4_, f32[512,128]{1,0:T(8,128)S(1)} %copy-done.10, ...), custom_call_target="tpu_custom_call" | custom-call | flops 5000000000 | bytes 15000000 | tf_op jit(solution)/shard_map/form/pallas_call | solution.py:276
  184.9 7.0 %all-to-all-start.5 = ((f32[8,640,128]{2,1,0:T(8,128)}), f32[8,640,128]{2,1,0:T(8,128)}, u32[]{:S(2)}, u32[]{:S(2)}) async-start(f32[8,640,128]{2,1,0:T(8,128)} %bitcast.59), calls=%async_computation.5 | async-start | bytes 5242880 | tf_op jit(solution)/shard_map/all_to_all | solution.py:435
  202.9 9.3 %collective-permute-start.5 = (f32[512,128]{1,0:T(8,128)}, f32[512,128]{1,0:T(8,128)S(1)}, u32[]{:S(2)}, u32[]{:S(2)}) collective-permute-start(f32[512,128]{1,0:T(8,128)} %get-tuple-element.76), channel_id=1, source_target_pairs={{0,12},{2,14},{4,0},{6,2},{8,4},{10,6},{12,8},{14,10},{1,13},{3,15... | collective-permute-start | bytes 786440 | tf_op jit(solution)/shard_map/ppermute | solution.py:424
  214.1 7.0 %form.9 = f32[8,5,128,128]{3,2,1,0:T(8,128)} custom-call(s32[32]{0:T(128)S(1)} %get-tuple-element.119.refs_0_, s32[32]{0:T(128)S(1)} %get-tuple-element.118.refs_1_, s32[2]{0:T(128)S(1)} %pad_add_fusion.refs_2_, f32[512,128]{1,0:T(8,128)S(1)} %copy-done.6, f32[512,128]{1,0:T(8,128)S(1)} %collective-permute-done.24.refs_4_, f32[512,128]{1,0:T(8,128)S(1)} %copy-done.12, ...), custom_call_target="tpu_custom_call" | custom-call | flops 5000000000 | bytes 15000000 | tf_op jit(solution)/shard_map/form/pallas_call | solution.py:276
  226.1 7.3 %all-to-all-start.6 = ((f32[8,640,128]{2,1,0:T(8,128)}), f32[8,640,128]{2,1,0:T(8,128)}, u32[]{:S(2)}, u32[]{:S(2)}) async-start(f32[8,640,128]{2,1,0:T(8,128)} %bitcast.62), calls=%async_computation.6 | async-start | bytes 5242880 | tf_op jit(solution)/shard_map/all_to_all | solution.py:435
  238.0 4.9 %collective-permute-start.4 = (f32[512,128]{1,0:T(8,128)}, f32[512,128]{1,0:T(8,128)S(1)}, u32[]{:S(2)}, u32[]{:S(2)}) collective-permute-start(f32[512,128]{1,0:T(8,128)} %get-tuple-element.75), channel_id=1, source_target_pairs={{0,10},{2,12},{4,14},{6,0},{8,2},{10,4},{12,6},{14,8},{1,11},{3,13... | collective-permute-start | bytes 786440 | tf_op jit(solution)/shard_map/ppermute | solution.py:424
  255.8 7.0 %form.6 = f32[8,5,128,128]{3,2,1,0:T(8,128)} custom-call(s32[32]{0:T(128)S(1)} %get-tuple-element.119.refs_0_, s32[32]{0:T(128)S(1)} %get-tuple-element.118.refs_1_, s32[2]{0:T(128)S(1)} %pad_add_fusion.refs_2_, f32[512,128]{1,0:T(8,128)S(1)} %copy-done.5, f32[512,128]{1,0:T(8,128)S(1)} %collective-permute-done.refs_4_, ...), custom_call_target="tpu_custom_call" | custom-call | flops 5000000000 | bytes 15000000 | tf_op jit(solution)/shard_map/form/pallas_call | solution.py:276
  262.8 10.4 %all-to-all-done.6.rest_3_ = f32[8,640,128]{2,1,0:T(8,128)} async-done(((f32[8,640,128]{2,1,0:T(8,128)}), f32[8,640,128]{2,1,0:T(8,128)}, u32[]{:S(2)}, u32[]{:S(2)}) %all-to-all-start.6) | async-done | bytes 2621472 | tf_op jit(solution)/shard_map/all_to_all | solution.py:435
  273.2 6.9 %all-to-all-start.2 = ((f32[8,640,128]{2,1,0:T(8,128)}), f32[8,640,128]{2,1,0:T(8,128)}, u32[]{:S(2)}, u32[]{:S(2)}) async-start(f32[8,640,128]{2,1,0:T(8,128)} %bitcast.60), calls=%async_computation.2 | async-start | bytes 5242880 | tf_op jit(solution)/shard_map/all_to_all | solution.py:435
  289.5 6.9 %collect.1.acc_ref = f32[12,1536,128]{2,1,0:T(8,128)S(1)} custom-call(s32[8,5]{1,0:T(8,128)S(1)} %subtract_select_fusion.1.rows_ref, s32[8,5]{1,0:T(8,128)S(1)} %subtract_select_fusion.cols_ref, f32[8,640,128]{2,1,0:T(8,128)S(1)} %all-to-all-done.3.rest_0_, f32[8,640,128]{2,1,0:T(8,128)} %all-to-all-done.4.rest_1_, f32[8,640,128]{2,1,0:T(8,128)} %all-to-all-done.5.rest_2_, ...), custom_call_target="tpu_custom_call" | custom-call | bytes 20000000 | tf_op jit(solution)/shard_map/collect/pallas_call | solution.py:325
  300.1 18.0 %all-to-all-done.2.part_ref = f32[8,640,128]{2,1,0:T(8,128)} async-done(((f32[8,640,128]{2,1,0:T(8,128)}), f32[8,640,128]{2,1,0:T(8,128)}, u32[]{:S(2)}, u32[]{:S(2)}) %all-to-all-start.2) | async-done | bytes 2621472 | tf_op jit(solution)/shard_map/all_to_all | solution.py:435
  318.0 8.8 %finish.1 = f32[1536,1536]{1,0:T(8,128)} custom-call(s32[8,5]{1,0:T(8,128)S(1)} %subtract_select_fusion.1.rows_ref, s32[8,5]{1,0:T(8,128)S(1)} %subtract_select_fusion.cols_ref, f32[8,640,128]{2,1,0:T(8,128)} %all-to-all-done.2.part_ref, f32[12,1536,128]{2,1,0:T(8,128)} %copy-done), custom_call_target="tpu_custom_call" | custom-call | bytes 20000000 | tf_op jit(solution)/shard_map/finish/pallas_call | solution.py:377
  (137 shorter events, 97.9 us)
Async XLA Ops:
  7.2 81.8 %all-gather.3.cloned.1.call-start = ((), (), s32[]{:S(2)}) async-start(), calls=%async_computation.7 | async-start | bytes 9437184 | tf_op jit(solution)/shard_map/all_gather | solution.py:402
  9.9 22.9 %all-to-all-start = ((f32[8,64,512]{2,1,0:T(8,128)}), f32[8,64,512]{2,1,0:T(8,128)S(1)}, u32[]{:S(2)}, u32[]{:S(2)}) async-start(f32[8,64,512]{2,1,0:T(8,128)} %broadcast_in_dim.42), calls=%async_computation | async-start | bytes 2097152 | tf_op jit(solution)/shard_map/all_to_all | solution.py:404
  32.9 52.7 %all-to-all-start.1 = ((f32[8,512,128]{2,1,0:T(8,128)}), f32[8,512,128]{2,1,0:T(8,128)S(1)}, u32[]{:S(2)}, u32[]{:S(2)}) async-start(f32[8,512,128]{2,1,0:T(8,128)} %get-tuple-element.64), calls=%async_computation.1 | async-start | bytes 4194304 | tf_op jit(solution)/shard_map/all_to_all | solution.py:416
  85.5 22.5 %collective-permute-start.7 = (f32[512,128]{1,0:T(8,128)}, f32[512,128]{1,0:T(8,128)}, u32[]{:S(2)}, u32[]{:S(2)}) collective-permute-start(f32[512,128]{1,0:T(8,128)} %get-tuple-element.78), channel_id=1, source_target_pairs={{0,8},{2,10},{4,12},{6,14},{8,0},{10,2},{12,4},{14,6},{1,9},{3,11}... | collective-permute-start | bytes 786440 | tf_op jit(solution)/shard_map/ppermute | solution.py:424
  87.0 21.1 %collective-permute-start.8 = (f32[512,128]{1,0:T(8,128)}, f32[512,128]{1,0:T(8,128)}, u32[]{:S(2)}, u32[]{:S(2)}) collective-permute-start(f32[512,128]{1,0:T(8,128)} %get-tuple-element.79), channel_id=1, source_target_pairs={{0,4},{2,6},{4,8},{6,10},{8,12},{10,14},{12,0},{14,2},{1,5},{3,7},... | collective-permute-start | bytes 786440 | tf_op jit(solution)/shard_map/ppermute | solution.py:424
  88.4 19.6 %collective-permute-start.9 = (f32[512,128]{1,0:T(8,128)}, f32[512,128]{1,0:T(8,128)}, u32[]{:S(2)}, u32[]{:S(2)}) collective-permute-start(f32[512,128]{1,0:T(8,128)} %get-tuple-element.80), channel_id=1, source_target_pairs={{0,12},{2,14},{4,0},{6,2},{8,4},{10,6},{12,8},{14,10},{1,13},{3,15... | collective-permute-start | bytes 786440 | tf_op jit(solution)/shard_map/ppermute | solution.py:424
  108.1 40.4 %all-to-all-start.3 = ((f32[8,640,128]{2,1,0:T(8,128)}), f32[8,640,128]{2,1,0:T(8,128)S(1)}, u32[]{:S(2)}, u32[]{:S(2)}) async-start(f32[8,640,128]{2,1,0:T(8,128)} %bitcast.61), calls=%async_computation.3 | async-start | bytes 5242880 | tf_op jit(solution)/shard_map/all_to_all | solution.py:435
  115.7 18.5 %collective-permute-start.11 = (f32[512,128]{1,0:T(8,128)S(1)}, f32[512,128]{1,0:T(8,128)S(1)}, u32[]{:S(2)}, u32[]{:S(2)}) collective-permute-start(f32[512,128]{1,0:T(8,128)S(1)} %copy-done.22), channel_id=1, source_target_pairs={{0,6},{2,8},{4,10},{6,12},{8,14},{10,0},{12,2},{14,4},{1,7},{3,9},... | collective-permute-start | bytes 786440 | tf_op jit(solution)/shard_map/ppermute | solution.py:424
  118.1 16.1 %collective-permute-start.12 = (f32[512,128]{1,0:T(8,128)}, f32[512,128]{1,0:T(8,128)S(1)}, u32[]{:S(2)}, u32[]{:S(2)}) collective-permute-start(f32[512,128]{1,0:T(8,128)} %get-tuple-element.85), channel_id=1, source_target_pairs={{0,10},{2,12},{4,14},{6,0},{8,2},{10,4},{12,6},{14,8},{1,11},{3,13... | collective-permute-start | bytes 786440 | tf_op jit(solution)/shard_map/ppermute | solution.py:424
  120.4 20.8 %collective-permute-start.14 = (f32[512,128]{1,0:T(8,128)}, f32[512,128]{1,0:T(8,128)S(1)}, u32[]{:S(2)}, u32[]{:S(2)}) collective-permute-start(f32[512,128]{1,0:T(8,128)} %get-tuple-element.87), channel_id=1, source_target_pairs={{0,8},{2,10},{4,12},{6,14},{8,0},{10,2},{12,4},{14,6},{1,9},{3,11}... | collective-permute-start | bytes 786440 | tf_op jit(solution)/shard_map/ppermute | solution.py:424
  122.5 18.9 %collective-permute-start.15 = (f32[512,128]{1,0:T(8,128)}, f32[512,128]{1,0:T(8,128)S(1)}, u32[]{:S(2)}, u32[]{:S(2)}) collective-permute-start(f32[512,128]{1,0:T(8,128)} %get-tuple-element.88), channel_id=1, source_target_pairs={{0,4},{2,6},{4,8},{6,10},{8,12},{10,14},{12,0},{14,2},{1,5},{3,7},... | collective-permute-start | bytes 786440 | tf_op jit(solution)/shard_map/ppermute | solution.py:424
  148.4 36.5 %all-to-all-start.4 = ((f32[8,640,128]{2,1,0:T(8,128)}), f32[8,640,128]{2,1,0:T(8,128)}, u32[]{:S(2)}, u32[]{:S(2)}) async-start(f32[8,640,128]{2,1,0:T(8,128)} %bitcast.58), calls=%async_computation.4 | async-start | bytes 5242880 | tf_op jit(solution)/shard_map/all_to_all | solution.py:435
  157.7 15.9 %collective-permute-start.19 = (f32[512,128]{1,0:T(8,128)}, f32[512,128]{1,0:T(8,128)S(1)}, u32[]{:S(2)}, u32[]{:S(2)}) collective-permute-start(f32[512,128]{1,0:T(8,128)} %get-tuple-element.94), channel_id=1, source_target_pairs={{0,10},{2,12},{4,14},{6,0},{8,2},{10,4},{12,6},{14,8},{1,11},{3,13... | collective-permute-start | bytes 786440 | tf_op jit(solution)/shard_map/ppermute | solution.py:424
  160.0 22.5 %collective-permute-start.21 = (f32[512,128]{1,0:T(8,128)}, f32[512,128]{1,0:T(8,128)S(1)}, u32[]{:S(2)}, u32[]{:S(2)}) collective-permute-start(f32[512,128]{1,0:T(8,128)} %get-tuple-element.96), channel_id=1, source_target_pairs={{0,8},{2,10},{4,12},{6,14},{8,0},{10,2},{12,4},{14,6},{1,9},{3,11}... | collective-permute-start | bytes 786440 | tf_op jit(solution)/shard_map/ppermute | solution.py:424
  164.0 18.6 %collective-permute-start.22 = (f32[512,128]{1,0:T(8,128)}, f32[512,128]{1,0:T(8,128)S(1)}, u32[]{:S(2)}, u32[]{:S(2)}) collective-permute-start(f32[512,128]{1,0:T(8,128)} %get-tuple-element.97), channel_id=1, source_target_pairs={{0,4},{2,6},{4,8},{6,10},{8,12},{10,14},{12,0},{14,2},{1,5},{3,7},... | collective-permute-start | bytes 786440 | tf_op jit(solution)/shard_map/ppermute | solution.py:424
  164.0 19.3 %collective-permute-start.23 = (f32[512,128]{1,0:T(8,128)}, f32[512,128]{1,0:T(8,128)S(1)}, u32[]{:S(2)}, u32[]{:S(2)}) collective-permute-start(f32[512,128]{1,0:T(8,128)} %get-tuple-element.98), channel_id=1, source_target_pairs={{0,12},{2,14},{4,0},{6,2},{8,4},{10,6},{12,8},{14,10},{1,13},{3,15... | collective-permute-start | bytes 786440 | tf_op jit(solution)/shard_map/ppermute | solution.py:424
  184.9 41.2 %all-to-all-start.5 = ((f32[8,640,128]{2,1,0:T(8,128)}), f32[8,640,128]{2,1,0:T(8,128)}, u32[]{:S(2)}, u32[]{:S(2)}) async-start(f32[8,640,128]{2,1,0:T(8,128)} %bitcast.59), calls=%async_computation.5 | async-start | bytes 5242880 | tf_op jit(solution)/shard_map/all_to_all | solution.py:435
  196.2 16.0 %collective-permute-start.26 = (f32[512,128]{1,0:T(8,128)}, f32[512,128]{1,0:T(8,128)S(1)}, u32[]{:S(2)}, u32[]{:S(2)}) collective-permute-start(f32[512,128]{1,0:T(8,128)} %get-tuple-element.103), channel_id=1, source_target_pairs={{0,10},{2,12},{4,14},{6,0},{8,2},{10,4},{12,6},{14,8},{1,11},{3,13... | collective-permute-start | bytes 786440 | tf_op jit(solution)/shard_map/ppermute | solution.py:424
  200.2 20.9 %collective-permute-start.1 = (f32[512,128]{1,0:T(8,128)}, f32[512,128]{1,0:T(8,128)S(1)}, u32[]{:S(2)}, u32[]{:S(2)}) collective-permute-start(f32[512,128]{1,0:T(8,128)} %get-tuple-element.72), channel_id=1, source_target_pairs={{0,4},{2,6},{4,8},{6,10},{8,12},{10,14},{12,0},{14,2},{1,5},{3,7},... | collective-permute-start | bytes 786440 | tf_op jit(solution)/shard_map/ppermute | solution.py:424
  201.9 19.2 %collective-permute-start.3 = (f32[512,128]{1,0:T(8,128)}, f32[512,128]{1,0:T(8,128)S(1)}, u32[]{:S(2)}, u32[]{:S(2)}) collective-permute-start(f32[512,128]{1,0:T(8,128)} %get-tuple-element.74), channel_id=1, source_target_pairs={{0,8},{2,10},{4,12},{6,14},{8,0},{10,2},{12,4},{14,6},{1,9},{3,11}... | collective-permute-start | bytes 786440 | tf_op jit(solution)/shard_map/ppermute | solution.py:424
  202.9 18.9 %collective-permute-start.5 = (f32[512,128]{1,0:T(8,128)}, f32[512,128]{1,0:T(8,128)S(1)}, u32[]{:S(2)}, u32[]{:S(2)}) collective-permute-start(f32[512,128]{1,0:T(8,128)} %get-tuple-element.76), channel_id=1, source_target_pairs={{0,12},{2,14},{4,0},{6,2},{8,4},{10,6},{12,8},{14,10},{1,13},{3,15... | collective-permute-start | bytes 786440 | tf_op jit(solution)/shard_map/ppermute | solution.py:424
  226.1 47.1 %all-to-all-start.6 = ((f32[8,640,128]{2,1,0:T(8,128)}), f32[8,640,128]{2,1,0:T(8,128)}, u32[]{:S(2)}, u32[]{:S(2)}) async-start(f32[8,640,128]{2,1,0:T(8,128)} %bitcast.62), calls=%async_computation.6 | async-start | bytes 5242880 | tf_op jit(solution)/shard_map/all_to_all | solution.py:435
  238.0 16.8 %collective-permute-start.4 = (f32[512,128]{1,0:T(8,128)}, f32[512,128]{1,0:T(8,128)S(1)}, u32[]{:S(2)}, u32[]{:S(2)}) collective-permute-start(f32[512,128]{1,0:T(8,128)} %get-tuple-element.75), channel_id=1, source_target_pairs={{0,10},{2,12},{4,14},{6,0},{8,2},{10,4},{12,6},{14,8},{1,11},{3,13... | collective-permute-start | bytes 786440 | tf_op jit(solution)/shard_map/ppermute | solution.py:424
  273.2 44.9 %all-to-all-start.2 = ((f32[8,640,128]{2,1,0:T(8,128)}), f32[8,640,128]{2,1,0:T(8,128)}, u32[]{:S(2)}, u32[]{:S(2)}) async-start(f32[8,640,128]{2,1,0:T(8,128)} %bitcast.60), calls=%async_computation.2 | async-start | bytes 5242880 | tf_op jit(solution)/shard_map/all_to_all | solution.py:435
  (35 other events, 327.8 us)
Sparse Core Ops, SparseCore 0:
  9.7 75.5 all-gather.2
